TPU v7x, 256 devices: a whole 4x4x8 slice. The times are simulated.
256 devices in a mesh: engine: 16 (over x, z_lo, core), expert: 16 (over z_hi, y).
Axes of the slice: x: 4, y: 4, z: 8 (z_hi: 4, z_lo: 2; z = z_hi * 2 + z_lo), core: 2. Of those that a mesh axis runs over, the one named last changes fastest.
Arguments:
- tokens: bfloat16 [2, 32768, 4096], P(None, ('engine', 'expert')), may hold values from -6 to 6
- expert_ids: int32 [2, 32768, 2], P(None, ('engine', 'expert')), may hold values from 0 to 15, all different within a row; in each aligned block of 128 rows (0 to 127, 128 to 255, ..., all dimensions but the last counted through in order) at most 24 rows name the same one
- route_gain: float32 [2, 32768, 2], P(None, ('engine', 'expert')), may hold values from 0.1 to 1
- gate_up_master: float32 [16, 4096, 1536], P('expert', 'engine'), may hold values from -0.09375 to 0.09375
- gate_up_moment: float32 [16, 4096, 1536], P('expert', 'engine'), may hold values from -0.09375 to 0.09375
- gate_up_grad: bfloat16 [16, 4096, 1536], P('expert', 'engine'), may hold values from -0.09375 to 0.09375
- down_master: float32 [16, 768, 4096], P('expert', None, 'engine'), may hold values from -0.21875 to 0.21875
- down_moment: float32 [16, 768, 4096], P('expert', None, 'engine'), may hold values from -0.21875 to 0.21875
- down_grad: bfloat16 [16, 768, 4096], P('expert', None, 'engine'), may hold values from -0.21875 to 0.21875
Outputs:
- mixed: bfloat16 [2, 32768, 4096], P(None, ('engine', 'expert'))
Inputs may be any that keep to these rules, and one draw needn't show every extreme that they name: `expert_ids`: in each aligned block of 128 rows of one step, no expert is named by more than 24 rows, a bound that some block reaches; a row names 2 different experts.
All inputs are finite; a program needn't handle non-finite values.
Results may differ from a plain program's by a relative error of at most 0.0081.
Values may be sent and summed in bfloat16 or wider, within the bound.
No kernel may reach another device: no remote copies, remote signals or barrier semaphores. Data moves between devices by JAX's collectives and lax.ppermute only.
A program may use at most 128 MiB of HBM per device.

v0:
```python
import jax
import jax.numpy as jnp
from jax import lax
from jax.sharding import PartitionSpec as P


def updated(master, moment, grad):
    return (master - 0.5 * (0.8 * moment + 0.2 * grad.astype(jnp.float32))).astype(jnp.bfloat16)


def per_device(
    tokens,
    expert_ids,
    route_gain,
    gate_up_master,
    gate_up_moment,
    gate_up_grad,
    down_master,
    down_moment,
    down_grad,
):
    steps, row_dev, top_k = expert_ids.shape
    hidden_units = down_master.shape[1]
    experts = gate_up_master.shape[0] * lax.axis_size("expert")
    capacity = 3 * row_dev * top_k // (2 * experts)
    gate_up_weight = updated(gate_up_master, gate_up_moment, gate_up_grad)
    down_weight = updated(down_master, down_moment, down_grad)
    flat_ids = expert_ids.reshape(steps, row_dev * top_k)
    picked = (flat_ids[:, :, None] == jnp.arange(experts, dtype=jnp.int32)[None, None, :]).astype(
        jnp.int32
    )
    earlier = jnp.cumsum(picked, axis=1) - picked
    slot_index = jnp.sum(earlier * picked, axis=2)
    target = (flat_ids * capacity + slot_index).reshape(steps, row_dev, top_k).transpose(0, 2, 1)
    places = jnp.arange(experts * capacity, dtype=jnp.int32)
    matches = target[:, None, :, :] == places[None, :, None, None]
    dispatch_table = jnp.sum(matches.astype(jnp.int32), axis=2).astype(jnp.bfloat16)
    outgoing = jnp.einsum(
        "spr,srd->spd", dispatch_table, tokens, preferred_element_type=jnp.float32
    ).astype(jnp.bfloat16)
    outgoing = outgoing.reshape(steps, experts, capacity, tokens.shape[2])
    received = lax.all_to_all(outgoing, "expert", split_axis=1, concat_axis=2, tiled=True)
    projected = jnp.einsum(
        "tesd,edf->tesf",
        received,
        lax.all_gather(gate_up_weight, "engine", axis=1, tiled=True),
        preferred_element_type=jnp.float32,
    )
    hidden = (jax.nn.silu(projected[..., :hidden_units]) * projected[..., hidden_units:]).astype(
        jnp.bfloat16
    )
    expert_out = jnp.einsum(
        "tesf,efd->tesd",
        hidden,
        lax.all_gather(down_weight, "engine", axis=2, tiled=True),
        preferred_element_type=jnp.float32,
    ).astype(jnp.bfloat16)
    returned = lax.all_to_all(expert_out, "expert", split_axis=2, concat_axis=1, tiled=True)
    returned = returned.reshape(steps, experts * capacity, tokens.shape[2])
    share = (route_gain / jnp.sum(route_gain, axis=2, keepdims=True)).astype(jnp.bfloat16)
    share_by_k = share.transpose(0, 2, 1)[:, None, :, :]
    weighted = jnp.where(matches, share_by_k, jnp.zeros((), jnp.bfloat16))
    combine_table = jnp.sum(weighted.astype(jnp.float32), axis=2).astype(jnp.bfloat16)
    mixed = jnp.einsum("spr,spd->srd", combine_table, returned, preferred_element_type=jnp.float32)
    return mixed.astype(jnp.bfloat16)


def solution(mesh):
    return jax.shard_map(
        per_device,
        mesh=mesh,
        in_specs=(
            P(None, ("engine", "expert"), None),
            P(None, ("engine", "expert"), None),
            P(None, ("engine", "expert"), None),
            P("expert", "engine", None),
            P("expert", "engine", None),
            P("expert", "engine", None),
            P("expert", None, "engine"),
            P("expert", None, "engine"),
            P("expert", None, "engine"),
        ),
        out_specs=P(None, ("engine", "expert"), None),
        check_vma=False,
    )
```

profile of v0, /device:TPU:8, one launch (start us, length us, event | category | flops | bytes accessed | tf_op | source)
XLA Modules:
  0.0 474.6 jit_solution(18320085007874012513)
XLA Ops:
  6.5 0.0 copy-start
  6.5 0.0 all-gather.5.cloned.1.call-start
  6.5 3.2 copy.74
  9.7 3.0 copy.76
  12.7 1.4 copy.75
  14.1 0.0 copy-start.5
  14.2 3.1 subtract_convert_fusion
  17.3 0.0 all-gather.5.cloned.1.call-update
  17.3 0.0 copy-done.5
  17.3 0.1 copy.67
  17.4 0.1 eq.42
  17.6 0.1 eq.38
  17.8 1.2 reduce-window.6
  18.9 0.2 slice_reduce_fusion
  19.2 0.1 fusion.27
  19.3 0.1 reduce_sum.42
  19.4 0.1 copy.70
  19.5 0.1 convert_reduce_fusion
  19.6 0.0 copy-done
  19.6 1.8 convolution_convert_fusion
  21.4 3.0 copy.77
  24.5 0.0 copy-start.2
  24.5 0.0 copy-start.3
  24.5 11.7 %all-to-all-start = ((bf16[2,16,24,4096]{3,2,0,1:T(8,128)(2,1)}), bf16[2,16,24,4096]{3,2,0,1:T(8,128)(2,1)}, u32[]{:S(2)}, u32[]{:S(2)}) async-start(bf16[2,16,24,4096]{3,2,0,1:T(8,128)(2,1)} %copy.77), calls=%async_computation | async-start | bytes 12582912 | tf_op jit(solution)/shard_map/all_to_all | solution.py:42
  36.1 0.0 copy-start.4
  36.2 0.2 all-gather.3.cloned.1.call-start
  36.4 0.0 copy-done.2
  36.4 0.3 copy.71
  36.7 0.0 copy-done.3
  36.7 0.3 copy.73
  37.0 0.2 copy-done.4
  37.1 0.2 copy.72
  37.3 0.9 subtract_convert_fusion.1
  38.2 0.0 all-gather.3.cloned.1.call-update
  38.3 193.8 %all-to-all-done = bf16[2,16,24,4096]{3,2,0,1:T(8,128)(2,1)} async-done(((bf16[2,16,24,4096]{3,2,0,1:T(8,128)(2,1)}), bf16[2,16,24,4096]{3,2,0,1:T(8,128)(2,1)}, u32[]{:S(2)}, u32[]{:S(2)}) %all-to-all-start) | async-done | bytes 6291488 | tf_op jit(solution)/shard_map/all_to_all | solution.py:42
  232.1 6.2 %copy.78 = bf16[2,16,24,4096]{3,2,1,0:T(8,128)(2,1)} copy(bf16[2,16,24,4096]{3,2,0,1:T(8,128)(2,1)} %all-to-all-done) | data formatting | bytes 12582912 | tf_op jit(solution)/shard_map/all_to_all | solution.py:42
  238.2 0.0 all-gather.5.cloned.1.call-done
  238.2 15.9 %fusion.13 = f32[2,1,384,1536]{2,3,0,1:T(8,128)} fusion(bf16[2,384,4096]{2,1,0:T(8,128)(2,1)} %bitcast.58, bf16[1,4096,1536]{1,2,0:T(8,128)(2,1)} %all-gather.5.cloned.1.call-done), kind=kOutput, calls=%fused_computation.11 | convolution fusion | flops 9663676416 | bytes 23592960 | tf_op jit(solution)/shard_map/tesd,edf->tesf/dot_general | solution.py:43
  254.1 18.1 %all-gather.3.cloned.1.call-done = bf16[1,768,4096]{1,2,0:T(8,128)(2,1)} async-done(((bf16[1,768,256]{1,2,0:T(8,128)(2,1)}), bf16[1,768,4096]{1,2,0:T(8,128)(2,1)}) %all-gather.3.cloned.1.call-update) | async-done | bytes 6291472 | tf_op jit(solution)/shard_map/all_gather | solution.py:55
  272.2 10.6 %fusion.7 = bf16[2,1,384,4096]{2,3,0,1:T(8,128)(2,1)} fusion(bf16[1,768,4096]{1,2,0:T(8,128)(2,1)} %all-gather.3.cloned.1.call-done, f32[2,1,384,1536]{2,3,0,1:T(8,128)} %fusion.13), kind=kOutput, calls=%fused_computation.9 | convolution fusion | flops 4838522880 | bytes 17301504 | tf_op jit(solution)/shard_map/tesf,efd->tesd/dot_general | solution.py:52
  282.7 16.2 %copy.80 = bf16[2,1,384,4096]{3,0,1,2:T(2,128)(2,1)} copy(bf16[2,1,384,4096]{2,3,0,1:T(8,128)(2,1)} %fusion.7) | data formatting | bytes 12582912 | tf_op jit(solution)/shard_map/convert_element_type | solution.py:57
  299.0 9.9 %all-to-all-start.1 = ((bf16[2,1,384,4096]{3,0,1,2:T(2,128)(2,1)}), bf16[2,1,384,4096]{3,0,1,2:T(2,128)(2,1)}, u32[]{:S(2)}, u32[]{:S(2)}) async-start(bf16[2,1,384,4096]{3,0,1,2:T(2,128)(2,1)} %copy.80), calls=%async_computation.1 | async-start | bytes 12582912 | tf_op jit(solution)/shard_map/all_to_all | solution.py:58
  308.9 0.0 copy-done.6
  308.9 0.0 copy-start.1
  308.9 0.1 fusion.23
  309.0 147.3 %all-to-all-done.1 = bf16[2,1,384,4096]{3,0,1,2:T(2,128)(2,1)} async-done(((bf16[2,1,384,4096]{3,0,1,2:T(2,128)(2,1)}), bf16[2,1,384,4096]{3,0,1,2:T(2,128)(2,1)}, u32[]{:S(2)}, u32[]{:S(2)}) %all-to-all-start.1) | async-done | bytes 6291488 | tf_op jit(solution)/shard_map/all_to_all | solution.py:58
  456.3 11.4 %fusion.10 = bf16[2,128,4096]{2,1,0:T(8,128)(2,1)} fusion(bf16[2,384,128]{2,1,0:T(8,128)(2,1)S(1)} %fusion.23, bf16[2,1,384,4096]{3,0,1,2:T(2,128)(2,1)} %all-to-all-done.1), kind=kOutput, calls=%fused_computation.10 | convolution fusion | flops 806354944 | bytes 8585216 | tf_op jit(solution)/shard_map/spr,spd->srd/dot_general | solution.py:64
  467.8 0.0 copy-done.1
  (6 shorter events, 0.1 us)
Async XLA Ops:
  6.5 13.1 %copy-start = (bf16[2,128,4096]{2,1,0:T(8,128)(2,1)S(1)}, bf16[2,128,4096]{2,1,0:T(8,128)(2,1)}, u32[]{:S(2)}) copy-start(bf16[2,128,4096]{2,1,0:T(8,128)(2,1)} %param.9) | copy-start | bytes 6291460
  6.5 231.7 %all-gather.5.cloned.1.call-start = ((), (), s32[]{:S(2)}) async-start(), calls=%async_computation.3 | async-start | bytes 13369344 | tf_op jit(solution)/shard_map/all_gather | solution.py:46
  14.1 3.2 copy-start.5
  24.5 11.9 %copy-start.2 = (f32[1,768,256]{2,1,0:T(8,128)S(1)}, f32[1,768,256]{2,1,0:T(8,128)}, u32[]{:S(2)}) copy-start(f32[1,768,256]{2,1,0:T(8,128)} %param.16) | copy-start | bytes 2359300
  24.5 12.2 %copy-start.3 = (f32[1,768,256]{2,1,0:T(8,128)S(1)}, f32[1,768,256]{2,1,0:T(8,128)}, u32[]{:S(2)}) copy-start(f32[1,768,256]{2,1,0:T(8,128)} %param.15) | copy-start | bytes 2359300
  24.5 207.6 %all-to-all-start = ((bf16[2,16,24,4096]{3,2,0,1:T(8,128)(2,1)}), bf16[2,16,24,4096]{3,2,0,1:T(8,128)(2,1)}, u32[]{:S(2)}, u32[]{:S(2)}) async-start(bf16[2,16,24,4096]{3,2,0,1:T(8,128)(2,1)} %copy.77), calls=%async_computation | async-start | bytes 12582912 | tf_op jit(solution)/shard_map/all_to_all | solution.py:42
  36.1 1.0 copy-start.4
  36.2 236.0 %all-gather.3.cloned.1.call-start = ((), (), s32[]{:S(2)}) async-start(), calls=%async_computation.2 | async-start | bytes 6684672 | tf_op jit(solution)/shard_map/all_gather | solution.py:55
  298.9 9.9 %copy-start.6 = (f32[2,128,2]{1,2,0:T(2,128)S(1)}, f32[2,128,2]{1,2,0:T(2,128)}, u32[]{:S(2)}) copy-start(f32[2,128,2]{1,2,0:T(2,128)} %param.11) | copy-start | bytes 6148
  299.0 157.4 %all-to-all-start.1 = ((bf16[2,1,384,4096]{3,0,1,2:T(2,128)(2,1)}), bf16[2,1,384,4096]{3,0,1,2:T(2,128)(2,1)}, u32[]{:S(2)}, u32[]{:S(2)}) async-start(bf16[2,1,384,4096]{3,0,1,2:T(2,128)(2,1)} %copy.80), calls=%async_computation.1 | async-start | bytes 12582912 | tf_op jit(solution)/shard_map/all_to_all | solution.py:58
  308.9 158.9 %copy-start.1 = (bf16[2,128,4096]{2,1,0:T(8,128)(2,1)S(1)}, bf16[2,128,4096]{2,1,0:T(8,128)(2,1)}, u32[]{:S(2)}) copy-start(bf16[2,128,4096]{2,1,0:T(8,128)(2,1)} %param.9) | copy-start | bytes 6291460
Sparse Core Ops, SparseCore 0:
  17.4 203.1 all-gather.4
  222.4 49.6 all-gather.2
where the time goes:
time: 476 us; the launch traced here: 475 us
  waiting for transfers between devices  359 us (75%)
  matrix products  39.7 us (8%)
  local copies, waits for them, and re-layouts  34.8 us (7%)
  starting transfers between devices  21.9 us (5%)
  between operations  13.5 us (3%)
  other arithmetic  5.55 us (1%)
    all_to_all x1, waiting for transfers between devices, per_device(): lax.all_to_all(outgoing, 'expert', split_axis=1, concat_axis=2, tiled=True)  194 us
    all_to_all x1, waiting for transfers between devices, per_device(): lax.all_to_all(expert_out, 'expert', split_axis=2, concat_axis=1, tiled=T...  147 us
    all_gather x1, waiting for transfers between devices, per_device(): lax.all_gather(down_weight, 'engine', axis=2, tiled=True)  18.1 us
    convert_element_type x1, local copies, waits for them, and re-layouts, per_device(): expert_out = jnp.einsum('tesf,efd->tesd', hidden, lax.all_gather(down_wei...  16.2 us
    dot_general x1, matrix products, per_device(): jnp.einsum('tesd,edf->tesf', received, lax.all_gather(gate_up_weight, 'en...  15.9 us
    all_to_all x1, starting transfers between devices, per_device(): lax.all_to_all(outgoing, 'expert', split_axis=1, concat_axis=2, tiled=True)  11.7 us
    dot_general x1, matrix products, per_device(): jnp.einsum('spr,spd->srd', combine_table, returned, preferred_element_typ...  11.4 us
    dot_general x1, matrix products, per_device(): jnp.einsum('tesf,efd->tesd', hidden, lax.all_gather(down_weight, 'engine'...  10.6 us
  transfers between devices with their start and end apart: 4, of which 3 were waited for; matrix products, arithmetic and copies ran while one was open for 6% of the time, Pallas kernels for 0%

commit v1 on v0

v1 whole, which is shorter than its diff:
```python
import jax
import jax.numpy as jnp
from jax import lax
from jax.experimental import pallas as pl
from jax.experimental.pallas import tpu as pltpu
from jax.sharding import Mesh, PartitionSpec as P

AXES = ("x", "zl", "core", "zh", "y")
NX, NZL, NC, NZH, NY = 4, 2, 2, 4, 4
MIB = 1 << 20


def updated(master, moment, grad):
    return (master - 0.5 * (0.8 * moment + 0.2 * grad.astype(jnp.float32))).astype(jnp.bfloat16)


def flat(x, zl, c, zh):
    return ((x * NZL + zl) * NC + c) * NZH + zh


def offset_of(x, zl, c):
    return (x + 2 * zl + c) % NZH


def places():
    return [
        (x, zl, c, zh)
        for x in range(NX)
        for zl in range(NZL)
        for c in range(NC)
        for zh in range(NZH)
    ]


SHIFT_Z = [
    (flat(x, zl, c, zh), flat(x, zl, c, (zh + offset_of(x, zl, c)) % NZH))
    for x, zl, c, zh in places()
]
MOVE_X = [
    (flat(x, zl, c, zh), flat((zh - offset_of(x, zl, c)) % NX, zl, c, zh))
    for x, zl, c, zh in places()
]


def ring_index(z):
    return (z % NZL) * NZH + z // NZL


NZ = NZL * NZH
UP = [(ring_index(z), ring_index((z + 1) % NZ)) for z in range(NZ)]
DOWN = [(ring_index(z), ring_index((z - 1) % NZ)) for z in range(NZ)]


def spread(block):
    block = lax.ppermute(block, ("x", "zl", "core", "zh"), SHIFT_Z)
    return lax.ppermute(block, ("x", "zl", "core", "zh"), MOVE_X)


def up(block):
    return lax.ppermute(block, ("zl", "zh"), UP)


def down(block):
    return lax.ppermute(block, ("zl", "zh"), DOWN)


def other_core(block):
    return lax.ppermute(block, "core", [(0, 1), (1, 0)])


def ring(block):
    half = block.shape[0] // 2
    u1, d1 = up(block), down(block)
    u2, d2 = up(u1), down(d1)
    u3, d3 = up(u2), down(d2)
    u4, d4 = up(u3[:half]), down(d3[half:])
    mine = [block, u1, d1, u2, d2, u3, d3, u4, d4]
    return mine + [other_core(piece) for piece in mine]


def shard_table():
    x, zl, c, zh = (lax.axis_index(name) for name in ("x", "zl", "core", "zh"))
    z = NZL * zh + zl
    entries = []
    for core in (c, 1 - c):
        for step in (0, 1, -1, 2, -2, 3, -3, 4):
            at = (z - step + NZ) % NZ
            at_zl, at_zh = at % NZL, at // NZL
            from_x = (at_zh - x - 2 * at_zl - core + 2 * NX) % NX
            entries.append((from_x * NZL + at_zl) * NC + core)
    return jnp.stack(entries).astype(jnp.int32)


def weight_copies(table, pieces, target, sems):
    rows = pieces[0].shape[0]
    half = rows // 2
    copies = []
    for n, piece in enumerate(pieces):
        core, k = divmod(n, 9)
        slot = table[core * 8 + min(k, 7)]
        first = half if k == 8 else 0
        copies.append(
            pltpu.make_async_copy(
                piece, target.at[slot, pl.ds(first, piece.shape[0]), :], sems.at[n]
            )
        )
    return copies


def hidden_kernel(table, x_hbm, *refs):
    pieces, (h_ref, x_buf, w_buf, sems, x_sem) = refs[:18], refs[18:]
    copies = weight_copies(table, pieces, w_buf, sems)
    x_copy = pltpu.make_async_copy(x_hbm, x_buf, x_sem)
    x_copy.start()
    for copy in copies:
        copy.start()
    x_copy.wait()
    for copy in copies:
        copy.wait()
    shards, depth, wide = w_buf.shape
    units = wide // 2
    tile = 256
    for n in range(units // tile):
        w_gate = w_buf[:, :, n * tile : (n + 1) * tile].reshape(shards * depth, tile)
        w_up = w_buf[:, :, units + n * tile : units + (n + 1) * tile].reshape(shards * depth, tile)
        gate = jnp.dot(x_buf[...], w_gate, preferred_element_type=jnp.float32)
        upper = jnp.dot(x_buf[...], w_up, preferred_element_type=jnp.float32)
        h_ref[:, n * tile : (n + 1) * tile] = (gate / (1.0 + jnp.exp(-gate)) * upper).astype(
            h_ref.dtype
        )


def out_kernel(table, h_ref, *refs):
    pieces, (o_ref, w_buf, sems) = refs[:18], refs[18:]
    copies = weight_copies(table, pieces, w_buf, sems)
    for copy in copies:
        copy.start()
    for copy in copies:
        copy.wait()
    shards, _, wide = w_buf.shape
    for s in range(shards):
        o_ref[:, s * wide : (s + 1) * wide] = jnp.dot(
            h_ref[...], w_buf[s], preferred_element_type=jnp.float32
        ).astype(o_ref.dtype)


ANY = pl.BlockSpec(memory_space=pl.ANY)
VMEM = pl.BlockSpec(memory_space=pltpu.VMEM)
SMEM = pl.BlockSpec(memory_space=pltpu.SMEM)


def hidden_of(table, x, pieces):
    rows, wide = x.shape
    depth, cols = pieces[0].shape
    return pl.pallas_call(
        hidden_kernel,
        out_shape=jax.ShapeDtypeStruct((rows, cols // 2), jnp.bfloat16),
        in_specs=[SMEM, ANY] + [ANY] * len(pieces),
        out_specs=VMEM,
        scratch_shapes=[
            pltpu.VMEM((rows, wide), jnp.bfloat16),
            pltpu.VMEM((16, depth, cols), jnp.bfloat16),
            pltpu.SemaphoreType.DMA((len(pieces),)),
            pltpu.SemaphoreType.DMA,
        ],
        compiler_params=pltpu.CompilerParams(vmem_limit_bytes=40 * MIB),
        cost_estimate=pl.CostEstimate(
            flops=2 * rows * wide * cols, bytes_accessed=19 * MIB, transcendentals=rows * cols // 2
        ),
        name="hidden",
    )(table, x, *pieces)


def outputs_of(table, h, pieces):
    rows, units = h.shape
    _, cols = pieces[0].shape
    return pl.pallas_call(
        out_kernel,
        out_shape=jax.ShapeDtypeStruct((rows, 16 * cols), jnp.bfloat16),
        in_specs=[SMEM, VMEM] + [ANY] * len(pieces),
        out_specs=VMEM,
        scratch_shapes=[
            pltpu.VMEM((16, units, cols), jnp.bfloat16),
            pltpu.SemaphoreType.DMA((len(pieces),)),
        ],
        compiler_params=pltpu.CompilerParams(vmem_limit_bytes=30 * MIB),
        cost_estimate=pl.CostEstimate(
            flops=2 * rows * units * cols * 16, bytes_accessed=13 * MIB, transcendentals=0
        ),
        name="expert_out",
    )(table, h, *pieces)


def per_device(
    tokens,
    expert_ids,
    route_gain,
    gate_up_master,
    gate_up_moment,
    gate_up_grad,
    down_master,
    down_moment,
    down_grad,
):
    steps, row_dev, top_k = expert_ids.shape
    width = tokens.shape[2]
    experts = NX * NY
    capacity = 3 * row_dev * top_k // (2 * experts)
    per_expert = steps * capacity
    rows = steps * row_dev
    gate_up_weight = updated(gate_up_master[0], gate_up_moment[0], gate_up_grad[0])
    gate_up_pieces = ring(spread(gate_up_weight))
    down_weight = updated(down_master[0], down_moment[0], down_grad[0])
    down_pieces = ring(spread(down_weight))
    table = shard_table()

    names = expert_ids[..., None] == jnp.arange(experts, dtype=jnp.int32)
    named = jnp.any(names, axis=2).astype(jnp.bfloat16)
    order = jnp.arange(row_dev)
    before = (order[:, None] > order[None, :]).astype(jnp.bfloat16)
    earlier = jnp.einsum("rq,sqe->sre", before, named, preferred_element_type=jnp.float32)
    slot_index = jnp.sum(jnp.where(names, earlier[:, :, None, :], 0.0), axis=3).astype(jnp.int32)
    step_base = capacity * jnp.arange(steps, dtype=jnp.int32)[:, None, None]
    target = (expert_ids * per_expert + step_base + slot_index).reshape(rows, top_k)
    slots = jnp.arange(experts * per_expert, dtype=jnp.int32)
    hits = target[:, None, :] == slots[None, :, None]
    dispatch_table = jnp.any(hits, axis=2).astype(jnp.bfloat16)
    outgoing = jnp.einsum(
        "rp,rd->pd",
        dispatch_table,
        tokens.reshape(rows, width),
        preferred_element_type=jnp.float32,
    ).astype(jnp.bfloat16)
    received = lax.all_to_all(outgoing, ("x", "y"), split_axis=0, concat_axis=0, tiled=True)

    hidden = hidden_of(table, received, gate_up_pieces)
    expert_out = outputs_of(table, hidden, down_pieces)

    returned = lax.all_to_all(expert_out, ("x", "y"), split_axis=0, concat_axis=0, tiled=True)
    share = (route_gain / jnp.sum(route_gain, axis=2, keepdims=True)).astype(jnp.bfloat16)
    share = share.reshape(rows, 1, top_k)
    combine_table = jnp.sum(
        jnp.where(hits, share.astype(jnp.float32), 0.0), axis=2
    ).astype(jnp.bfloat16)
    mixed = jnp.dot(combine_table, returned, preferred_element_type=jnp.float32)
    return mixed.astype(jnp.bfloat16).reshape(steps, row_dev, width)


def solution(mesh):
    grid = Mesh(mesh.devices.reshape(NX, NZL, NC, NZH, NY), AXES)
    engine, expert = ("x", "zl", "core"), ("zh", "y")
    rows = P(None, AXES, None)
    return jax.shard_map(
        per_device,
        mesh=grid,
        in_specs=(
            rows,
            rows,
            rows,
            P(expert, engine, None),
            P(expert, engine, None),
            P(expert, engine, None),
            P(expert, None, engine),
            P(expert, None, engine),
            P(expert, None, engine),
        ),
        out_specs=rows,
        check_vma=False,
    )
```

time: 476 us -> 425 us (0.89)
  the two profiles are of different devices: /device:TPU:8 before, /device:TPU:92 now
where the time goes in v1:
time: 425 us; the launch traced here: 420 us
  waiting for transfers between devices  250 us (59%)
  starting transfers between devices  103 us (24%)
  local copies, waits for them, and re-layouts  25.6 us (6%)
  Pallas kernels  25.1 us (6%)
  matrix products  10.6 us (2%)
  other arithmetic  5.38 us (1%)
    all_to_all x1, waiting for transfers between devices, per_device(): lax.all_to_all(expert_out, ('x', 'y'), split_axis=0, concat_axis=0, tiled...  111 us
    ppermute x2, waiting for transfers between devices, spread(): return lax.ppermute(block, ('x', 'zl', 'core', 'zh'), MOVE_X)  58.4 us
    all_to_all x1, starting transfers between devices, per_device(): lax.all_to_all(expert_out, ('x', 'y'), split_axis=0, concat_axis=0, tiled...  32.1 us
    ppermute x8, waiting for transfers between devices, up(): return lax.ppermute(block, ('zl', 'zh'), UP)  30.8 us
    ppermute x2, waiting for transfers between devices, spread(): block = lax.ppermute(block, ('x', 'zl', 'core', 'zh'), SHIFT_Z)  27 us
    ppermute x8, starting transfers between devices, up(): return lax.ppermute(block, ('zl', 'zh'), UP)  26.4 us
    unnamed x90, local copies, waits for them, and re-layouts  24.4 us
    ppermute x8, waiting for transfers between devices, down(): return lax.ppermute(block, ('zl', 'zh'), DOWN)  22 us
  transfers between devices with their start and end apart: 40, of which 15 were waited for; matrix products, arithmetic and copies ran while one was open for 1% of the time, Pallas kernels for 4%

profile of v1, /device:TPU:92, one launch (start us, length us, event | category | flops | bytes accessed | tf_op | source)
XLA Modules:
  0.0 419.8 jit_solution(3641532760501018770)
XLA Ops:
  2.7 4.5 %convolution_convert_fusion = bf16[768,4096]{1,0:T(8,128)(2,1)} fusion(pred[256,768]{1,0:T(8,128)(4,1)S(1)} %fusion.1, bf16[256,4096]{1,0:T(8,128)(2,1)S(1)} %bitcast.44), kind=kOutput, calls=%fused_computation.1 | convolution fusion | flops 1613758464 | bytes 8585216 | tf_op jit(solution)/shard_map/rp,rd->pd/dot_general | solution.py:228
  7.2 7.2 %all-to-all-start = ((bf16[16,48,4096]{2,1,0:T(8,128)(2,1)}), bf16[16,48,4096]{2,1,0:T(8,128)(2,1)}, u32[]{:S(2)}, u32[]{:S(2)}) async-start(bf16[16,48,4096]{2,1,0:T(8,128)(2,1)} %bitcast.46), calls=%async_computation | async-start | bytes 12582912 | tf_op jit(solution)/shard_map/all_to_all | solution.py:234
  14.5 2.4 fusion.6
  16.9 7.3 %collective-permute-start = (bf16[256,1536]{1,0:T(8,128)(2,1)S(1)}, bf16[256,1536]{1,0:T(8,128)(2,1)S(1)}, u32[]{:S(2)}, u32[]{:S(2)}) collective-permute-start(bf16[256,1536]{1,0:T(8,128)(2,1)S(1)} %fusion.6), channel_id=1, source_target_pairs={{0,0},{4,4},{8,8},{12,12},{16,20},{20,24},{24,28},{28,16},{32,40},... | collective-permute-start | bytes 2359304 | tf_op jit(solution)/shard_map/ppermute | solution.py:55
  24.2 27.0 %collective-permute-done = bf16[256,1536]{1,0:T(8,128)(2,1)S(1)} collective-permute-done((bf16[256,1536]{1,0:T(8,128)(2,1)S(1)}, bf16[256,1536]{1,0:T(8,128)(2,1)S(1)}, u32[]{:S(2)}, u32[]{:S(2)}) %collective-permute-start) | collective-permute-done | bytes 786464 | tf_op jit(solution)/shard_map/ppermute | solution.py:55
  51.2 1.9 collective-permute-start.1
  53.4 3.5 collective-permute-start.19
  56.9 51.8 %collective-permute-done.1.refs_0_ = bf16[256,1536]{1,0:T(8,128)(2,1)S(1)} collective-permute-done((bf16[256,1536]{1,0:T(8,128)(2,1)S(1)}, bf16[256,1536]{1,0:T(8,128)(2,1)S(1)}, u32[]{:S(2)}, u32[]{:S(2)}) %collective-permute-start.1) | collective-permute-done | bytes 786464 | tf_op jit(solution)/shard_map/ppermute | solution.py:56
  108.7 1.9 collective-permute-start.20
  110.6 4.2 %collective-permute-start.3 = (bf16[256,1536]{1,0:T(8,128)(2,1)S(1)}, bf16[256,1536]{1,0:T(8,128)(2,1)S(1)}, u32[]{:S(2)}, u32[]{:S(2)}) collective-permute-start(bf16[256,1536]{1,0:T(8,128)(2,1)S(1)} %collective-permute-done.1.refs_0_), channel_id=1, source_target_pairs={{0,44},{32,0},{4,32},{36,4},{8,36},{40,8},{12,40},{44,12},{1,45},{... | collective-permute-start | bytes 2359304 | tf_op jit(solution)/shard_map/ppermute | solution.py:64
  114.8 6.7 %collective-permute-done.20.refs_0_ = bf16[768,256]{1,0:T(8,128)(2,1)S(1)} collective-permute-done((bf16[768,256]{1,0:T(8,128)(2,1)S(1)}, bf16[768,256]{1,0:T(8,128)(2,1)S(1)}, u32[]{:S(2)}, u32[]{:S(2)}) %collective-permute-start.20) | collective-permute-done | bytes 393248 | tf_op jit(solution)/shard_map/ppermute | solution.py:56
  121.5 2.2 collective-permute-start.21
  124.0 5.2 %collective-permute-start.4 = (bf16[256,1536]{1,0:T(8,128)(2,1)S(1)}, bf16[256,1536]{1,0:T(8,128)(2,1)S(1)}, u32[]{:S(2)}, u32[]{:S(2)}) collective-permute-start(bf16[256,1536]{1,0:T(8,128)(2,1)S(1)} %collective-permute-done.2.refs_1_), channel_id=1, source_target_pairs={{0,32},{32,4},{4,36},{36,8},{8,40},{40,12},{12,44},{44,0},{1,33},{... | collective-permute-start | bytes 2359304 | tf_op jit(solution)/shard_map/ppermute | solution.py:60
  129.3 4.3 %collective-permute-done.21.refs_1_ = bf16[768,256]{1,0:T(8,128)(2,1)S(1)} collective-permute-done((bf16[768,256]{1,0:T(8,128)(2,1)S(1)}, bf16[768,256]{1,0:T(8,128)(2,1)S(1)}, u32[]{:S(2)}, u32[]{:S(2)}) %collective-permute-start.21) | collective-permute-done | bytes 393248 | tf_op jit(solution)/shard_map/ppermute | solution.py:60
  133.5 4.2 collective-permute-start.23
  137.7 3.5 collective-permute-done.22.refs_2_
  141.2 2.5 collective-permute-start.24
  145.3 10.8 %collective-permute-done.23.refs_3_ = bf16[768,256]{1,0:T(8,128)(2,1)S(1)} collective-permute-done((bf16[768,256]{1,0:T(8,128)(2,1)S(1)}, bf16[768,256]{1,0:T(8,128)(2,1)S(1)}, u32[]{:S(2)}, u32[]{:S(2)}) %collective-permute-start.23) | collective-permute-done | bytes 393248 | tf_op jit(solution)/shard_map/ppermute | solution.py:60
  156.1 4.2 %collective-permute-start.25 = (bf16[768,256]{1,0:T(8,128)(2,1)S(1)}, bf16[768,256]{1,0:T(8,128)(2,1)S(1)}, u32[]{:S(2)}, u32[]{:S(2)}) collective-permute-start(bf16[768,256]{1,0:T(8,128)(2,1)S(1)} %collective-permute-done.23.refs_3_), channel_id=1, source_target_pairs={{0,32},{32,4},{4,36},{36,8},{8,40},{40,12},{12,44},{44,0},{1,33},{... | collective-permute-start | bytes 1179656 | tf_op jit(solution)/shard_map/ppermute | solution.py:60
  160.3 3.9 collective-permute-start.6
  165.7 2.2 collective-permute-start.26
  168.0 1.9 collective-permute-done.25.refs_5_
  171.4 3.7 collective-permute-start.27
  175.1 3.6 collective-permute-done.26.refs_6_
  181.8 5.5 %collective-permute-done.27.refs_7_ = bf16[384,256]{1,0:T(8,128)(2,1)S(1)} collective-permute-done((bf16[384,256]{1,0:T(8,128)(2,1)S(1)}, bf16[384,256]{1,0:T(8,128)(2,1)S(1)}, u32[]{:S(2)}, u32[]{:S(2)}) %collective-permute-start.27) | collective-permute-done | bytes 196640 | tf_op jit(solution)/shard_map/ppermute | solution.py:60
  189.6 5.9 %collective-permute-done.7.refs_6_ = bf16[256,1536]{1,0:T(8,128)(2,1)} collective-permute-done((bf16[256,1536]{1,0:T(8,128)(2,1)}, bf16[256,1536]{1,0:T(8,128)(2,1)}, u32[]{:S(2)}, u32[]{:S(2)}) %collective-permute-start.7) | collective-permute-done | bytes 786464 | tf_op jit(solution)/shard_map/ppermute | solution.py:64
  195.5 0.9 collective-permute-start.28
  196.5 1.0 slice.17
  197.5 5.7 %collective-permute-done.28.refs_8_ = bf16[384,256]{1,0:T(8,128)(2,1)S(1)} collective-permute-done((bf16[384,256]{1,0:T(8,128)(2,1)S(1)}, bf16[384,256]{1,0:T(8,128)(2,1)S(1)}, u32[]{:S(2)}, u32[]{:S(2)}) %collective-permute-start.28) | collective-permute-done | bytes 196640 | tf_op jit(solution)/shard_map/ppermute | solution.py:64
  205.6 0.9 copy-done.16
  206.5 3.0 collective-permute-start.8
  210.3 8.1 %collective-permute-done.8.refs_7_ = bf16[128,1536]{1,0:T(8,128)(2,1)} collective-permute-done((bf16[128,1536]{1,0:T(8,128)(2,1)S(1)}, bf16[128,1536]{1,0:T(8,128)(2,1)}, u32[]{:S(2)}, u32[]{:S(2)}) %collective-permute-start.8) | collective-permute-done | bytes 393248 | tf_op jit(solution)/shard_map/ppermute | solution.py:60
  218.5 3.2 collective-permute-done.9.refs_8_
  222.4 9.8 %collective-permute-start.34 = (bf16[768,256]{1,0:T(8,128)(2,1)S(1)}, bf16[768,256]{1,0:T(8,128)(2,1)}, u32[]{:S(2)}, u32[]{:S(2)}) collective-permute-start(bf16[768,256]{1,0:T(8,128)(2,1)S(1)} %collective-permute-done.25.refs_5_), channel_id=1, source_target_pairs={{0,16},{16,0},{1,17},{17,1},{2,18},{18,2},{3,19},{19,3},{4,20},{20... | collective-permute-start | bytes 1179656 | tf_op jit(solution)/shard_map/ppermute | solution.py:68
  232.9 1.1 copy-done.5
  234.0 1.1 copy-done.7
  235.1 1.1 copy-done.9
  236.3 1.1 copy-done.11
  237.4 1.1 copy-done.13
  238.5 1.1 copy-done.15
  239.7 1.1 copy-done.17
  240.8 1.1 copy-done.19
  242.0 15.2 %hidden.1.h_ref = bf16[768,768]{1,0:T(8,128)(2,1)S(1)} custom-call(s32[16]{0:T(128)S(1)} %stack.67.table, bf16[768,4096]{1,0:T(8,128)(2,1)} %bitcast.22.x_hbm, bf16[256,1536]{1,0:T(8,128)(2,1)S(1)} %copy-done.5, bf16[256,1536]{1,0:T(8,128)(2,1)S(1)} %copy-done.7, bf16[256,1536]{1,0:T(8,128)(2,1)S(1)} %copy-done.9, bf16[256,1536]{1,0:T(8,128)(2,1)S(1)} %copy-done.11, ...), custom_call_target="tpu_custom_call" | custom-call | flops 9663676416 | bytes 19922944 | tf_op jit(solution)/shard_map/hidden/pallas_call | solution.py:155
  257.4 9.9 %expert_out.1 = bf16[768,4096]{1,0:T(8,128)(2,1)S(1)} custom-call(s32[16]{0:T(128)S(1)} %stack.67.table, bf16[768,768]{1,0:T(8,128)(2,1)S(1)} %hidden.1.h_ref, bf16[768,256]{1,0:T(8,128)(2,1)S(1)} %copy-done.21, bf16[768,256]{1,0:T(8,128)(2,1)S(1)} %copy-done.23, bf16[768,256]{1,0:T(8,128)(2,1)S(1)} %copy-done.25, bf16[768,256]{1,0:T(8,128)(2,1)S(1)} %copy-done.29, ...), custom_call_target="tpu_custom_call" | custom-call | flops 4831838208 | bytes 13631488 | tf_op jit(solution)/shard_map/expert_out/pallas_call | solution.py:177
  267.4 2.7 copy-done.1
  270.0 32.1 %all-to-all-start.1 = ((bf16[16,48,4096]{2,1,0:T(8,128)(2,1)}), bf16[16,48,4096]{2,1,0:T(8,128)(2,1)}, u32[]{:S(2)}, u32[]{:S(2)}) async-start(bf16[16,48,4096]{2,1,0:T(8,128)(2,1)} %bitcast.45), calls=%async_computation.1 | async-start | bytes 12582912 | tf_op jit(solution)/shard_map/all_to_all | solution.py:239
  302.3 111.4 %all-to-all-done.1 = bf16[16,48,4096]{2,1,0:T(8,128)(2,1)} async-done(((bf16[16,48,4096]{2,1,0:T(8,128)(2,1)}), bf16[16,48,4096]{2,1,0:T(8,128)(2,1)}, u32[]{:S(2)}, u32[]{:S(2)}) %all-to-all-start.1) | async-done | bytes 6291488 | tf_op jit(solution)/shard_map/all_to_all | solution.py:239
  413.7 5.9 %convolution_convert_fusion.1 = bf16[256,4096]{1,0:T(8,128)(2,1)} fusion(bf16[768,4096]{1,0:T(8,128)(2,1)} %bitcast.26, bf16[256,768]{1,0:T(8,128)(2,1)S(1)} %select_reduce_fusion), kind=kOutput, calls=%fused_computation.2 | convolution fusion | flops 1611661312 | bytes 8781824 | tf_op jit(solution)/shard_map/dot_general | solution.py:245
  (141 shorter events, 18.2 us)
Async XLA Ops:
  7.2 225.7 %all-to-all-start = ((bf16[16,48,4096]{2,1,0:T(8,128)(2,1)}), bf16[16,48,4096]{2,1,0:T(8,128)(2,1)}, u32[]{:S(2)}, u32[]{:S(2)}) async-start(bf16[16,48,4096]{2,1,0:T(8,128)(2,1)} %bitcast.46), calls=%async_computation | async-start | bytes 12582912 | tf_op jit(solution)/shard_map/all_to_all | solution.py:234
  14.5 38.7 %copy-start.41 = (f32[1,768,256]{2,1,0:T(8,128)S(1)}, f32[1,768,256]{2,1,0:T(8,128)}, u32[]{:S(2)}) copy-start(f32[1,768,256]{2,1,0:T(8,128)} %param.15) | copy-start | bytes 2359300
  14.5 38.7 %copy-start.42 = (f32[1,768,256]{2,1,0:T(8,128)S(1)}, f32[1,768,256]{2,1,0:T(8,128)}, u32[]{:S(2)}) copy-start(f32[1,768,256]{2,1,0:T(8,128)} %param.16) | copy-start | bytes 2359300
  14.5 38.7 %copy-start.43 = (bf16[1,768,256]{2,1,0:T(8,128)(2,1)S(1)}, bf16[1,768,256]{2,1,0:T(8,128)(2,1)}, u32[]{:S(2)}) copy-start(bf16[1,768,256]{2,1,0:T(8,128)(2,1)} %param.17) | copy-start | bytes 1179652
  16.9 34.3 %collective-permute-start = (bf16[256,1536]{1,0:T(8,128)(2,1)S(1)}, bf16[256,1536]{1,0:T(8,128)(2,1)S(1)}, u32[]{:S(2)}, u32[]{:S(2)}) collective-permute-start(bf16[256,1536]{1,0:T(8,128)(2,1)S(1)} %fusion.6), channel_id=1, source_target_pairs={{0,0},{4,4},{8,8},{12,12},{16,20},{20,24},{24,28},{28,16},{32,40},... | collective-permute-start | bytes 2359304 | tf_op jit(solution)/shard_map/ppermute | solution.py:55
  51.2 57.4 %collective-permute-start.1 = (bf16[256,1536]{1,0:T(8,128)(2,1)S(1)}, bf16[256,1536]{1,0:T(8,128)(2,1)S(1)}, u32[]{:S(2)}, u32[]{:S(2)}) collective-permute-start(bf16[256,1536]{1,0:T(8,128)(2,1)S(1)} %collective-permute-done), channel_id=1, source_target_pairs={{0,0},{4,68},{8,136},{12,204},{16,208},{20,20},{24,88},{28,156},{3... | collective-permute-start | bytes 2359304 | tf_op jit(solution)/shard_map/ppermute | solution.py:56
  53.4 55.3 %collective-permute-start.19 = (bf16[768,256]{1,0:T(8,128)(2,1)S(1)}, bf16[768,256]{1,0:T(8,128)(2,1)S(1)}, u32[]{:S(2)}, u32[]{:S(2)}) collective-permute-start(bf16[768,256]{1,0:T(8,128)(2,1)S(1)} %fusion.7), channel_id=1, source_target_pairs={{0,0},{4,4},{8,8},{12,12},{16,20},{20,24},{24,28},{28,16},{32,40},... | collective-permute-start | bytes 1179656 | tf_op jit(solution)/shard_map/ppermute | solution.py:55
  108.7 15.3 %collective-permute-start.2 = (bf16[256,1536]{1,0:T(8,128)(2,1)S(1)}, bf16[256,1536]{1,0:T(8,128)(2,1)S(1)}, u32[]{:S(2)}, u32[]{:S(2)}) collective-permute-start(bf16[256,1536]{1,0:T(8,128)(2,1)S(1)} %collective-permute-done.1.refs_0_), channel_id=1, source_target_pairs={{0,32},{32,4},{4,36},{36,8},{8,40},{40,12},{12,44},{44,0},{1,33},{... | collective-permute-start | bytes 2359304 | tf_op jit(solution)/shard_map/ppermute | solution.py:60
  108.7 12.8 %collective-permute-start.20 = (bf16[768,256]{1,0:T(8,128)(2,1)S(1)}, bf16[768,256]{1,0:T(8,128)(2,1)S(1)}, u32[]{:S(2)}, u32[]{:S(2)}) collective-permute-start(bf16[768,256]{1,0:T(8,128)(2,1)S(1)} %collective-permute-done.19), channel_id=1, source_target_pairs={{0,0},{4,68},{8,136},{12,204},{16,208},{20,20},{24,88},{28,156},{3... | collective-permute-start | bytes 1179656 | tf_op jit(solution)/shard_map/ppermute | solution.py:56
  110.6 27.1 %collective-permute-start.3 = (bf16[256,1536]{1,0:T(8,128)(2,1)S(1)}, bf16[256,1536]{1,0:T(8,128)(2,1)S(1)}, u32[]{:S(2)}, u32[]{:S(2)}) collective-permute-start(bf16[256,1536]{1,0:T(8,128)(2,1)S(1)} %collective-permute-done.1.refs_0_), channel_id=1, source_target_pairs={{0,44},{32,0},{4,32},{36,4},{8,36},{40,8},{12,40},{44,12},{1,45},{... | collective-permute-start | bytes 2359304 | tf_op jit(solution)/shard_map/ppermute | solution.py:64
  121.5 53.6 %copy-start.20 = (bf16[768,256]{1,0:T(8,128)(2,1)}, bf16[768,256]{1,0:T(8,128)(2,1)S(1)}, u32[]{:S(2)}) copy-start(bf16[768,256]{1,0:T(8,128)(2,1)S(1)} %collective-permute-done.20.refs_0_) | copy-start | bytes 1179652
  121.5 12.1 %collective-permute-start.21 = (bf16[768,256]{1,0:T(8,128)(2,1)S(1)}, bf16[768,256]{1,0:T(8,128)(2,1)S(1)}, u32[]{:S(2)}, u32[]{:S(2)}) collective-permute-start(bf16[768,256]{1,0:T(8,128)(2,1)S(1)} %collective-permute-done.20.refs_0_), channel_id=1, source_target_pairs={{0,32},{32,4},{4,36},{36,8},{8,40},{40,12},{12,44},{44,0},{1,33},{... | collective-permute-start | bytes 1179656 | tf_op jit(solution)/shard_map/ppermute | solution.py:60
  124.0 36.2 %collective-permute-start.4 = (bf16[256,1536]{1,0:T(8,128)(2,1)S(1)}, bf16[256,1536]{1,0:T(8,128)(2,1)S(1)}, u32[]{:S(2)}, u32[]{:S(2)}) collective-permute-start(bf16[256,1536]{1,0:T(8,128)(2,1)S(1)} %collective-permute-done.2.refs_1_), channel_id=1, source_target_pairs={{0,32},{32,4},{4,36},{36,8},{8,40},{40,12},{12,44},{44,0},{1,33},{... | collective-permute-start | bytes 2359304 | tf_op jit(solution)/shard_map/ppermute | solution.py:60
  129.2 12.0 %collective-permute-start.22 = (bf16[768,256]{1,0:T(8,128)(2,1)S(1)}, bf16[768,256]{1,0:T(8,128)(2,1)S(1)}, u32[]{:S(2)}, u32[]{:S(2)}) collective-permute-start(bf16[768,256]{1,0:T(8,128)(2,1)S(1)} %collective-permute-done.20.refs_0_), channel_id=1, source_target_pairs={{0,44},{32,0},{4,32},{36,4},{8,36},{40,8},{12,40},{44,12},{1,45},{... | collective-permute-start | bytes 1179656 | tf_op jit(solution)/shard_map/ppermute | solution.py:64
  129.3 14.5 %collective-permute-start.29 = (bf16[768,256]{1,0:T(8,128)(2,1)S(1)}, bf16[768,256]{1,0:T(8,128)(2,1)S(1)}, u32[]{:S(2)}, u32[]{:S(2)}) collective-permute-start(bf16[768,256]{1,0:T(8,128)(2,1)S(1)} %collective-permute-done.20.refs_0_), channel_id=1, source_target_pairs={{0,16},{16,0},{1,17},{17,1},{2,18},{18,2},{3,19},{19,3},{4,20},{20... | collective-permute-start | bytes 1179656 | tf_op jit(solution)/shard_map/ppermute | solution.py:68
  133.5 22.5 %collective-permute-start.23 = (bf16[768,256]{1,0:T(8,128)(2,1)S(1)}, bf16[768,256]{1,0:T(8,128)(2,1)S(1)}, u32[]{:S(2)}, u32[]{:S(2)}) collective-permute-start(bf16[768,256]{1,0:T(8,128)(2,1)S(1)} %collective-permute-done.21.refs_1_), channel_id=1, source_target_pairs={{0,32},{32,4},{4,36},{36,8},{8,40},{40,12},{12,44},{44,0},{1,33},{... | collective-permute-start | bytes 1179656 | tf_op jit(solution)/shard_map/ppermute | solution.py:60
  137.7 32.9 %collective-permute-start.5 = (bf16[256,1536]{1,0:T(8,128)(2,1)S(1)}, bf16[256,1536]{1,0:T(8,128)(2,1)}, u32[]{:S(2)}, u32[]{:S(2)}) collective-permute-start(bf16[256,1536]{1,0:T(8,128)(2,1)S(1)} %collective-permute-done.3.refs_2_), channel_id=1, source_target_pairs={{0,44},{32,0},{4,32},{36,4},{8,36},{40,8},{12,40},{44,12},{1,45},{... | collective-permute-start | bytes 2359304 | tf_op jit(solution)/shard_map/ppermute | solution.py:64
  141.2 23.0 %collective-permute-start.24 = (bf16[768,256]{1,0:T(8,128)(2,1)S(1)}, bf16[768,256]{1,0:T(8,128)(2,1)S(1)}, u32[]{:S(2)}, u32[]{:S(2)}) collective-permute-start(bf16[768,256]{1,0:T(8,128)(2,1)S(1)} %collective-permute-done.22.refs_2_), channel_id=1, source_target_pairs={{0,44},{32,0},{4,32},{36,4},{8,36},{40,8},{12,40},{44,12},{1,45},{... | collective-permute-start | bytes 1179656 | tf_op jit(solution)/shard_map/ppermute | solution.py:64
  144.5 20.5 %collective-permute-start.30 = (bf16[768,256]{1,0:T(8,128)(2,1)S(1)}, bf16[768,256]{1,0:T(8,128)(2,1)S(1)}, u32[]{:S(2)}, u32[]{:S(2)}) collective-permute-start(bf16[768,256]{1,0:T(8,128)(2,1)S(1)} %collective-permute-done.21.refs_1_), channel_id=1, source_target_pairs={{0,16},{16,0},{1,17},{17,1},{2,18},{18,2},{3,19},{19,3},{4,20},{20... | collective-permute-start | bytes 1179656 | tf_op jit(solution)/shard_map/ppermute | solution.py:68
  156.1 13.8 %collective-permute-start.25 = (bf16[768,256]{1,0:T(8,128)(2,1)S(1)}, bf16[768,256]{1,0:T(8,128)(2,1)S(1)}, u32[]{:S(2)}, u32[]{:S(2)}) collective-permute-start(bf16[768,256]{1,0:T(8,128)(2,1)S(1)} %collective-permute-done.23.refs_3_), channel_id=1, source_target_pairs={{0,32},{32,4},{4,36},{36,8},{8,40},{40,12},{12,44},{44,0},{1,33},{... | collective-permute-start | bytes 1179656 | tf_op jit(solution)/shard_map/ppermute | solution.py:60
  160.3 27.9 %collective-permute-start.6 = (bf16[256,1536]{1,0:T(8,128)(2,1)S(1)}, bf16[256,1536]{1,0:T(8,128)(2,1)S(1)}, u32[]{:S(2)}, u32[]{:S(2)}) collective-permute-start(bf16[256,1536]{1,0:T(8,128)(2,1)S(1)} %collective-permute-done.4.refs_3_), channel_id=1, source_target_pairs={{0,32},{32,4},{4,36},{36,8},{8,40},{40,12},{12,44},{44,0},{1,33},{... | collective-permute-start | bytes 2359304 | tf_op jit(solution)/shard_map/ppermute | solution.py:60
  164.2 25.4 %copy-start.30 = (bf16[768,256]{1,0:T(8,128)(2,1)}, bf16[768,256]{1,0:T(8,128)(2,1)S(1)}, u32[]{:S(2)}) copy-start(bf16[768,256]{1,0:T(8,128)(2,1)S(1)} %collective-permute-done.24.refs_4_) | copy-start | bytes 1179652
  164.2 6.5 %collective-permute-start.31 = (bf16[768,256]{1,0:T(8,128)(2,1)S(1)}, bf16[768,256]{1,0:T(8,128)(2,1)S(1)}, u32[]{:S(2)}, u32[]{:S(2)}) collective-permute-start(bf16[768,256]{1,0:T(8,128)(2,1)S(1)} %collective-permute-done.22.refs_2_), channel_id=1, source_target_pairs={{0,16},{16,0},{1,17},{17,1},{2,18},{18,2},{3,19},{19,3},{4,20},{20... | collective-permute-start | bytes 1179656 | tf_op jit(solution)/shard_map/ppermute | solution.py:68
  165.7 13.0 %collective-permute-start.26 = (bf16[768,256]{1,0:T(8,128)(2,1)S(1)}, bf16[768,256]{1,0:T(8,128)(2,1)S(1)}, u32[]{:S(2)}, u32[]{:S(2)}) collective-permute-start(bf16[768,256]{1,0:T(8,128)(2,1)S(1)} %collective-permute-done.24.refs_4_), channel_id=1, source_target_pairs={{0,44},{32,0},{4,32},{36,4},{8,36},{40,8},{12,40},{44,12},{1,45},{... | collective-permute-start | bytes 1179656 | tf_op jit(solution)/shard_map/ppermute | solution.py:64
  169.8 9.8 %collective-permute-start.32 = (bf16[768,256]{1,0:T(8,128)(2,1)S(1)}, bf16[768,256]{1,0:T(8,128)(2,1)S(1)}, u32[]{:S(2)}, u32[]{:S(2)}) collective-permute-start(bf16[768,256]{1,0:T(8,128)(2,1)S(1)} %collective-permute-done.23.refs_3_), channel_id=1, source_target_pairs={{0,16},{16,0},{1,17},{17,1},{2,18},{18,2},{3,19},{19,3},{4,20},{20... | collective-permute-start | bytes 1179656 | tf_op jit(solution)/shard_map/ppermute | solution.py:68
  170.6 24.9 %collective-permute-start.7 = (bf16[256,1536]{1,0:T(8,128)(2,1)}, bf16[256,1536]{1,0:T(8,128)(2,1)}, u32[]{:S(2)}, u32[]{:S(2)}) collective-permute-start(bf16[256,1536]{1,0:T(8,128)(2,1)} %collective-permute-done.5.refs_4_), channel_id=1, source_target_pairs={{0,44},{32,0},{4,32},{36,4},{8,36},{40,8},{12,40},{44,12},{1,45},{... | collective-permute-start | bytes 2359304 | tf_op jit(solution)/shard_map/ppermute | solution.py:64
  171.4 15.8 %collective-permute-start.27 = (bf16[384,256]{1,0:T(8,128)(2,1)S(1)}, bf16[384,256]{1,0:T(8,128)(2,1)S(1)}, u32[]{:S(2)}, u32[]{:S(2)}) collective-permute-start(bf16[384,256]{1,0:T(8,128)(2,1)S(1)} %slice.18), channel_id=1, source_target_pairs={{0,32},{32,4},{4,36},{36,8},{8,40},{40,12},{12,44},{44,0},{1,33},{... | collective-permute-start | bytes 589832 | tf_op jit(solution)/shard_map/ppermute | solution.py:60
  178.7 24.5 %collective-permute-start.10 = (bf16[256,1536]{1,0:T(8,128)(2,1)S(1)}, bf16[256,1536]{1,0:T(8,128)(2,1)S(1)}, u32[]{:S(2)}, u32[]{:S(2)}) collective-permute-start(bf16[256,1536]{1,0:T(8,128)(2,1)S(1)} %collective-permute-done.1.refs_0_), channel_id=1, source_target_pairs={{0,16},{16,0},{1,17},{17,1},{2,18},{18,2},{3,19},{19,3},{4,20},{20... | collective-permute-start | bytes 2359304 | tf_op jit(solution)/shard_map/ppermute | solution.py:68
  180.4 24.2 %collective-permute-start.11 = (bf16[256,1536]{1,0:T(8,128)(2,1)S(1)}, bf16[256,1536]{1,0:T(8,128)(2,1)S(1)}, u32[]{:S(2)}, u32[]{:S(2)}) collective-permute-start(bf16[256,1536]{1,0:T(8,128)(2,1)S(1)} %collective-permute-done.2.refs_1_), channel_id=1, source_target_pairs={{0,16},{16,0},{1,17},{17,1},{2,18},{18,2},{3,19},{19,3},{4,20},{20... | collective-permute-start | bytes 2359304 | tf_op jit(solution)/shard_map/ppermute | solution.py:68
  187.3 18.3 %collective-permute-start.12 = (bf16[256,1536]{1,0:T(8,128)(2,1)S(1)}, bf16[256,1536]{1,0:T(8,128)(2,1)S(1)}, u32[]{:S(2)}, u32[]{:S(2)}) collective-permute-start(bf16[256,1536]{1,0:T(8,128)(2,1)S(1)} %collective-permute-done.3.refs_2_), channel_id=1, source_target_pairs={{0,16},{16,0},{1,17},{17,1},{2,18},{18,2},{3,19},{19,3},{4,20},{20... | collective-permute-start | bytes 2359304 | tf_op jit(solution)/shard_map/ppermute | solution.py:68
  188.1 21.3 %collective-permute-start.13 = (bf16[256,1536]{1,0:T(8,128)(2,1)S(1)}, bf16[256,1536]{1,0:T(8,128)(2,1)S(1)}, u32[]{:S(2)}, u32[]{:S(2)}) collective-permute-start(bf16[256,1536]{1,0:T(8,128)(2,1)S(1)} %collective-permute-done.4.refs_3_), channel_id=1, source_target_pairs={{0,16},{16,0},{1,17},{17,1},{2,18},{18,2},{3,19},{19,3},{4,20},{20... | collective-permute-start | bytes 2359304 | tf_op jit(solution)/shard_map/ppermute | solution.py:68
  195.5 7.7 %collective-permute-start.28 = (bf16[384,256]{1,0:T(8,128)(2,1)S(1)}, bf16[384,256]{1,0:T(8,128)(2,1)S(1)}, u32[]{:S(2)}, u32[]{:S(2)}) collective-permute-start(bf16[384,256]{1,0:T(8,128)(2,1)S(1)} %slice.19), channel_id=1, source_target_pairs={{0,44},{32,0},{4,32},{36,4},{8,36},{40,8},{12,40},{44,12},{1,45},{... | collective-permute-start | bytes 589832 | tf_op jit(solution)/shard_map/ppermute | solution.py:64
  203.2 18.6 %collective-permute-start.14 = (bf16[256,1536]{1,0:T(8,128)(2,1)}, bf16[256,1536]{1,0:T(8,128)(2,1)}, u32[]{:S(2)}, u32[]{:S(2)}) collective-permute-start(bf16[256,1536]{1,0:T(8,128)(2,1)} %collective-permute-done.5.refs_4_), channel_id=1, source_target_pairs={{0,16},{16,0},{1,17},{17,1},{2,18},{18,2},{3,19},{19,3},{4,20},{20... | collective-permute-start | bytes 2359304 | tf_op jit(solution)/shard_map/ppermute | solution.py:68
  204.1 18.2 %collective-permute-start.15 = (bf16[256,1536]{1,0:T(8,128)(2,1)S(1)}, bf16[256,1536]{1,0:T(8,128)(2,1)}, u32[]{:S(2)}, u32[]{:S(2)}) collective-permute-start(bf16[256,1536]{1,0:T(8,128)(2,1)S(1)} %collective-permute-done.6.refs_5_), channel_id=1, source_target_pairs={{0,16},{16,0},{1,17},{17,1},{2,18},{18,2},{3,19},{19,3},{4,20},{20... | collective-permute-start | bytes 2359304 | tf_op jit(solution)/shard_map/ppermute | solution.py:68
  205.5 26.7 %collective-permute-start.16 = (bf16[256,1536]{1,0:T(8,128)(2,1)}, bf16[256,1536]{1,0:T(8,128)(2,1)}, u32[]{:S(2)}, u32[]{:S(2)}) collective-permute-start(bf16[256,1536]{1,0:T(8,128)(2,1)} %collective-permute-done.7.refs_6_), channel_id=1, source_target_pairs={{0,16},{16,0},{1,17},{17,1},{2,18},{18,2},{3,19},{19,3},{4,20},{20... | collective-permute-start | bytes 2359304 | tf_op jit(solution)/shard_map/ppermute | solution.py:68
  206.5 12.0 %collective-permute-start.8 = (bf16[128,1536]{1,0:T(8,128)(2,1)S(1)}, bf16[128,1536]{1,0:T(8,128)(2,1)}, u32[]{:S(2)}, u32[]{:S(2)}) collective-permute-start(bf16[128,1536]{1,0:T(8,128)(2,1)S(1)} %slice.16), channel_id=1, source_target_pairs={{0,32},{32,4},{4,36},{36,8},{8,40},{40,12},{12,44},{44,0},{1,33},{... | collective-permute-start | bytes 1179656 | tf_op jit(solution)/shard_map/ppermute | solution.py:60
  210.3 11.3 %collective-permute-start.9 = (bf16[128,1536]{1,0:T(8,128)(2,1)S(1)}, bf16[128,1536]{1,0:T(8,128)(2,1)}, u32[]{:S(2)}, u32[]{:S(2)}) collective-permute-start(bf16[128,1536]{1,0:T(8,128)(2,1)S(1)} %slice.17), channel_id=1, source_target_pairs={{0,44},{32,0},{4,32},{36,4},{8,36},{40,8},{12,40},{44,12},{1,45},{... | collective-permute-start | bytes 1179656 | tf_op jit(solution)/shard_map/ppermute | solution.py:64
  218.5 13.9 %collective-permute-start.17 = (bf16[128,1536]{1,0:T(8,128)(2,1)}, bf16[128,1536]{1,0:T(8,128)(2,1)}, u32[]{:S(2)}, u32[]{:S(2)}) collective-permute-start(bf16[128,1536]{1,0:T(8,128)(2,1)} %collective-permute-done.8.refs_7_), channel_id=1, source_target_pairs={{0,16},{16,0},{1,17},{17,1},{2,18},{18,2},{3,19},{19,3},{4,20},{20... | collective-permute-start | bytes 1179656 | tf_op jit(solution)/shard_map/ppermute | solution.py:68
  221.7 11.0 %collective-permute-start.18 = (bf16[128,1536]{1,0:T(8,128)(2,1)}, bf16[128,1536]{1,0:T(8,128)(2,1)}, u32[]{:S(2)}, u32[]{:S(2)}) collective-permute-start(bf16[128,1536]{1,0:T(8,128)(2,1)} %collective-permute-done.9.refs_8_), channel_id=1, source_target_pairs={{0,16},{16,0},{1,17},{17,1},{2,18},{18,2},{3,19},{19,3},{4,20},{20... | collective-permute-start | bytes 1179656 | tf_op jit(solution)/shard_map/ppermute | solution.py:68
  221.8 35.5 %collective-permute-start.33 = (bf16[768,256]{1,0:T(8,128)(2,1)}, bf16[768,256]{1,0:T(8,128)(2,1)}, u32[]{:S(2)}, u32[]{:S(2)}) collective-permute-start(bf16[768,256]{1,0:T(8,128)(2,1)} %copy-done.30), channel_id=1, source_target_pairs={{0,16},{16,0},{1,17},{17,1},{2,18},{18,2},{3,19},{19,3},{4,20},{20... | collective-permute-start | bytes 1179656 | tf_op jit(solution)/shard_map/ppermute | solution.py:68
  222.4 34.9 %collective-permute-start.34 = (bf16[768,256]{1,0:T(8,128)(2,1)S(1)}, bf16[768,256]{1,0:T(8,128)(2,1)}, u32[]{:S(2)}, u32[]{:S(2)}) collective-permute-start(bf16[768,256]{1,0:T(8,128)(2,1)S(1)} %collective-permute-done.25.refs_5_), channel_id=1, source_target_pairs={{0,16},{16,0},{1,17},{17,1},{2,18},{18,2},{3,19},{19,3},{4,20},{20... | collective-permute-start | bytes 1179656 | tf_op jit(solution)/shard_map/ppermute | solution.py:68
  232.2 25.1 %collective-permute-start.35 = (bf16[768,256]{1,0:T(8,128)(2,1)}, bf16[768,256]{1,0:T(8,128)(2,1)}, u32[]{:S(2)}, u32[]{:S(2)}) collective-permute-start(bf16[768,256]{1,0:T(8,128)(2,1)} %copy-done.2), channel_id=1, source_target_pairs={{0,16},{16,0},{1,17},{17,1},{2,18},{18,2},{3,19},{19,3},{4,20},{20... | collective-permute-start | bytes 1179656 | tf_op jit(solution)/shard_map/ppermute | solution.py:68
  232.3 24.9 %collective-permute-start.36 = (bf16[384,256]{1,0:T(8,128)(2,1)S(1)}, bf16[384,256]{1,0:T(8,128)(2,1)}, u32[]{:S(2)}, u32[]{:S(2)}) collective-permute-start(bf16[384,256]{1,0:T(8,128)(2,1)S(1)} %collective-permute-done.27.refs_7_), channel_id=1, source_target_pairs={{0,16},{16,0},{1,17},{17,1},{2,18},{18,2},{3,19},{19,3},{4,20},{20... | collective-permute-start | bytes 589832 | tf_op jit(solution)/shard_map/ppermute | solution.py:68
  232.7 24.6 %collective-permute-start.37 = (bf16[384,256]{1,0:T(8,128)(2,1)}, bf16[384,256]{1,0:T(8,128)(2,1)}, u32[]{:S(2)}, u32[]{:S(2)}) collective-permute-start(bf16[384,256]{1,0:T(8,128)(2,1)} %copy-done.38), channel_id=1, source_target_pairs={{0,16},{16,0},{1,17},{17,1},{2,18},{18,2},{3,19},{19,3},{4,20},{20... | collective-permute-start | bytes 589832 | tf_op jit(solution)/shard_map/ppermute | solution.py:68
  241.9 15.4 %copy-start.27 = (bf16[768,256]{1,0:T(8,128)(2,1)S(1)}, bf16[768,256]{1,0:T(8,128)(2,1)}, u32[]{:S(2)}) copy-start(bf16[768,256]{1,0:T(8,128)(2,1)} %copy-done.26) | copy-start | bytes 1179652
  242.0 15.4 %copy-start.29 = (bf16[768,256]{1,0:T(8,128)(2,1)S(1)}, bf16[768,256]{1,0:T(8,128)(2,1)}, u32[]{:S(2)}) copy-start(bf16[768,256]{1,0:T(8,128)(2,1)} %copy-done.28) | copy-start | bytes 1179652
  270.0 32.1 %copy-start.44 = (f32[2,128,2]{1,2,0:T(2,128)S(1)}, f32[2,128,2]{1,2,0:T(2,128)}, u32[]{:S(2)}) copy-start(f32[2,128,2]{1,2,0:T(2,128)} %param.11) | copy-start | bytes 6148
  270.0 143.7 %all-to-all-start.1 = ((bf16[16,48,4096]{2,1,0:T(8,128)(2,1)}), bf16[16,48,4096]{2,1,0:T(8,128)(2,1)}, u32[]{:S(2)}, u32[]{:S(2)}) async-start(bf16[16,48,4096]{2,1,0:T(8,128)(2,1)} %bitcast.45), calls=%async_computation.1 | async-start | bytes 12582912 | tf_op jit(solution)/shard_map/all_to_all | solution.py:239
  (37 other events, 189.0 us)

commit v2 on v1

v2 whole, which is shorter than its diff:
```python
import jax
import jax.numpy as jnp
import numpy as np
from jax import lax
from jax.experimental import pallas as pl
from jax.experimental.pallas import tpu as pltpu
from jax.sharding import Mesh, PartitionSpec as P

AXES = ("x", "zl", "core", "zh", "y")
NX, NZL, NC, NZH, NY = 4, 2, 2, 4, 4
MIB = 1 << 20


def updated(master, moment, grad):
    return (master - 0.5 * (0.8 * moment + 0.2 * grad.astype(jnp.float32))).astype(jnp.bfloat16)


def flat(x, zl, c, zh):
    return ((x * NZL + zl) * NC + c) * NZH + zh


def places():
    return [
        (x, zl, c, zh)
        for x in range(NX)
        for zl in range(NZL)
        for c in range(NC)
        for zh in range(NZH)
    ]


NZ = NZL * NZH


def host_of(x, zl, c, zh):
    hops = x if c == 0 else NX - 1 - x
    z = (NZL * zh + 1 + hops) % NZ if zl else (NZL * zh - hops) % NZ
    return zh, z % NZL, c, z // NZL


SPREAD = [(flat(*place), flat(*host_of(*place))) for place in places()]
SHARD_AT = {
    host_of(x, zl, c, zh): (x * NZL + zl) * NC + c for x, zl, c, zh in places()
}


def ring_index(z, c):
    return (z % NZL * NC + c) * NZH + z // NZL


def ring_step(z, c):
    return (z + 1 - 2 * c) % NZ


PASS_ON = [(ring_index(z, c), ring_index(ring_step(z, c), c)) for z in range(NZ) for c in range(NC)]


def spread(block):
    return lax.ppermute(block, ("x", "zl", "core", "zh"), SPREAD)


def pass_on(block):
    return lax.ppermute(block, ("zl", "core", "zh"), PASS_ON)


def after(value, *others):
    return lax.optimization_barrier((value,) + others)[0]


def other_core(block):
    return lax.ppermute(block, "core", [(0, 1), (1, 0)])


def ring(block):
    mine = [block]
    for _ in range(NZ - 1):
        mine.append(pass_on(mine[-1]))
    return mine + [other_core(piece) for piece in mine]


def shards_at(x, zl, c, zh):
    z = NZL * zh + zl
    entries = []
    for core in (c, 1 - c):
        for step in range(NZ):
            at = (z - step * (1 - 2 * core)) % NZ
            entries.append(SHARD_AT[x, at % NZL, core, at // NZL])
    return entries


SHARDS = np.array([shards_at(*place) for place in places()], np.int32)


def shard_table():
    x, zl, c, zh = (lax.axis_index(name) for name in ("x", "zl", "core", "zh"))
    return lax.dynamic_index_in_dim(jnp.asarray(SHARDS), flat(x, zl, c, zh), keepdims=False)


def hidden_kernel(table, x_hbm, *refs):
    pieces, (h_ref, x_buf, w_buf, sems, x_sem) = refs[:16], refs[16:]
    copies = [
        pltpu.make_async_copy(piece, w_buf.at[table[n]], sems.at[n])
        for n, piece in enumerate(pieces)
    ]
    x_copy = pltpu.make_async_copy(x_hbm, x_buf, x_sem)
    x_copy.start()
    for copy in copies:
        copy.start()
    x_copy.wait()
    for copy in copies:
        copy.wait()
    shards, depth, wide = w_buf.shape
    units = wide // 2
    tile = 256

    def columns(n, carry):
        first = pl.multiple_of(n * tile, tile)
        w_gate = w_buf[:, :, pl.ds(first, tile)].reshape(shards * depth, tile)
        w_up = w_buf[:, :, pl.ds(units + first, tile)].reshape(shards * depth, tile)
        gate = jnp.dot(x_buf[...], w_gate, preferred_element_type=jnp.float32)
        upper = jnp.dot(x_buf[...], w_up, preferred_element_type=jnp.float32)
        h_ref[:, pl.ds(first, tile)] = (gate / (1.0 + jnp.exp(-gate)) * upper).astype(h_ref.dtype)
        return carry

    lax.fori_loop(0, units // tile, columns, 0)


def out_kernel(table, h_ref, *refs):
    pieces, (o_ref, w_buf, sems) = refs[:16], refs[16:]
    wide = pieces[0].shape[1]
    copies = [
        pltpu.make_async_copy(
            piece, w_buf.at[:, pl.ds(pl.multiple_of(table[n] * wide, wide), wide)], sems.at[n]
        )
        for n, piece in enumerate(pieces)
    ]
    for copy in copies:
        copy.start()
    for copy in copies:
        copy.wait()
    tile = 1024

    def columns(n, carry):
        at = pl.ds(pl.multiple_of(n * tile, tile), tile)
        o_ref[:, at] = jnp.dot(
            h_ref[...], w_buf[:, at], preferred_element_type=jnp.float32
        ).astype(o_ref.dtype)
        return carry

    lax.fori_loop(0, w_buf.shape[1] // tile, columns, 0)


ANY = pl.BlockSpec(memory_space=pl.ANY)
VMEM = pl.BlockSpec(memory_space=pltpu.VMEM)
SMEM = pl.BlockSpec(memory_space=pltpu.SMEM)


def hidden_of(table, x, pieces):
    rows, wide = x.shape
    depth, cols = pieces[0].shape
    return pl.pallas_call(
        hidden_kernel,
        out_shape=jax.ShapeDtypeStruct((rows, cols // 2), jnp.bfloat16),
        in_specs=[SMEM, ANY] + [ANY] * len(pieces),
        out_specs=VMEM,
        scratch_shapes=[
            pltpu.VMEM((rows, wide), jnp.bfloat16),
            pltpu.VMEM((16, depth, cols), jnp.bfloat16),
            pltpu.SemaphoreType.DMA((len(pieces),)),
            pltpu.SemaphoreType.DMA,
        ],
        compiler_params=pltpu.CompilerParams(vmem_limit_bytes=22 * MIB),
        cost_estimate=pl.CostEstimate(
            flops=2 * rows * wide * cols, bytes_accessed=19 * MIB, transcendentals=rows * cols // 2
        ),
        name="hidden",
    )(table, x, *pieces)


def outputs_of(table, h, pieces):
    rows, units = h.shape
    _, cols = pieces[0].shape
    return pl.pallas_call(
        out_kernel,
        out_shape=jax.ShapeDtypeStruct((rows, 16 * cols), jnp.bfloat16),
        in_specs=[SMEM, VMEM] + [ANY] * len(pieces),
        out_specs=VMEM,
        scratch_shapes=[
            pltpu.VMEM((units, 16 * cols), jnp.bfloat16),
            pltpu.SemaphoreType.DMA((len(pieces),)),
        ],
        compiler_params=pltpu.CompilerParams(vmem_limit_bytes=16 * MIB),
        cost_estimate=pl.CostEstimate(
            flops=2 * rows * units * cols * 16, bytes_accessed=13 * MIB, transcendentals=0
        ),
        name="expert_out",
    )(table, h, *pieces)


def per_device(
    tokens,
    expert_ids,
    route_gain,
    gate_up_master,
    gate_up_moment,
    gate_up_grad,
    down_master,
    down_moment,
    down_grad,
):
    steps, row_dev, top_k = expert_ids.shape
    width = tokens.shape[2]
    experts = NX * NY
    capacity = 3 * row_dev * top_k // (2 * experts)
    gate_up_weight = updated(gate_up_master[0], gate_up_moment[0], gate_up_grad[0])
    down_weight = updated(down_master[0], down_moment[0], down_grad[0])
    gate_up_block = spread(gate_up_weight)
    down_block = spread(down_weight)
    gate_up_pieces = ring(gate_up_block)
    down_pieces = ring(down_block)
    table = shard_table()

    names = expert_ids[..., None] == jnp.arange(experts, dtype=jnp.int32)
    named = jnp.any(names, axis=2).astype(jnp.bfloat16)
    order = jnp.arange(row_dev)
    before = (order[:, None] > order[None, :]).astype(jnp.bfloat16)
    earlier = jnp.einsum("rq,sqe->sre", before, named, preferred_element_type=jnp.float32)
    slot_index = jnp.sum(jnp.where(names, earlier[:, :, None, :], 0.0), axis=3).astype(jnp.int32)
    target = expert_ids * capacity + slot_index
    slots = jnp.arange(experts * capacity, dtype=jnp.int32)
    hits = target[:, :, None, :] == slots[None, None, :, None]
    dispatch_table = jnp.any(hits, axis=3).astype(jnp.bfloat16)
    share = (route_gain / jnp.sum(route_gain, axis=2, keepdims=True)).astype(jnp.bfloat16)
    combine_table = jnp.sum(
        jnp.where(hits, share[:, :, None, :].astype(jnp.float32), 0.0), axis=3
    ).astype(jnp.bfloat16)

    gate = (gate_up_block, down_block)
    mixed = []
    received = []
    for s in range(steps):
        outgoing = jnp.einsum(
            "rp,rd->pd", dispatch_table[s], tokens[s], preferred_element_type=jnp.float32
        ).astype(jnp.bfloat16)
        arrived = lax.all_to_all(
            after(outgoing, *gate), ("x", "y"), split_axis=0, concat_axis=0, tiled=True
        )
        received.append(arrived)
        gate = (arrived, gate_up_pieces[3])
    hiddens = [hidden_of(table, block, gate_up_pieces) for block in received]
    for s in range(steps):
        expert_out = outputs_of(table, hiddens[s], down_pieces)
        returned = lax.all_to_all(expert_out, ("x", "y"), split_axis=0, concat_axis=0, tiled=True)
        mixed.append(
            jnp.dot(combine_table[s], returned, preferred_element_type=jnp.float32).astype(
                jnp.bfloat16
            )
        )
    return jnp.stack(mixed)


def solution(mesh):
    grid = Mesh(mesh.devices.reshape(NX, NZL, NC, NZH, NY), AXES)
    engine, expert = ("x", "zl", "core"), ("zh", "y")
    rows = P(None, AXES, None)
    return jax.shard_map(
        per_device,
        mesh=grid,
        in_specs=(
            rows,
            rows,
            rows,
            P(expert, engine, None),
            P(expert, engine, None),
            P(expert, engine, None),
            P(expert, None, engine),
            P(expert, None, engine),
            P(expert, None, engine),
        ),
        out_specs=rows,
        check_vma=False,
    )
```

time: 425 us -> 296 us (0.70)
  the two profiles are of different devices: /device:TPU:92 before, /device:TPU:8 now
where the time goes in v2:
time: 296 us; the launch traced here: 295 us
  waiting for transfers between devices  143 us (48%)
  starting transfers between devices  79.8 us (27%)
  Pallas kernels  36.1 us (12%)
  local copies, waits for them, and re-layouts  20 us (7%)
  matrix products  11 us (4%)
  other arithmetic  4.77 us (2%)
    ppermute x14, waiting for transfers between devices, pass_on(): return lax.ppermute(block, ('zl', 'core', 'zh'), PASS_ON)  85.7 us
    all_to_all x2, waiting for transfers between devices, per_device(): lax.all_to_all(expert_out, ('x', 'y'), split_axis=0, concat_axis=0, tiled...  55.5 us
    all_to_all x2, starting transfers between devices, per_device(): lax.all_to_all(after(outgoing, *gate), ('x', 'y'), split_axis=0, concat_a...  47.7 us
    pallas_call x2, Pallas kernels, hidden_of(): pl.pallas_call(hidden_kernel, out_shape=jax.ShapeDtypeStruct((rows, cols...  21 us
    all_to_all x2, starting transfers between devices, per_device(): lax.all_to_all(expert_out, ('x', 'y'), split_axis=0, concat_axis=0, tiled...  19.8 us
    unnamed x94, local copies, waits for them, and re-layouts  19.3 us
    pallas_call x2, Pallas kernels, outputs_of(): pl.pallas_call(out_kernel, out_shape=jax.ShapeDtypeStruct((rows, 16 * col...  15.1 us
    ppermute x14, starting transfers between devices, pass_on(): return lax.ppermute(block, ('zl', 'core', 'zh'), PASS_ON)  7.06 us
  transfers between devices with their start and end apart: 36, of which 12 were waited for; matrix products, arithmetic and copies ran while one was open for 4% of the time, Pallas kernels for 10%

profile of v2, /device:TPU:8, one launch (start us, length us, event | category | flops | bytes accessed | tf_op | source)
XLA Modules:
  0.0 295.2 jit_solution(7105846637989440598)
XLA Ops:
  0.0 2.7 fusion.10
  2.7 1.7 collective-permute-start
  5.5 2.0 collective-permute-start.2
  7.7 2.7 convolution_convert_fusion.1
  10.4 40.5 %all-to-all-start = ((bf16[16,24,4096]{2,1,0:T(8,128)(2,1)}), bf16[16,24,4096]{2,1,0:T(8,128)(2,1)S(1)}, u32[]{:S(2)}, u32[]{:S(2)}) async-start(bf16[16,24,4096]{2,1,0:T(8,128)(2,1)} %bitcast.47), calls=%async_computation | async-start | bytes 6291456 | tf_op jit(solution)/shard_map/all_to_all | solution.py:245
  50.9 13.4 %collective-permute-done.3.refs_2_ = bf16[256,1536]{1,0:T(8,128)(2,1)S(1)} collective-permute-done((bf16[256,1536]{1,0:T(8,128)(2,1)}, bf16[256,1536]{1,0:T(8,128)(2,1)S(1)}, u32[]{:S(2)}, u32[]{:S(2)}) %collective-permute-start.3) | collective-permute-done | bytes 786464 | tf_op jit(solution)/shard_map/ppermute | solution.py:63
  64.3 13.2 %collective-permute-done.4.refs_3_ = bf16[256,1536]{1,0:T(8,128)(2,1)S(1)} collective-permute-done((bf16[256,1536]{1,0:T(8,128)(2,1)S(1)}, bf16[256,1536]{1,0:T(8,128)(2,1)S(1)}, u32[]{:S(2)}, u32[]{:S(2)}) %collective-permute-start.4) | collective-permute-done | bytes 786464 | tf_op jit(solution)/shard_map/ppermute | solution.py:63
  77.5 17.5 %collective-permute-done.17.refs_1_ = bf16[768,256]{1,0:T(8,128)(2,1)} collective-permute-done((bf16[768,256]{1,0:T(8,128)(2,1)S(1)}, bf16[768,256]{1,0:T(8,128)(2,1)}, u32[]{:S(2)}, u32[]{:S(2)}) %collective-permute-start.17) | collective-permute-done | bytes 393248 | tf_op jit(solution)/shard_map/ppermute | solution.py:63
  95.2 3.9 %convolution_convert_fusion = bf16[384,4096]{1,0:T(8,128)(2,1)} fusion(bf16[2,128,4096]{2,1,0:T(8,128)(2,1)} %param.10, pred[2,128,384]{2,1,0:T(8,128)(4,1)} %copy-done.43), kind=kOutput, calls=%fused_computation.1 | convolution fusion | flops 404226048 | bytes 4243456 | tf_op jit(solution)/shard_map/rp,rd->pd/dot_general | solution.py:242
  99.1 7.2 %all-to-all-start.2 = ((bf16[16,24,4096]{2,1,0:T(8,128)(2,1)}), bf16[16,24,4096]{2,1,0:T(8,128)(2,1)}, u32[]{:S(2)}, u32[]{:S(2)}) async-start(bf16[16,24,4096]{2,1,0:T(8,128)(2,1)} %bitcast.46), calls=%async_computation.2 | async-start | bytes 6291456 | tf_op jit(solution)/shard_map/all_to_all | solution.py:245
  106.3 1.2 collective-permute-start.19
  107.5 9.4 %collective-permute-done.19.refs_3_ = bf16[768,256]{1,0:T(8,128)(2,1)S(1)} collective-permute-done((bf16[768,256]{1,0:T(8,128)(2,1)}, bf16[768,256]{1,0:T(8,128)(2,1)S(1)}, u32[]{:S(2)}, u32[]{:S(2)}) %collective-permute-start.19) | collective-permute-done | bytes 393248 | tf_op jit(solution)/shard_map/ppermute | solution.py:63
  117.0 2.4 collective-permute-start.7
  119.8 6.0 %collective-permute-done.20.refs_4_ = bf16[768,256]{1,0:T(8,128)(2,1)S(1)} collective-permute-done((bf16[768,256]{1,0:T(8,128)(2,1)S(1)}, bf16[768,256]{1,0:T(8,128)(2,1)S(1)}, u32[]{:S(2)}, u32[]{:S(2)}) %collective-permute-start.20) | collective-permute-done | bytes 393248 | tf_op jit(solution)/shard_map/ppermute | solution.py:63
  125.9 0.8 copy-done.6
  126.8 0.8 copy-done.9
  128.0 10.5 %collective-permute-done.21.refs_5_ = bf16[768,256]{1,0:T(8,128)(2,1)S(1)} collective-permute-done((bf16[768,256]{1,0:T(8,128)(2,1)S(1)}, bf16[768,256]{1,0:T(8,128)(2,1)S(1)}, u32[]{:S(2)}, u32[]{:S(2)}) %collective-permute-start.21) | collective-permute-done | bytes 393248 | tf_op jit(solution)/shard_map/ppermute | solution.py:63
  139.3 1.2 collective-permute-start.8
  140.5 0.9 copy-done.30
  141.4 6.9 %collective-permute-done.22.refs_6_ = bf16[768,256]{1,0:T(8,128)(2,1)S(1)} collective-permute-done((bf16[768,256]{1,0:T(8,128)(2,1)S(1)}, bf16[768,256]{1,0:T(8,128)(2,1)S(1)}, u32[]{:S(2)}, u32[]{:S(2)}) %collective-permute-start.22) | collective-permute-done | bytes 393248 | tf_op jit(solution)/shard_map/ppermute | solution.py:63
  148.3 0.8 copy-done.15
  149.0 0.8 copy-done.18
  149.8 0.9 copy-done.33
  151.2 0.9 copy-done.36
  152.1 8.8 %collective-permute-done.23.refs_7_ = bf16[768,256]{1,0:T(8,128)(2,1)S(1)} collective-permute-done((bf16[768,256]{1,0:T(8,128)(2,1)S(1)}, bf16[768,256]{1,0:T(8,128)(2,1)S(1)}, u32[]{:S(2)}, u32[]{:S(2)}) %collective-permute-start.23) | collective-permute-done | bytes 393248 | tf_op jit(solution)/shard_map/ppermute | solution.py:63
  160.9 0.8 copy-done.21
  163.5 0.8 collective-permute-done.15.refs_14_
  164.5 1.0 collective-permute-done.16.refs_15_
  165.6 1.1 copy-done.25
  166.7 1.1 copy-done.28
  167.9 1.1 copy-done.31
  169.0 1.1 copy-done.34
  170.1 1.1 copy-done.37
  171.3 10.9 %hidden.3.h_ref = bf16[384,768]{1,0:T(8,128)(2,1)S(1)} custom-call(s32[16]{0:T(128)S(1)} %dynamic-slice_bitcast_fusion.table, bf16[384,4096]{1,0:T(8,128)(2,1)} %bitcast.17.x_hbm, bf16[256,1536]{1,0:T(8,128)(2,1)} %collective-permute-done.refs_0_, bf16[256,1536]{1,0:T(8,128)(2,1)} %collective-permute-done.2.refs_1_, bf16[256,1536]{1,0:T(8,128)(2,1)S(1)} %copy-done.25, ...), custom_call_target="tpu_custom_call" | custom-call | flops 4831838208 | bytes 19922944 | tf_op jit(solution)/shard_map/hidden/pallas_call | solution.py:161
  182.4 7.5 %expert_out.3 = bf16[384,4096]{1,0:T(8,128)(2,1)} custom-call(s32[16]{0:T(128)S(1)} %dynamic-slice_bitcast_fusion.table, bf16[384,768]{1,0:T(8,128)(2,1)S(1)} %hidden.3.h_ref, bf16[768,256]{1,0:T(8,128)(2,1)S(1)} %collective-permute-done.1.refs_0_, bf16[768,256]{1,0:T(8,128)(2,1)} %collective-permute-done.17.refs_1_, ...), custom_call_target="tpu_custom_call" | custom-call | flops 2415919104 | bytes 13631488 | tf_op jit(solution)/shard_map/expert_out/pallas_call | solution.py:183
  189.9 7.3 %all-to-all-start.3 = ((bf16[16,24,4096]{2,1,0:T(8,128)(2,1)}), bf16[16,24,4096]{2,1,0:T(8,128)(2,1)}, u32[]{:S(2)}, u32[]{:S(2)}) async-start(bf16[16,24,4096]{2,1,0:T(8,128)(2,1)} %bitcast.18), calls=%async_computation.3 | async-start | bytes 6291456 | tf_op jit(solution)/shard_map/all_to_all | solution.py:253
  197.2 1.1 copy-done.26
  198.3 1.1 copy-done.29
  199.4 1.1 copy-done.32
  200.6 1.1 copy-done.35
  201.7 1.1 copy-done.38
  202.9 10.1 %hidden.2.h_ref = bf16[384,768]{1,0:T(8,128)(2,1)S(1)} custom-call(s32[16]{0:T(128)S(1)} %dynamic-slice_bitcast_fusion.table, bf16[384,4096]{1,0:T(8,128)(2,1)S(1)} %bitcast.45, bf16[256,1536]{1,0:T(8,128)(2,1)} %collective-permute-done.refs_0_, bf16[256,1536]{1,0:T(8,128)(2,1)} %collective-permute-done.2.refs_1_, bf16[256,1536]{1,0:T(8,128)(2,1)S(1)} %copy-done.26, ...), custom_call_target="tpu_custom_call" | custom-call | flops 4831838208 | bytes 19922944 | tf_op jit(solution)/shard_map/hidden/pallas_call | solution.py:161
  213.0 7.6 %expert_out.2 = bf16[384,4096]{1,0:T(8,128)(2,1)} custom-call(s32[16]{0:T(128)S(1)} %dynamic-slice_bitcast_fusion.table, bf16[384,768]{1,0:T(8,128)(2,1)S(1)} %hidden.2.h_ref, bf16[768,256]{1,0:T(8,128)(2,1)S(1)} %collective-permute-done.1.refs_0_, bf16[768,256]{1,0:T(8,128)(2,1)} %collective-permute-done.17.refs_1_, ...), custom_call_target="tpu_custom_call" | custom-call | flops 2415919104 | bytes 13631488 | tf_op jit(solution)/shard_map/expert_out/pallas_call | solution.py:183
  220.6 18.1 %all-to-all-done.3 = bf16[16,24,4096]{2,1,0:T(8,128)(2,1)} async-done(((bf16[16,24,4096]{2,1,0:T(8,128)(2,1)}), bf16[16,24,4096]{2,1,0:T(8,128)(2,1)}, u32[]{:S(2)}, u32[]{:S(2)}) %all-to-all-start.3) | async-done | bytes 3145760 | tf_op jit(solution)/shard_map/all_to_all | solution.py:253
  238.7 12.5 %all-to-all-start.1 = ((bf16[16,24,4096]{2,1,0:T(8,128)(2,1)}), bf16[16,24,4096]{2,1,0:T(8,128)(2,1)S(1)}, u32[]{:S(2)}, u32[]{:S(2)}) async-start(bf16[16,24,4096]{2,1,0:T(8,128)(2,1)} %bitcast.10), calls=%async_computation.1 | async-start | bytes 6291456 | tf_op jit(solution)/shard_map/all_to_all | solution.py:253
  251.5 3.6 %fusion.2 = bf16[1,128,4096]{2,1,0:T(8,128)(2,1)} fusion(bf16[384,4096]{1,0:T(8,128)(2,1)} %bitcast.19, bf16[2,128,384]{2,1,0:T(8,128)(2,1)S(1)} %select_reduce_fusion), kind=kOutput, calls=%fused_computation.6 | convolution fusion | flops 403177472 | bytes 4292608 | tf_op jit(solution)/shard_map/dot_general | solution.py:255
  255.1 37.4 %all-to-all-done.1 = bf16[16,24,4096]{2,1,0:T(8,128)(2,1)S(1)} async-done(((bf16[16,24,4096]{2,1,0:T(8,128)(2,1)}), bf16[16,24,4096]{2,1,0:T(8,128)(2,1)S(1)}, u32[]{:S(2)}, u32[]{:S(2)}) %all-to-all-start.1) | async-done | bytes 3145760 | tf_op jit(solution)/shard_map/all_to_all | solution.py:253
  293.7 1.5 pad_maximum_fusion
  (137 shorter events, 7.5 us)
Async XLA Ops:
  2.7 2.8 collective-permute-start
  4.6 5.8 %collective-permute-start.1 = (bf16[768,256]{1,0:T(8,128)(2,1)S(1)}, bf16[768,256]{1,0:T(8,128)(2,1)S(1)}, u32[]{:S(2)}, u32[]{:S(2)}) collective-permute-start(bf16[768,256]{1,0:T(8,128)(2,1)S(1)} %fusion.12), channel_id=1, source_target_pairs={{0,0},{4,68},{8,136},{12,204},{16,56},{20,124},{24,176},{28,244},{... | collective-permute-start | bytes 1179656 | tf_op jit(solution)/shard_map/ppermute | solution.py:59
  5.5 45.3 %collective-permute-start.2 = (bf16[256,1536]{1,0:T(8,128)(2,1)}, bf16[256,1536]{1,0:T(8,128)(2,1)}, u32[]{:S(2)}, u32[]{:S(2)}) collective-permute-start(bf16[256,1536]{1,0:T(8,128)(2,1)} %collective-permute-done.refs_0_), channel_id=1, source_target_pairs={{0,32},{16,60},{32,4},{48,16},{4,36},{20,48},{36,8},{52,20},{8,40}... | collective-permute-start | bytes 2359304 | tf_op jit(solution)/shard_map/ppermute | solution.py:63
  10.4 88.7 %all-to-all-start = ((bf16[16,24,4096]{2,1,0:T(8,128)(2,1)}), bf16[16,24,4096]{2,1,0:T(8,128)(2,1)S(1)}, u32[]{:S(2)}, u32[]{:S(2)}) async-start(bf16[16,24,4096]{2,1,0:T(8,128)(2,1)} %bitcast.47), calls=%async_computation | async-start | bytes 6291456 | tf_op jit(solution)/shard_map/all_to_all | solution.py:245
  50.8 13.5 %collective-permute-start.3 = (bf16[256,1536]{1,0:T(8,128)(2,1)}, bf16[256,1536]{1,0:T(8,128)(2,1)S(1)}, u32[]{:S(2)}, u32[]{:S(2)}) collective-permute-start(bf16[256,1536]{1,0:T(8,128)(2,1)} %collective-permute-done.2.refs_1_), channel_id=1, source_target_pairs={{0,32},{16,60},{32,4},{48,16},{4,36},{20,48},{36,8},{52,20},{8,40}... | collective-permute-start | bytes 2359304 | tf_op jit(solution)/shard_map/ppermute | solution.py:63
  64.3 30.7 %copy-start.24 = (bf16[256,1536]{1,0:T(8,128)(2,1)}, bf16[256,1536]{1,0:T(8,128)(2,1)S(1)}, u32[]{:S(2)}) copy-start(bf16[256,1536]{1,0:T(8,128)(2,1)S(1)} %collective-permute-done.3.refs_2_) | copy-start | bytes 2359300
  64.3 13.2 %collective-permute-start.4 = (bf16[256,1536]{1,0:T(8,128)(2,1)S(1)}, bf16[256,1536]{1,0:T(8,128)(2,1)S(1)}, u32[]{:S(2)}, u32[]{:S(2)}) collective-permute-start(bf16[256,1536]{1,0:T(8,128)(2,1)S(1)} %collective-permute-done.3.refs_2_), channel_id=1, source_target_pairs={{0,32},{16,60},{32,4},{48,16},{4,36},{20,48},{36,8},{52,20},{8,40}... | collective-permute-start | bytes 2359304 | tf_op jit(solution)/shard_map/ppermute | solution.py:63
  77.5 17.5 %copy-start.27 = (bf16[256,1536]{1,0:T(8,128)(2,1)}, bf16[256,1536]{1,0:T(8,128)(2,1)S(1)}, u32[]{:S(2)}) copy-start(bf16[256,1536]{1,0:T(8,128)(2,1)S(1)} %collective-permute-done.4.refs_3_) | copy-start | bytes 2359300
  77.5 17.5 %collective-permute-start.5 = (bf16[256,1536]{1,0:T(8,128)(2,1)S(1)}, bf16[256,1536]{1,0:T(8,128)(2,1)}, u32[]{:S(2)}, u32[]{:S(2)}) collective-permute-start(bf16[256,1536]{1,0:T(8,128)(2,1)S(1)} %collective-permute-done.4.refs_3_), channel_id=1, source_target_pairs={{0,32},{16,60},{32,4},{48,16},{4,36},{20,48},{36,8},{52,20},{8,40}... | collective-permute-start | bytes 2359304 | tf_op jit(solution)/shard_map/ppermute | solution.py:63
  77.5 17.5 %collective-permute-start.17 = (bf16[768,256]{1,0:T(8,128)(2,1)S(1)}, bf16[768,256]{1,0:T(8,128)(2,1)}, u32[]{:S(2)}, u32[]{:S(2)}) collective-permute-start(bf16[768,256]{1,0:T(8,128)(2,1)S(1)} %collective-permute-done.1.refs_0_), channel_id=1, source_target_pairs={{0,32},{16,60},{32,4},{48,16},{4,36},{20,48},{36,8},{52,20},{8,40}... | collective-permute-start | bytes 1179656 | tf_op jit(solution)/shard_map/ppermute | solution.py:63
  95.1 11.2 %collective-permute-start.18 = (bf16[768,256]{1,0:T(8,128)(2,1)}, bf16[768,256]{1,0:T(8,128)(2,1)}, u32[]{:S(2)}, u32[]{:S(2)}) collective-permute-start(bf16[768,256]{1,0:T(8,128)(2,1)} %collective-permute-done.17.refs_1_), channel_id=1, source_target_pairs={{0,32},{16,60},{32,4},{48,16},{4,36},{20,48},{36,8},{52,20},{8,40}... | collective-permute-start | bytes 1179656 | tf_op jit(solution)/shard_map/ppermute | solution.py:63
  95.1 21.9 %collective-permute-start.6 = (bf16[256,1536]{1,0:T(8,128)(2,1)}, bf16[256,1536]{1,0:T(8,128)(2,1)}, u32[]{:S(2)}, u32[]{:S(2)}) collective-permute-start(bf16[256,1536]{1,0:T(8,128)(2,1)} %collective-permute-done.5.refs_4_), channel_id=1, source_target_pairs={{0,32},{16,60},{32,4},{48,16},{4,36},{20,48},{36,8},{52,20},{8,40}... | collective-permute-start | bytes 2359304 | tf_op jit(solution)/shard_map/ppermute | solution.py:63
  99.1 66.5 %all-to-all-start.2 = ((bf16[16,24,4096]{2,1,0:T(8,128)(2,1)}), bf16[16,24,4096]{2,1,0:T(8,128)(2,1)}, u32[]{:S(2)}, u32[]{:S(2)}) async-start(bf16[16,24,4096]{2,1,0:T(8,128)(2,1)} %bitcast.46), calls=%async_computation.2 | async-start | bytes 6291456 | tf_op jit(solution)/shard_map/all_to_all | solution.py:245
  106.3 10.6 %collective-permute-start.19 = (bf16[768,256]{1,0:T(8,128)(2,1)}, bf16[768,256]{1,0:T(8,128)(2,1)S(1)}, u32[]{:S(2)}, u32[]{:S(2)}) collective-permute-start(bf16[768,256]{1,0:T(8,128)(2,1)} %collective-permute-done.18.refs_2_), channel_id=1, source_target_pairs={{0,32},{16,60},{32,4},{48,16},{4,36},{20,48},{36,8},{52,20},{8,40}... | collective-permute-start | bytes 1179656 | tf_op jit(solution)/shard_map/ppermute | solution.py:63
  116.9 9.0 %collective-permute-start.20 = (bf16[768,256]{1,0:T(8,128)(2,1)S(1)}, bf16[768,256]{1,0:T(8,128)(2,1)S(1)}, u32[]{:S(2)}, u32[]{:S(2)}) collective-permute-start(bf16[768,256]{1,0:T(8,128)(2,1)S(1)} %collective-permute-done.19.refs_3_), channel_id=1, source_target_pairs={{0,32},{16,60},{32,4},{48,16},{4,36},{20,48},{36,8},{52,20},{8,40}... | collective-permute-start | bytes 1179656 | tf_op jit(solution)/shard_map/ppermute | solution.py:63
  117.0 22.3 %collective-permute-start.7 = (bf16[256,1536]{1,0:T(8,128)(2,1)}, bf16[256,1536]{1,0:T(8,128)(2,1)}, u32[]{:S(2)}, u32[]{:S(2)}) collective-permute-start(bf16[256,1536]{1,0:T(8,128)(2,1)} %collective-permute-done.6.refs_5_), channel_id=1, source_target_pairs={{0,32},{16,60},{32,4},{48,16},{4,36},{20,48},{36,8},{52,20},{8,40}... | collective-permute-start | bytes 2359304 | tf_op jit(solution)/shard_map/ppermute | solution.py:63
  119.3 21.2 %collective-permute-start.9 = (bf16[256,1536]{1,0:T(8,128)(2,1)}, bf16[256,1536]{1,0:T(8,128)(2,1)S(1)}, u32[]{:S(2)}, u32[]{:S(2)}) collective-permute-start(bf16[256,1536]{1,0:T(8,128)(2,1)} %collective-permute-done.refs_0_), channel_id=1, source_target_pairs={{0,16},{16,0},{1,17},{17,1},{2,18},{18,2},{3,19},{19,3},{4,20},{20... | collective-permute-start | bytes 2359304 | tf_op jit(solution)/shard_map/ppermute | solution.py:71
  119.3 6.6 %collective-permute-start.24 = (bf16[768,256]{1,0:T(8,128)(2,1)S(1)}, bf16[768,256]{1,0:T(8,128)(2,1)S(1)}, u32[]{:S(2)}, u32[]{:S(2)}) collective-permute-start(bf16[768,256]{1,0:T(8,128)(2,1)S(1)} %collective-permute-done.1.refs_0_), channel_id=1, source_target_pairs={{0,16},{16,0},{1,17},{17,1},{2,18},{18,2},{3,19},{19,3},{4,20},{20... | collective-permute-start | bytes 1179656 | tf_op jit(solution)/shard_map/ppermute | solution.py:71
  119.8 6.9 %collective-permute-start.25 = (bf16[768,256]{1,0:T(8,128)(2,1)}, bf16[768,256]{1,0:T(8,128)(2,1)S(1)}, u32[]{:S(2)}, u32[]{:S(2)}) collective-permute-start(bf16[768,256]{1,0:T(8,128)(2,1)} %collective-permute-done.17.refs_1_), channel_id=1, source_target_pairs={{0,16},{16,0},{1,17},{17,1},{2,18},{18,2},{3,19},{19,3},{4,20},{20... | collective-permute-start | bytes 1179656 | tf_op jit(solution)/shard_map/ppermute | solution.py:71
  125.9 12.6 %collective-permute-start.21 = (bf16[768,256]{1,0:T(8,128)(2,1)S(1)}, bf16[768,256]{1,0:T(8,128)(2,1)S(1)}, u32[]{:S(2)}, u32[]{:S(2)}) collective-permute-start(bf16[768,256]{1,0:T(8,128)(2,1)S(1)} %collective-permute-done.20.refs_4_), channel_id=1, source_target_pairs={{0,32},{16,60},{32,4},{48,16},{4,36},{20,48},{36,8},{52,20},{8,40}... | collective-permute-start | bytes 1179656 | tf_op jit(solution)/shard_map/ppermute | solution.py:63
  126.7 23.1 %collective-permute-start.10 = (bf16[256,1536]{1,0:T(8,128)(2,1)}, bf16[256,1536]{1,0:T(8,128)(2,1)S(1)}, u32[]{:S(2)}, u32[]{:S(2)}) collective-permute-start(bf16[256,1536]{1,0:T(8,128)(2,1)} %collective-permute-done.2.refs_1_), channel_id=1, source_target_pairs={{0,16},{16,0},{1,17},{17,1},{2,18},{18,2},{3,19},{19,3},{4,20},{20... | collective-permute-start | bytes 2359304 | tf_op jit(solution)/shard_map/ppermute | solution.py:71
  127.6 23.7 %collective-permute-start.11 = (bf16[256,1536]{1,0:T(8,128)(2,1)}, bf16[256,1536]{1,0:T(8,128)(2,1)S(1)}, u32[]{:S(2)}, u32[]{:S(2)}) collective-permute-start(bf16[256,1536]{1,0:T(8,128)(2,1)} %copy-done.24), channel_id=1, source_target_pairs={{0,16},{16,0},{1,17},{17,1},{2,18},{18,2},{3,19},{19,3},{4,20},{20... | collective-permute-start | bytes 2359304 | tf_op jit(solution)/shard_map/ppermute | solution.py:71
  139.3 9.0 %collective-permute-start.22 = (bf16[768,256]{1,0:T(8,128)(2,1)S(1)}, bf16[768,256]{1,0:T(8,128)(2,1)S(1)}, u32[]{:S(2)}, u32[]{:S(2)}) collective-permute-start(bf16[768,256]{1,0:T(8,128)(2,1)S(1)} %collective-permute-done.21.refs_5_), channel_id=1, source_target_pairs={{0,32},{16,60},{32,4},{48,16},{4,36},{20,48},{36,8},{52,20},{8,40}... | collective-permute-start | bytes 1179656 | tf_op jit(solution)/shard_map/ppermute | solution.py:63
  139.3 22.4 %collective-permute-start.8 = (bf16[256,1536]{1,0:T(8,128)(2,1)}, bf16[256,1536]{1,0:T(8,128)(2,1)}, u32[]{:S(2)}, u32[]{:S(2)}) collective-permute-start(bf16[256,1536]{1,0:T(8,128)(2,1)} %collective-permute-done.7.refs_6_), channel_id=1, source_target_pairs={{0,32},{16,60},{32,4},{48,16},{4,36},{20,48},{36,8},{52,20},{8,40}... | collective-permute-start | bytes 2359304 | tf_op jit(solution)/shard_map/ppermute | solution.py:63
  141.4 7.6 %collective-permute-start.26 = (bf16[768,256]{1,0:T(8,128)(2,1)}, bf16[768,256]{1,0:T(8,128)(2,1)S(1)}, u32[]{:S(2)}, u32[]{:S(2)}) collective-permute-start(bf16[768,256]{1,0:T(8,128)(2,1)} %collective-permute-done.18.refs_2_), channel_id=1, source_target_pairs={{0,16},{16,0},{1,17},{17,1},{2,18},{18,2},{3,19},{19,3},{4,20},{20... | collective-permute-start | bytes 1179656 | tf_op jit(solution)/shard_map/ppermute | solution.py:71
  149.0 11.9 %collective-permute-start.23 = (bf16[768,256]{1,0:T(8,128)(2,1)S(1)}, bf16[768,256]{1,0:T(8,128)(2,1)S(1)}, u32[]{:S(2)}, u32[]{:S(2)}) collective-permute-start(bf16[768,256]{1,0:T(8,128)(2,1)S(1)} %collective-permute-done.22.refs_6_), channel_id=1, source_target_pairs={{0,32},{16,60},{32,4},{48,16},{4,36},{20,48},{36,8},{52,20},{8,40}... | collective-permute-start | bytes 1179656 | tf_op jit(solution)/shard_map/ppermute | solution.py:63
  149.8 13.1 %collective-permute-start.12 = (bf16[256,1536]{1,0:T(8,128)(2,1)}, bf16[256,1536]{1,0:T(8,128)(2,1)}, u32[]{:S(2)}, u32[]{:S(2)}) collective-permute-start(bf16[256,1536]{1,0:T(8,128)(2,1)} %copy-done.27), channel_id=1, source_target_pairs={{0,16},{16,0},{1,17},{17,1},{2,18},{18,2},{3,19},{19,3},{4,20},{20... | collective-permute-start | bytes 2359304 | tf_op jit(solution)/shard_map/ppermute | solution.py:71
  150.7 12.2 %collective-permute-start.13 = (bf16[256,1536]{1,0:T(8,128)(2,1)}, bf16[256,1536]{1,0:T(8,128)(2,1)}, u32[]{:S(2)}, u32[]{:S(2)}) collective-permute-start(bf16[256,1536]{1,0:T(8,128)(2,1)} %collective-permute-done.5.refs_4_), channel_id=1, source_target_pairs={{0,16},{16,0},{1,17},{17,1},{2,18},{18,2},{3,19},{19,3},{4,20},{20... | collective-permute-start | bytes 2359304 | tf_op jit(solution)/shard_map/ppermute | solution.py:71
  152.1 11.3 %collective-permute-start.14 = (bf16[256,1536]{1,0:T(8,128)(2,1)}, bf16[256,1536]{1,0:T(8,128)(2,1)}, u32[]{:S(2)}, u32[]{:S(2)}) collective-permute-start(bf16[256,1536]{1,0:T(8,128)(2,1)} %collective-permute-done.6.refs_5_), channel_id=1, source_target_pairs={{0,16},{16,0},{1,17},{17,1},{2,18},{18,2},{3,19},{19,3},{4,20},{20... | collective-permute-start | bytes 2359304 | tf_op jit(solution)/shard_map/ppermute | solution.py:71
  161.7 2.6 collective-permute-start.15
  161.7 3.7 %collective-permute-start.16 = (bf16[256,1536]{1,0:T(8,128)(2,1)}, bf16[256,1536]{1,0:T(8,128)(2,1)}, u32[]{:S(2)}, u32[]{:S(2)}) collective-permute-start(bf16[256,1536]{1,0:T(8,128)(2,1)} %collective-permute-done.8.refs_7_), channel_id=1, source_target_pairs={{0,16},{16,0},{1,17},{17,1},{2,18},{18,2},{3,19},{19,3},{4,20},{20... | collective-permute-start | bytes 2359304 | tf_op jit(solution)/shard_map/ppermute | solution.py:71
  162.9 19.3 %collective-permute-start.27 = (bf16[768,256]{1,0:T(8,128)(2,1)}, bf16[768,256]{1,0:T(8,128)(2,1)}, u32[]{:S(2)}, u32[]{:S(2)}) collective-permute-start(bf16[768,256]{1,0:T(8,128)(2,1)} %copy-done), channel_id=1, source_target_pairs={{0,16},{16,0},{1,17},{17,1},{2,18},{18,2},{3,19},{19,3},{4,20},{20... | collective-permute-start | bytes 1179656 | tf_op jit(solution)/shard_map/ppermute | solution.py:71
  162.9 19.3 %collective-permute-start.28 = (bf16[768,256]{1,0:T(8,128)(2,1)}, bf16[768,256]{1,0:T(8,128)(2,1)}, u32[]{:S(2)}, u32[]{:S(2)}) collective-permute-start(bf16[768,256]{1,0:T(8,128)(2,1)} %copy-done.3), channel_id=1, source_target_pairs={{0,16},{16,0},{1,17},{17,1},{2,18},{18,2},{3,19},{19,3},{4,20},{20... | collective-permute-start | bytes 1179656 | tf_op jit(solution)/shard_map/ppermute | solution.py:71
  163.4 18.8 %collective-permute-start.29 = (bf16[768,256]{1,0:T(8,128)(2,1)}, bf16[768,256]{1,0:T(8,128)(2,1)}, u32[]{:S(2)}, u32[]{:S(2)}) collective-permute-start(bf16[768,256]{1,0:T(8,128)(2,1)} %copy-done.12), channel_id=1, source_target_pairs={{0,16},{16,0},{1,17},{17,1},{2,18},{18,2},{3,19},{19,3},{4,20},{20... | collective-permute-start | bytes 1179656 | tf_op jit(solution)/shard_map/ppermute | solution.py:71
  164.3 18.0 %collective-permute-start.30 = (bf16[768,256]{1,0:T(8,128)(2,1)}, bf16[768,256]{1,0:T(8,128)(2,1)}, u32[]{:S(2)}, u32[]{:S(2)}) collective-permute-start(bf16[768,256]{1,0:T(8,128)(2,1)} %copy-done.15), channel_id=1, source_target_pairs={{0,16},{16,0},{1,17},{17,1},{2,18},{18,2},{3,19},{19,3},{4,20},{20... | collective-permute-start | bytes 1179656 | tf_op jit(solution)/shard_map/ppermute | solution.py:71
  165.4 16.8 %collective-permute-start.31 = (bf16[768,256]{1,0:T(8,128)(2,1)}, bf16[768,256]{1,0:T(8,128)(2,1)}, u32[]{:S(2)}, u32[]{:S(2)}) collective-permute-start(bf16[768,256]{1,0:T(8,128)(2,1)} %copy-done.21), channel_id=1, source_target_pairs={{0,16},{16,0},{1,17},{17,1},{2,18},{18,2},{3,19},{19,3},{4,20},{20... | collective-permute-start | bytes 1179656 | tf_op jit(solution)/shard_map/ppermute | solution.py:71
  171.2 11.0 %copy-start.1 = (bf16[768,256]{1,0:T(8,128)(2,1)S(1)}, bf16[768,256]{1,0:T(8,128)(2,1)}, u32[]{:S(2)}) copy-start(bf16[768,256]{1,0:T(8,128)(2,1)} %copy-done) | copy-start | bytes 1179652
  171.3 11.1 %copy-start.4 = (bf16[768,256]{1,0:T(8,128)(2,1)S(1)}, bf16[768,256]{1,0:T(8,128)(2,1)}, u32[]{:S(2)}) copy-start(bf16[768,256]{1,0:T(8,128)(2,1)} %copy-done.3) | copy-start | bytes 1179652
  171.3 11.1 %copy-start.7 = (bf16[768,256]{1,0:T(8,128)(2,1)S(1)}, bf16[768,256]{1,0:T(8,128)(2,1)}, u32[]{:S(2)}) copy-start(bf16[768,256]{1,0:T(8,128)(2,1)} %copy-done.6) | copy-start | bytes 1179652
  171.3 11.1 %copy-start.10 = (bf16[768,256]{1,0:T(8,128)(2,1)S(1)}, bf16[768,256]{1,0:T(8,128)(2,1)}, u32[]{:S(2)}) copy-start(bf16[768,256]{1,0:T(8,128)(2,1)} %copy-done.9) | copy-start | bytes 1179652
  171.3 11.1 %copy-start.13 = (bf16[768,256]{1,0:T(8,128)(2,1)S(1)}, bf16[768,256]{1,0:T(8,128)(2,1)}, u32[]{:S(2)}) copy-start(bf16[768,256]{1,0:T(8,128)(2,1)} %copy-done.12) | copy-start | bytes 1179652
  171.3 11.1 %copy-start.16 = (bf16[768,256]{1,0:T(8,128)(2,1)S(1)}, bf16[768,256]{1,0:T(8,128)(2,1)}, u32[]{:S(2)}) copy-start(bf16[768,256]{1,0:T(8,128)(2,1)} %copy-done.15) | copy-start | bytes 1179652
  171.3 11.1 %copy-start.19 = (bf16[768,256]{1,0:T(8,128)(2,1)S(1)}, bf16[768,256]{1,0:T(8,128)(2,1)}, u32[]{:S(2)}) copy-start(bf16[768,256]{1,0:T(8,128)(2,1)} %copy-done.18) | copy-start | bytes 1179652
  171.3 11.1 %copy-start.22 = (bf16[768,256]{1,0:T(8,128)(2,1)S(1)}, bf16[768,256]{1,0:T(8,128)(2,1)}, u32[]{:S(2)}) copy-start(bf16[768,256]{1,0:T(8,128)(2,1)} %copy-done.21) | copy-start | bytes 1179652
  189.9 48.8 %all-to-all-start.3 = ((bf16[16,24,4096]{2,1,0:T(8,128)(2,1)}), bf16[16,24,4096]{2,1,0:T(8,128)(2,1)}, u32[]{:S(2)}, u32[]{:S(2)}) async-start(bf16[16,24,4096]{2,1,0:T(8,128)(2,1)} %bitcast.18), calls=%async_computation.3 | async-start | bytes 6291456 | tf_op jit(solution)/shard_map/all_to_all | solution.py:253
  202.8 10.2 %copy-start.14 = (bf16[768,256]{1,0:T(8,128)(2,1)S(1)}, bf16[768,256]{1,0:T(8,128)(2,1)}, u32[]{:S(2)}) copy-start(bf16[768,256]{1,0:T(8,128)(2,1)} %copy-done.12) | copy-start | bytes 1179652
  238.7 12.5 %copy-start.46 = (f32[2,128,2]{1,2,0:T(2,128)S(1)}, f32[2,128,2]{1,2,0:T(2,128)}, u32[]{:S(2)}) copy-start(f32[2,128,2]{1,2,0:T(2,128)} %param.12) | copy-start | bytes 6148
  238.7 53.7 %all-to-all-start.1 = ((bf16[16,24,4096]{2,1,0:T(8,128)(2,1)}), bf16[16,24,4096]{2,1,0:T(8,128)(2,1)S(1)}, u32[]{:S(2)}, u32[]{:S(2)}) async-start(bf16[16,24,4096]{2,1,0:T(8,128)(2,1)} %bitcast.10), calls=%async_computation.1 | async-start | bytes 6291456 | tf_op jit(solution)/shard_map/all_to_all | solution.py:253
  (35 other events, 124.3 us)

commit v3 on v2

v3 whole, which is shorter than its diff:
```python
import jax
import jax.numpy as jnp
import numpy as np
from jax import lax
from jax.experimental import pallas as pl
from jax.experimental.pallas import tpu as pltpu
from jax.sharding import Mesh, PartitionSpec as P

AXES = ("x", "zl", "core", "zh", "y")
NX, NZL, NC, NZH, NY = 4, 2, 2, 4, 4
MIB = 1 << 20
TILE = 256
OUT_TILE = 1024
CUT = 1152


def updated(master, moment, grad):
    return (master - 0.5 * (0.8 * moment + 0.2 * grad.astype(jnp.float32))).astype(jnp.bfloat16)


def flat(x, zl, c, zh):
    return ((x * NZL + zl) * NC + c) * NZH + zh


def places():
    return [
        (x, zl, c, zh)
        for x in range(NX)
        for zl in range(NZL)
        for c in range(NC)
        for zh in range(NZH)
    ]


NZ = NZL * NZH


def host_of(x, zl, c, zh):
    hops = x if c == 0 else NX - 1 - x
    z = (NZL * zh + 1 + hops) % NZ if zl else (NZL * zh - hops) % NZ
    return zh, z % NZL, c, z // NZL


SPREAD = [(flat(*place), flat(*host_of(*place))) for place in places()]
SHARD_AT = {
    host_of(x, zl, c, zh): (x * NZL + zl) * NC + c for x, zl, c, zh in places()
}


def ring_index(z, c):
    return (z % NZL * NC + c) * NZH + z // NZL


def ring_step(z, c):
    return (z + 1 - 2 * c) % NZ


PASS_ON = [(ring_index(z, c), ring_index(ring_step(z, c), c)) for z in range(NZ) for c in range(NC)]


def in_hbm(value):
    return pltpu.with_memory_space_constraint(value, pltpu.HBM)


def spread(block):
    return in_hbm(lax.ppermute(block, ("x", "zl", "core", "zh"), SPREAD))


def pass_on(block):
    return in_hbm(lax.ppermute(block, ("zl", "core", "zh"), PASS_ON))


def other_core(block):
    return in_hbm(lax.ppermute(block, "core", [(0, 1), (1, 0)]))


def after(value, *others):
    return lax.optimization_barrier((value,) + others)[0]


def rings(first, second, ready):
    mine, others = ([first], [second]), ([], [])
    for step in range(NZ):
        for stream in (0, 1):
            others[stream].append(other_core(mine[stream][step]))
        if step == NZ - 1:
            break
        for stream in (0, 1):
            block = mine[stream][step]
            if step:
                block = after(block, mine[1 - stream][step - 1], others[stream][step - 1])
            else:
                block = after(block, *ready)
            mine[stream].append(pass_on(block))
    return [mine[stream] + others[stream] for stream in (0, 1)]


def shards_at(x, zl, c, zh):
    z = NZL * zh + zl
    entries = []
    for core in (c, 1 - c):
        for step in range(NZ):
            at = (z - step * (1 - 2 * core)) % NZ
            entries.append(SHARD_AT[x, at % NZL, core, at // NZL])
    return entries


SHARDS = np.array([shards_at(*place) for place in places()], np.int32)


def shard_table():
    x, zl, c, zh = (lax.axis_index(name) for name in ("x", "zl", "core", "zh"))
    return lax.dynamic_index_in_dim(jnp.asarray(SHARDS), flat(x, zl, c, zh), keepdims=False)


def first_kernel(master, moment, grad, o_ref):
    o_ref[...] = packed(master, moment, grad, 0, o_ref.shape[1])


def second_kernel(master, moment, grad, down_master, down_moment, down_grad, o_ref):
    depth, wide = master.shape
    o_ref[:, : wide - CUT] = packed(master, moment, grad, CUT, wide)
    for j in range(down_master.shape[0] // depth):
        rows = pl.ds(j * depth, depth)
        o_ref[:, wide - CUT + j * depth : wide - CUT + (j + 1) * depth] = updated(
            down_master[rows, :], down_moment[rows, :], down_grad[rows, :]
        )


def packed(master, moment, grad, low, high):
    units = master.shape[1] // 2
    parts = []
    for n in range(units // TILE):
        for first in (n * TILE, units + n * TILE):
            at = len(parts) * TILE
            begin, end = max(low, at), min(high, at + TILE)
            parts.append(None)
            if begin < end:
                cols = pl.ds(first + begin - at, end - begin)
                parts[-1] = updated(master[:, cols], moment[:, cols], grad[:, cols])
    return jnp.concatenate([part for part in parts if part is not None], axis=1)


def first_block(gate_up):
    return pl.pallas_call(
        first_kernel,
        out_shape=jax.ShapeDtypeStruct((gate_up[0].shape[0], CUT), jnp.bfloat16),
        name="first_block",
    )(*gate_up)


def second_block(gate_up, down):
    return pl.pallas_call(
        second_kernel,
        out_shape=jax.ShapeDtypeStruct((gate_up[0].shape[0], CUT), jnp.bfloat16),
        name="second_block",
    )(*gate_up, *down)


def expert_kernel(table, x_hbm, *refs):
    firsts, seconds = refs[:16], refs[16:32]
    o_hbm, x_buf, up_buf, down_buf, o_buf, up_sems, down_sems, x_sem, o_sems = refs[32:]
    shards, depth, wide = up_buf.shape
    units = wide // 2
    blocks = units // depth
    tiles = units // TILE
    rest = wide - CUT
    x_copy = pltpu.make_async_copy(x_hbm, x_buf, x_sem)
    x_copy.start()
    up_copies = [[] for _ in range(tiles)]
    down_copies = []
    for n, (first, second) in enumerate(zip(firsts, seconds)):
        slot = table[n]

        def copy_columns(source, low, high, target, m):
            return pltpu.make_async_copy(
                source.at[:, pl.ds(low, high - low)],
                up_buf.at[slot, :, pl.ds(target, high - low)],
                up_sems.at[(tiles + 1) * n + m],
            )

        for m in range(tiles):
            low, high = 2 * TILE * m, 2 * TILE * (m + 1)
            if low < CUT:
                up_copies[m].append(copy_columns(first, low, min(high, CUT), low, m))
            if high > CUT:
                up_copies[m].append(copy_columns(second, 0, rest, CUT, tiles))
        at = pl.ds(pl.multiple_of(slot * depth, depth), depth)
        down_copies += [
            pltpu.make_async_copy(
                second.at[:, pl.ds(rest + j * depth, depth)],
                down_buf.at[pl.ds(j * depth, depth), at],
                down_sems.at[blocks * n + j],
            )
            for j in range(blocks)
        ]
    for copies in up_copies:
        for copy in copies:
            copy.start()
    for copy in down_copies:
        copy.start()
    x_copy.wait()
    hidden = []
    for m in range(tiles):
        for copy in up_copies[m]:
            copy.wait()
        weight = up_buf[:, :, 2 * TILE * m : 2 * TILE * (m + 1)].reshape(shards * depth, 2 * TILE)
        both = jnp.dot(x_buf[...], weight, preferred_element_type=jnp.float32)
        gate, upper = both[:, :TILE], both[:, TILE:]
        hidden.append((gate / (1.0 + jnp.exp(-gate)) * upper).astype(jnp.bfloat16))
    hidden = jnp.concatenate(hidden, axis=1)
    for copy in down_copies:
        copy.wait()

    def out_copy(n):
        at = pl.ds(pl.multiple_of(n * OUT_TILE, OUT_TILE), OUT_TILE)
        return pltpu.make_async_copy(o_buf.at[:, at], o_hbm.at[:, at], o_sems.at[n])

    def columns(n, carry):
        at = pl.ds(pl.multiple_of(n * OUT_TILE, OUT_TILE), OUT_TILE)
        o_buf[:, at] = jnp.dot(
            hidden, down_buf[:, at], preferred_element_type=jnp.float32
        ).astype(o_buf.dtype)
        out_copy(n).start()
        return carry

    out_tiles = down_buf.shape[1] // OUT_TILE
    lax.fori_loop(0, out_tiles, columns, 0)
    for n in range(out_tiles):
        out_copy(n).wait()


HBM = pl.BlockSpec(memory_space=pltpu.HBM)
VMEM = pl.BlockSpec(memory_space=pltpu.VMEM)
SMEM = pl.BlockSpec(memory_space=pltpu.SMEM)


def experts_of(table, x, firsts, seconds, units):
    rows, width = x.shape
    depth = firsts[0].shape[0]
    return pl.pallas_call(
        expert_kernel,
        out_shape=jax.ShapeDtypeStruct((rows, width), jnp.bfloat16),
        in_specs=[SMEM, HBM] + [HBM] * 32,
        out_specs=HBM,
        scratch_shapes=[
            pltpu.VMEM((rows, width), jnp.bfloat16),
            pltpu.VMEM((16, depth, 2 * units), jnp.bfloat16),
            pltpu.VMEM((units, width), jnp.bfloat16),
            pltpu.VMEM((rows, width), jnp.bfloat16),
            pltpu.SemaphoreType.DMA((16 * (units // TILE + 1),)),
            pltpu.SemaphoreType.DMA((16 * (units // depth),)),
            pltpu.SemaphoreType.DMA,
            pltpu.SemaphoreType.DMA((width // OUT_TILE,)),
        ],
        compiler_params=pltpu.CompilerParams(vmem_limit_bytes=40 * MIB),
        cost_estimate=pl.CostEstimate(
            flops=6 * rows * width * units,
            bytes_accessed=24 * MIB,
            transcendentals=rows * units,
        ),
        name="experts",
    )(table, x, *firsts, *seconds)


def per_device(
    tokens,
    expert_ids,
    route_gain,
    gate_up_master,
    gate_up_moment,
    gate_up_grad,
    down_master,
    down_moment,
    down_grad,
):
    steps, row_dev, top_k = expert_ids.shape
    width = tokens.shape[2]
    experts = NX * NY
    capacity = 3 * row_dev * top_k // (2 * experts)
    units = down_master.shape[1]
    gate_up = (gate_up_master[0], gate_up_moment[0], gate_up_grad[0])
    down = (down_master[0], down_moment[0], down_grad[0])
    packed_first = first_block(gate_up)
    first = spread(packed_first)
    table = shard_table()

    names = expert_ids[..., None] == jnp.arange(experts, dtype=jnp.int32)
    named = jnp.any(names, axis=2).astype(jnp.bfloat16)
    order = jnp.arange(row_dev)
    before = (order[:, None] > order[None, :]).astype(jnp.bfloat16)
    earlier = jnp.einsum("rq,sqe->sre", before, named, preferred_element_type=jnp.float32)
    slot_index = jnp.sum(jnp.where(names, earlier[:, :, None, :], 0.0), axis=3).astype(jnp.int32)
    target = expert_ids * capacity + slot_index
    slots = jnp.arange(experts * capacity, dtype=jnp.int32)
    hits = target[:, :, None, :] == slots[None, None, :, None]
    dispatch_table = jnp.any(hits, axis=3).astype(jnp.bfloat16)
    share = (route_gain / jnp.sum(route_gain, axis=2, keepdims=True)).astype(jnp.bfloat16)
    combine_table = jnp.sum(
        jnp.where(hits, share[:, :, None, :].astype(jnp.float32), 0.0), axis=3
    ).astype(jnp.bfloat16)

    outgoing = [
        jnp.einsum(
            "rp,rd->pd", dispatch_table[s], tokens[s], preferred_element_type=jnp.float32
        ).astype(jnp.bfloat16)
        for s in range(steps)
    ]
    packed_second = second_block(gate_up, down)
    second = spread(packed_second)
    firsts, seconds = rings(first, second, outgoing)
    gate = (packed_first, packed_second)
    mixed = []
    received = []
    for s in range(steps):
        arrived = lax.all_to_all(
            after(outgoing[s], *gate), ("x", "y"), split_axis=0, concat_axis=0, tiled=True
        )
        received.append(arrived)
        gate = (arrived, firsts[1], seconds[1])
    for s in range(steps):
        expert_out = experts_of(table, received[s], firsts, seconds, units)
        returned = lax.all_to_all(expert_out, ("x", "y"), split_axis=0, concat_axis=0, tiled=True)
        mixed.append(
            jnp.dot(combine_table[s], returned, preferred_element_type=jnp.float32).astype(
                jnp.bfloat16
            )
        )
    return jnp.stack(mixed)


def solution(mesh):
    grid = Mesh(mesh.devices.reshape(NX, NZL, NC, NZH, NY), AXES)
    engine, expert = ("x", "zl", "core"), ("zh", "y")
    rows = P(None, AXES, None)
    return jax.shard_map(
        per_device,
        mesh=grid,
        in_specs=(
            rows,
            rows,
            rows,
            P(expert, engine, None),
            P(expert, engine, None),
            P(expert, engine, None),
            P(expert, None, engine),
            P(expert, None, engine),
            P(expert, None, engine),
        ),
        out_specs=rows,
        check_vma=False,
    )
```

time: 296 us -> 254 us (0.86)
  starting transfers between devices: 79.8 us -> 57.1 us
  local copies, waits for them, and re-layouts: 20 us -> 3.63 us
  waiting for transfers between devices: 143 us -> 139 us
  Pallas kernels: 36.1 us -> 39.5 us
    all_to_all x2, starting transfers between devices: 47.7 us -> 15.6 us  [per_device(): lax.all_to_all(after(outgoing[s], *gate), ('x', 'y'), split_axis=0, conca...]
    unnamed x94 -> x38, local copies, waits for them, and re-layouts: 19.3 us -> 2.94 us
    ppermute x32, starting transfers between devices: 12.3 us -> 22.8 us  [the longest x2 11.9 us: spread(): return in_hbm(lax.ppermute(block, ('x', 'zl', 'core', 'zh'), SPREAD))]
    ppermute x32, waiting for transfers between devices: 87.5 us -> 79.7 us  [the longest x14 78 us: pass_on(): return in_hbm(lax.ppermute(block, ('zl', 'core', 'zh'), PASS_ON))]
    all_to_all x2, waiting for transfers between devices: 55.5 us -> 59.5 us  [per_device(): lax.all_to_all(expert_out, ('x', 'y'), split_axis=0, concat_axis=0, tiled...]
    pallas_call x4, Pallas kernels: 36.1 us -> 39.5 us  [the longest x2 32.5 us: experts_of(): pl.pallas_call(expert_kernel, out_shape=jax.ShapeDtypeStruct((rows, width...]
  transfers between devices with their start and end apart: 36 -> 36, of which waited for: 12 -> 16; matrix products, arithmetic and copies ran while one was open for 4% -> 5% of each run, Pallas kernels for 10% -> 14%
where the time goes in v3:
time: 254 us; the launch traced here: 253 us
  waiting for transfers between devices  139 us (55%)
  starting transfers between devices  57.1 us (22%)
  Pallas kernels  39.5 us (16%)
  matrix products  11 us (4%)
  local copies, waits for them, and re-layouts  3.63 us (1%)
    ppermute x14, waiting for transfers between devices, pass_on(): return in_hbm(lax.ppermute(block, ('zl', 'core', 'zh'), PASS_ON))  78 us
    all_to_all x2, waiting for transfers between devices, per_device(): lax.all_to_all(expert_out, ('x', 'y'), split_axis=0, concat_axis=0, tiled...  59.5 us
    pallas_call x2, Pallas kernels, experts_of(): pl.pallas_call(expert_kernel, out_shape=jax.ShapeDtypeStruct((rows, width...  32.5 us
    all_to_all x2, starting transfers between devices, per_device(): lax.all_to_all(expert_out, ('x', 'y'), split_axis=0, concat_axis=0, tiled...  18.8 us
    all_to_all x2, starting transfers between devices, per_device(): lax.all_to_all(after(outgoing[s], *gate), ('x', 'y'), split_axis=0, conca...  15.6 us
    ppermute x2, starting transfers between devices, spread(): return in_hbm(lax.ppermute(block, ('x', 'zl', 'core', 'zh'), SPREAD))  11.9 us
    ppermute x16, starting transfers between devices, other_core(): return in_hbm(lax.ppermute(block, 'core', [(0, 1), (1, 0)]))  8.88 us
    dot_general x2, matrix products, per_device(): jnp.einsum('rp,rd->pd', dispatch_table[s], tokens[s], preferred_element_t...  6.6 us
  transfers between devices with their start and end apart: 36, of which 16 were waited for; matrix products, arithmetic and copies ran while one was open for 5% of the time, Pallas kernels for 14%

profile of v3, /device:TPU:8, one launch (start us, length us, event | category | flops | bytes accessed | tf_op | source)
XLA Modules:
  0.0 252.8 jit_solution(2916454387498730074)
XLA Ops:
  0.0 3.1 %first_block.1 = bf16[256,1152]{1,0:T(8,128)(2,1)} custom-call(f32[256,1536]{1,0:T(8,128)} %bitcast.52, f32[256,1536]{1,0:T(8,128)} %bitcast.54, bf16[256,1536]{1,0:T(8,128)(2,1)} %bitcast.56), custom_call_target="tpu_custom_call" | custom-call | tf_op jit(solution)/shard_map/first_block/pallas_call | solution.py:145
  3.1 6.0 %collective-permute-start = (bf16[256,1152]{1,0:T(8,128)(2,1)}, bf16[256,1152]{1,0:T(8,128)(2,1)}, u32[]{:S(2)}, u32[]{:S(2)}) collective-permute-start(bf16[256,1152]{1,0:T(8,128)(2,1)} %first_block.1), channel_id=1, source_target_pairs={{0,0},{4,68},{8,136},{12,204},{16,56},{20,124},{24,176},{28,244},{... | collective-permute-start | bytes 1769480 | tf_op jit(solution)/shard_map/ppermute | solution.py:66
  9.1 3.9 %second_block.1 = bf16[256,1152]{1,0:T(8,128)(2,1)} custom-call(f32[256,1536]{1,0:T(8,128)} %bitcast.53, f32[256,1536]{1,0:T(8,128)} %bitcast.55, bf16[256,1536]{1,0:T(8,128)(2,1)} %bitcast.57, f32[768,256]{1,0:T(8,128)} %bitcast.58, f32[768,256]{1,0:T(8,128)} %bitcast.59, bf16[768,256]{1,0:T(8,128)(2,1)} %bitcast.60), custom_call_target="tpu_custom_call" | custom-call | tf_op jit(solution)/shard_map/second_block/pallas_call | solution.py:153
  13.0 6.0 %collective-permute-start.2 = (bf16[256,1152]{1,0:T(8,128)(2,1)}, bf16[256,1152]{1,0:T(8,128)(2,1)}, u32[]{:S(2)}, u32[]{:S(2)}) collective-permute-start(bf16[256,1152]{1,0:T(8,128)(2,1)} %second_block.1), channel_id=1, source_target_pairs={{0,0},{4,68},{8,136},{12,204},{16,56},{20,124},{24,176},{28,244},{... | collective-permute-start | bytes 1769480 | tf_op jit(solution)/shard_map/ppermute | solution.py:66
  19.0 0.1 convolution_bitcast_fusion
  19.2 0.1 fusion.10
  19.3 2.7 %convolution_convert_fusion.1 = bf16[384,4096]{1,0:T(8,128)(2,1)} fusion(bf16[2,128,4096]{2,1,0:T(8,128)(2,1)S(1)} %copy-done.2, pred[2,128,384]{2,1,0:T(8,128)(4,1)S(1)} %fusion.10), kind=kOutput, calls=%fused_computation.2 | convolution fusion | flops 404226048 | bytes 4243456 | tf_op jit(solution)/shard_map/rp,rd->pd/dot_general | solution.py:304
  22.0 8.7 %all-to-all-start = ((bf16[16,24,4096]{2,1,0:T(8,128)(2,1)}), bf16[16,24,4096]{2,1,0:T(8,128)(2,1)S(1)}, u32[]{:S(2)}, u32[]{:S(2)}) async-start(bf16[16,24,4096]{2,1,0:T(8,128)(2,1)} %bitcast.50), calls=%async_computation | async-start | bytes 6291456 | tf_op jit(solution)/shard_map/all_to_all | solution.py:316
  30.7 3.9 %convolution_convert_fusion = bf16[384,4096]{1,0:T(8,128)(2,1)} fusion(bf16[2,128,4096]{2,1,0:T(8,128)(2,1)} %param.10, pred[2,128,384]{2,1,0:T(8,128)(4,1)S(1)} %fusion.10), kind=kOutput, calls=%fused_computation.1 | convolution fusion | flops 404226048 | bytes 4243456 | tf_op jit(solution)/shard_map/rp,rd->pd/dot_general | solution.py:304
  34.6 1.0 collective-permute-start.1
  35.7 2.2 collective-permute-start.3
  37.9 2.5 collective-permute-start.8
  40.4 8.5 %collective-permute-done.1.refs_1_ = bf16[256,1152]{1,0:T(8,128)(2,1)S(1)} collective-permute-done((bf16[256,1152]{1,0:T(8,128)(2,1)}, bf16[256,1152]{1,0:T(8,128)(2,1)S(1)}, u32[]{:S(2)}, u32[]{:S(2)}) %collective-permute-start.1) | collective-permute-done | bytes 589856 | tf_op jit(solution)/shard_map/ppermute | solution.py:70
  49.0 0.1 collective-permute-start.6
  49.1 6.1 %collective-permute-done.5.refs_17_ = bf16[256,1152]{1,0:T(8,128)(2,1)S(1)} collective-permute-done((bf16[256,1152]{1,0:T(8,128)(2,1)}, bf16[256,1152]{1,0:T(8,128)(2,1)S(1)}, u32[]{:S(2)}, u32[]{:S(2)}) %collective-permute-start.5) | collective-permute-done | bytes 589856 | tf_op jit(solution)/shard_map/ppermute | solution.py:70
  55.3 0.1 collective-permute-start.12
  55.4 6.1 %collective-permute-done.4.refs_2_ = bf16[256,1152]{1,0:T(8,128)(2,1)S(1)} collective-permute-done((bf16[256,1152]{1,0:T(8,128)(2,1)S(1)}, bf16[256,1152]{1,0:T(8,128)(2,1)S(1)}, u32[]{:S(2)}, u32[]{:S(2)}) %collective-permute-start.4) | collective-permute-done | bytes 589856 | tf_op jit(solution)/shard_map/ppermute | solution.py:70
  61.7 6.1 %collective-permute-done.9.refs_18_ = bf16[256,1152]{1,0:T(8,128)(2,1)S(1)} collective-permute-done((bf16[256,1152]{1,0:T(8,128)(2,1)S(1)}, bf16[256,1152]{1,0:T(8,128)(2,1)S(1)}, u32[]{:S(2)}, u32[]{:S(2)}) %collective-permute-start.9) | collective-permute-done | bytes 589856 | tf_op jit(solution)/shard_map/ppermute | solution.py:70
  68.1 6.1 %collective-permute-done.7.refs_3_ = bf16[256,1152]{1,0:T(8,128)(2,1)S(1)} collective-permute-done((bf16[256,1152]{1,0:T(8,128)(2,1)S(1)}, bf16[256,1152]{1,0:T(8,128)(2,1)S(1)}, u32[]{:S(2)}, u32[]{:S(2)}) %collective-permute-start.7) | collective-permute-done | bytes 589856 | tf_op jit(solution)/shard_map/ppermute | solution.py:70
  74.3 0.3 collective-permute-start.14
  74.6 5.9 %collective-permute-done.13.refs_19_ = bf16[256,1152]{1,0:T(8,128)(2,1)S(1)} collective-permute-done((bf16[256,1152]{1,0:T(8,128)(2,1)S(1)}, bf16[256,1152]{1,0:T(8,128)(2,1)S(1)}, u32[]{:S(2)}, u32[]{:S(2)}) %collective-permute-start.13) | collective-permute-done | bytes 589856 | tf_op jit(solution)/shard_map/ppermute | solution.py:70
  80.7 6.2 %collective-permute-done.11.refs_4_ = bf16[256,1152]{1,0:T(8,128)(2,1)} collective-permute-done((bf16[256,1152]{1,0:T(8,128)(2,1)S(1)}, bf16[256,1152]{1,0:T(8,128)(2,1)}, u32[]{:S(2)}, u32[]{:S(2)}) %collective-permute-start.11) | collective-permute-done | bytes 589856 | tf_op jit(solution)/shard_map/ppermute | solution.py:70
  86.9 0.1 collective-permute-start.18
  87.0 6.2 %collective-permute-done.17.refs_20_ = bf16[256,1152]{1,0:T(8,128)(2,1)} collective-permute-done((bf16[256,1152]{1,0:T(8,128)(2,1)S(1)}, bf16[256,1152]{1,0:T(8,128)(2,1)}, u32[]{:S(2)}, u32[]{:S(2)}) %collective-permute-start.17) | collective-permute-done | bytes 589856 | tf_op jit(solution)/shard_map/ppermute | solution.py:70
  93.4 0.7 copy-done.17
  94.1 6.8 %all-to-all-start.2 = ((bf16[16,24,4096]{2,1,0:T(8,128)(2,1)}), bf16[16,24,4096]{2,1,0:T(8,128)(2,1)}, u32[]{:S(2)}, u32[]{:S(2)}) async-start(bf16[16,24,4096]{2,1,0:T(8,128)(2,1)} %bitcast.49), calls=%async_computation.2 | async-start | bytes 6291456 | tf_op jit(solution)/shard_map/all_to_all | solution.py:316
  100.9 0.5 collective-permute-start.19
  101.4 1.8 collective-permute-start.22
  103.3 2.6 %collective-permute-done.21.refs_21_ = bf16[256,1152]{1,0:T(8,128)(2,1)} collective-permute-done((bf16[256,1152]{1,0:T(8,128)(2,1)}, bf16[256,1152]{1,0:T(8,128)(2,1)}, u32[]{:S(2)}, u32[]{:S(2)}) %collective-permute-start.21) | collective-permute-done | bytes 589856 | tf_op jit(solution)/shard_map/ppermute | solution.py:70
  105.9 6.5 %collective-permute-done.19.refs_6_ = bf16[256,1152]{1,0:T(8,128)(2,1)} collective-permute-done((bf16[256,1152]{1,0:T(8,128)(2,1)}, bf16[256,1152]{1,0:T(8,128)(2,1)}, u32[]{:S(2)}, u32[]{:S(2)}) %collective-permute-start.19) | collective-permute-done | bytes 589856 | tf_op jit(solution)/shard_map/ppermute | solution.py:70
  112.4 6.3 %collective-permute-done.27.refs_22_ = bf16[256,1152]{1,0:T(8,128)(2,1)} collective-permute-done((bf16[256,1152]{1,0:T(8,128)(2,1)}, bf16[256,1152]{1,0:T(8,128)(2,1)}, u32[]{:S(2)}, u32[]{:S(2)}) %collective-permute-start.27) | collective-permute-done | bytes 589856 | tf_op jit(solution)/shard_map/ppermute | solution.py:70
  118.7 1.4 collective-permute-start.24
  120.2 4.9 %collective-permute-done.23.refs_7_ = bf16[256,1152]{1,0:T(8,128)(2,1)} collective-permute-done((bf16[256,1152]{1,0:T(8,128)(2,1)}, bf16[256,1152]{1,0:T(8,128)(2,1)}, u32[]{:S(2)}, u32[]{:S(2)}) %collective-permute-start.23) | collective-permute-done | bytes 589856 | tf_op jit(solution)/shard_map/ppermute | solution.py:70
  125.1 6.3 %collective-permute-done.29.refs_23_ = bf16[256,1152]{1,0:T(8,128)(2,1)} collective-permute-done((bf16[256,1152]{1,0:T(8,128)(2,1)}, bf16[256,1152]{1,0:T(8,128)(2,1)}, u32[]{:S(2)}, u32[]{:S(2)}) %collective-permute-start.29) | collective-permute-done | bytes 589856 | tf_op jit(solution)/shard_map/ppermute | solution.py:70
  131.4 0.7 dynamic-slice_bitcast_fusion.table
  132.1 1.6 collective-permute-done.31.refs_31_
  133.7 13.7 %experts.2 = bf16[384,4096]{1,0:T(8,128)(2,1)S(1)} custom-call(s32[16]{0:T(128)S(1)} %dynamic-slice_bitcast_fusion.table, bf16[384,4096]{1,0:T(8,128)(2,1)S(1)} %bitcast.47, bf16[256,1152]{1,0:T(8,128)(2,1)} %collective-permute-done.refs_0_, bf16[256,1152]{1,0:T(8,128)(2,1)} %copy-done.4, bf16[256,1152]{1,0:T(8,128)(2,1)} %copy-done.8, ...), custom_call_target="tpu_custom_call" | custom-call | flops 7247757312 | bytes 25165824 | tf_op jit(solution)/shard_map/experts/pallas_call | solution.py:241
  147.4 1.7 copy-done
  149.1 7.2 %all-to-all-start.1 = ((bf16[16,24,4096]{2,1,0:T(8,128)(2,1)}), bf16[16,24,4096]{2,1,0:T(8,128)(2,1)}, u32[]{:S(2)}, u32[]{:S(2)}) async-start(bf16[16,24,4096]{2,1,0:T(8,128)(2,1)} %bitcast.48), calls=%async_computation.1 | async-start | bytes 6291456 | tf_op jit(solution)/shard_map/all_to_all | solution.py:323
  156.4 18.8 %experts.3 = bf16[384,4096]{1,0:T(8,128)(2,1)} custom-call(s32[16]{0:T(128)S(1)} %dynamic-slice_bitcast_fusion.table, bf16[384,4096]{1,0:T(8,128)(2,1)} %bitcast.21.x_hbm, bf16[256,1152]{1,0:T(8,128)(2,1)} %collective-permute-done.refs_0_, bf16[256,1152]{1,0:T(8,128)(2,1)} %copy-done.4, bf16[256,1152]{1,0:T(8,128)(2,1)} %copy-done.8, ...), custom_call_target="tpu_custom_call" | custom-call | flops 7247757312 | bytes 25165824 | tf_op jit(solution)/shard_map/experts/pallas_call | solution.py:241
  175.1 22.7 %all-to-all-done.1 = bf16[16,24,4096]{2,1,0:T(8,128)(2,1)} async-done(((bf16[16,24,4096]{2,1,0:T(8,128)(2,1)}), bf16[16,24,4096]{2,1,0:T(8,128)(2,1)}, u32[]{:S(2)}, u32[]{:S(2)}) %all-to-all-start.1) | async-done | bytes 3145760 | tf_op jit(solution)/shard_map/all_to_all | solution.py:323
  197.8 11.6 %all-to-all-start.3 = ((bf16[16,24,4096]{2,1,0:T(8,128)(2,1)}), bf16[16,24,4096]{2,1,0:T(8,128)(2,1)S(1)}, u32[]{:S(2)}, u32[]{:S(2)}) async-start(bf16[16,24,4096]{2,1,0:T(8,128)(2,1)} %bitcast.22), calls=%async_computation.3 | async-start | bytes 6291456 | tf_op jit(solution)/shard_map/all_to_all | solution.py:323
  209.4 0.2 select_reduce_fusion
  209.6 3.6 %fusion.1 = bf16[1,128,4096]{2,1,0:T(8,128)(2,1)} fusion(bf16[384,4096]{1,0:T(8,128)(2,1)} %bitcast.17, bf16[2,128,384]{2,1,0:T(8,128)(2,1)S(1)} %select_reduce_fusion), kind=kOutput, calls=%fused_computation.5 | convolution fusion | flops 403177472 | bytes 4292608 | tf_op jit(solution)/shard_map/dot_general | solution.py:325
  213.2 36.9 %all-to-all-done.3 = bf16[16,24,4096]{2,1,0:T(8,128)(2,1)S(1)} async-done(((bf16[16,24,4096]{2,1,0:T(8,128)(2,1)}), bf16[16,24,4096]{2,1,0:T(8,128)(2,1)S(1)}, u32[]{:S(2)}, u32[]{:S(2)}) %all-to-all-start.3) | async-done | bytes 3145760 | tf_op jit(solution)/shard_map/all_to_all | solution.py:323
  250.1 0.7 fusion.2
  250.8 0.5 copy-done.1
  251.3 1.5 pad_maximum_fusion
  (79 shorter events, 1.0 us)
Async XLA Ops:
  3.1 31.5 %collective-permute-start = (bf16[256,1152]{1,0:T(8,128)(2,1)}, bf16[256,1152]{1,0:T(8,128)(2,1)}, u32[]{:S(2)}, u32[]{:S(2)}) collective-permute-start(bf16[256,1152]{1,0:T(8,128)(2,1)} %first_block.1), channel_id=1, source_target_pairs={{0,0},{4,68},{8,136},{12,204},{16,56},{20,124},{24,176},{28,244},{... | collective-permute-start | bytes 1769480 | tf_op jit(solution)/shard_map/ppermute | solution.py:66
  13.0 24.9 %collective-permute-start.2 = (bf16[256,1152]{1,0:T(8,128)(2,1)}, bf16[256,1152]{1,0:T(8,128)(2,1)}, u32[]{:S(2)}, u32[]{:S(2)}) collective-permute-start(bf16[256,1152]{1,0:T(8,128)(2,1)} %second_block.1), channel_id=1, source_target_pairs={{0,0},{4,68},{8,136},{12,204},{16,56},{20,124},{24,176},{28,244},{... | collective-permute-start | bytes 1769480 | tf_op jit(solution)/shard_map/ppermute | solution.py:66
  22.0 72.1 %all-to-all-start = ((bf16[16,24,4096]{2,1,0:T(8,128)(2,1)}), bf16[16,24,4096]{2,1,0:T(8,128)(2,1)S(1)}, u32[]{:S(2)}, u32[]{:S(2)}) async-start(bf16[16,24,4096]{2,1,0:T(8,128)(2,1)} %bitcast.50), calls=%async_computation | async-start | bytes 6291456 | tf_op jit(solution)/shard_map/all_to_all | solution.py:316
  34.6 14.3 %collective-permute-start.1 = (bf16[256,1152]{1,0:T(8,128)(2,1)}, bf16[256,1152]{1,0:T(8,128)(2,1)S(1)}, u32[]{:S(2)}, u32[]{:S(2)}) collective-permute-start(bf16[256,1152]{1,0:T(8,128)(2,1)} %collective-permute-done.refs_0_), channel_id=1, source_target_pairs={{0,32},{16,60},{32,4},{48,16},{4,36},{20,48},{36,8},{52,20},{8,40}... | collective-permute-start | bytes 1769480 | tf_op jit(solution)/shard_map/ppermute | solution.py:70
  35.7 13.3 %collective-permute-start.3 = (bf16[256,1152]{1,0:T(8,128)(2,1)}, bf16[256,1152]{1,0:T(8,128)(2,1)S(1)}, u32[]{:S(2)}, u32[]{:S(2)}) collective-permute-start(bf16[256,1152]{1,0:T(8,128)(2,1)} %collective-permute-done.refs_0_), channel_id=1, source_target_pairs={{0,16},{16,0},{1,17},{17,1},{2,18},{18,2},{3,19},{19,3},{4,20},{20... | collective-permute-start | bytes 1769480 | tf_op jit(solution)/shard_map/ppermute | solution.py:74
  37.9 17.3 %collective-permute-start.5 = (bf16[256,1152]{1,0:T(8,128)(2,1)}, bf16[256,1152]{1,0:T(8,128)(2,1)S(1)}, u32[]{:S(2)}, u32[]{:S(2)}) collective-permute-start(bf16[256,1152]{1,0:T(8,128)(2,1)} %collective-permute-done.2.refs_16_), channel_id=1, source_target_pairs={{0,32},{16,60},{32,4},{48,16},{4,36},{20,48},{36,8},{52,20},{8,40}... | collective-permute-start | bytes 1769480 | tf_op jit(solution)/shard_map/ppermute | solution.py:70
  37.9 17.3 %collective-permute-start.8 = (bf16[256,1152]{1,0:T(8,128)(2,1)}, bf16[256,1152]{1,0:T(8,128)(2,1)S(1)}, u32[]{:S(2)}, u32[]{:S(2)}) collective-permute-start(bf16[256,1152]{1,0:T(8,128)(2,1)} %collective-permute-done.2.refs_16_), channel_id=1, source_target_pairs={{0,16},{16,0},{1,17},{17,1},{2,18},{18,2},{3,19},{19,3},{4,20},{20... | collective-permute-start | bytes 1769480 | tf_op jit(solution)/shard_map/ppermute | solution.py:74
  48.9 44.4 %copy-start.4 = (bf16[256,1152]{1,0:T(8,128)(2,1)}, bf16[256,1152]{1,0:T(8,128)(2,1)S(1)}, u32[]{:S(2)}) copy-start(bf16[256,1152]{1,0:T(8,128)(2,1)S(1)} %collective-permute-done.1.refs_1_) | copy-start | bytes 1769476
  48.9 44.4 %copy-start.5 = (bf16[256,1152]{1,0:T(8,128)(2,1)}, bf16[256,1152]{1,0:T(8,128)(2,1)S(1)}, u32[]{:S(2)}) copy-start(bf16[256,1152]{1,0:T(8,128)(2,1)S(1)} %collective-permute-done.3.refs_8_) | copy-start | bytes 1769476
  48.9 12.6 %collective-permute-start.4 = (bf16[256,1152]{1,0:T(8,128)(2,1)S(1)}, bf16[256,1152]{1,0:T(8,128)(2,1)S(1)}, u32[]{:S(2)}, u32[]{:S(2)}) collective-permute-start(bf16[256,1152]{1,0:T(8,128)(2,1)S(1)} %collective-permute-done.1.refs_1_), channel_id=1, source_target_pairs={{0,32},{16,60},{32,4},{48,16},{4,36},{20,48},{36,8},{52,20},{8,40}... | collective-permute-start | bytes 1769480 | tf_op jit(solution)/shard_map/ppermute | solution.py:70
  49.0 12.6 %collective-permute-start.6 = (bf16[256,1152]{1,0:T(8,128)(2,1)S(1)}, bf16[256,1152]{1,0:T(8,128)(2,1)S(1)}, u32[]{:S(2)}, u32[]{:S(2)}) collective-permute-start(bf16[256,1152]{1,0:T(8,128)(2,1)S(1)} %collective-permute-done.1.refs_1_), channel_id=1, source_target_pairs={{0,16},{16,0},{1,17},{17,1},{2,18},{18,2},{3,19},{19,3},{4,20},{20... | collective-permute-start | bytes 1769480 | tf_op jit(solution)/shard_map/ppermute | solution.py:74
  55.2 38.1 %copy-start.6 = (bf16[256,1152]{1,0:T(8,128)(2,1)}, bf16[256,1152]{1,0:T(8,128)(2,1)S(1)}, u32[]{:S(2)}) copy-start(bf16[256,1152]{1,0:T(8,128)(2,1)S(1)} %collective-permute-done.5.refs_17_) | copy-start | bytes 1769476
  55.2 38.1 %copy-start.7 = (bf16[256,1152]{1,0:T(8,128)(2,1)}, bf16[256,1152]{1,0:T(8,128)(2,1)S(1)}, u32[]{:S(2)}) copy-start(bf16[256,1152]{1,0:T(8,128)(2,1)S(1)} %collective-permute-done.8.refs_24_) | copy-start | bytes 1769476
  55.2 12.6 %collective-permute-start.9 = (bf16[256,1152]{1,0:T(8,128)(2,1)S(1)}, bf16[256,1152]{1,0:T(8,128)(2,1)S(1)}, u32[]{:S(2)}, u32[]{:S(2)}) collective-permute-start(bf16[256,1152]{1,0:T(8,128)(2,1)S(1)} %collective-permute-done.5.refs_17_), channel_id=1, source_target_pairs={{0,32},{16,60},{32,4},{48,16},{4,36},{20,48},{36,8},{52,20},{8,40}... | collective-permute-start | bytes 1769480 | tf_op jit(solution)/shard_map/ppermute | solution.py:70
  55.3 12.6 %collective-permute-start.12 = (bf16[256,1152]{1,0:T(8,128)(2,1)S(1)}, bf16[256,1152]{1,0:T(8,128)(2,1)S(1)}, u32[]{:S(2)}, u32[]{:S(2)}) collective-permute-start(bf16[256,1152]{1,0:T(8,128)(2,1)S(1)} %collective-permute-done.5.refs_17_), channel_id=1, source_target_pairs={{0,16},{16,0},{1,17},{17,1},{2,18},{18,2},{3,19},{19,3},{4,20},{20... | collective-permute-start | bytes 1769480 | tf_op jit(solution)/shard_map/ppermute | solution.py:74
  61.5 31.8 %copy-start.8 = (bf16[256,1152]{1,0:T(8,128)(2,1)}, bf16[256,1152]{1,0:T(8,128)(2,1)S(1)}, u32[]{:S(2)}) copy-start(bf16[256,1152]{1,0:T(8,128)(2,1)S(1)} %collective-permute-done.4.refs_2_) | copy-start | bytes 1769476
  61.5 31.8 %copy-start.9 = (bf16[256,1152]{1,0:T(8,128)(2,1)}, bf16[256,1152]{1,0:T(8,128)(2,1)S(1)}, u32[]{:S(2)}) copy-start(bf16[256,1152]{1,0:T(8,128)(2,1)S(1)} %collective-permute-done.6.refs_9_) | copy-start | bytes 1769476
  61.6 12.6 %collective-permute-start.7 = (bf16[256,1152]{1,0:T(8,128)(2,1)S(1)}, bf16[256,1152]{1,0:T(8,128)(2,1)S(1)}, u32[]{:S(2)}, u32[]{:S(2)}) collective-permute-start(bf16[256,1152]{1,0:T(8,128)(2,1)S(1)} %collective-permute-done.4.refs_2_), channel_id=1, source_target_pairs={{0,32},{16,60},{32,4},{48,16},{4,36},{20,48},{36,8},{52,20},{8,40}... | collective-permute-start | bytes 1769480 | tf_op jit(solution)/shard_map/ppermute | solution.py:70
  61.6 12.6 %collective-permute-start.10 = (bf16[256,1152]{1,0:T(8,128)(2,1)S(1)}, bf16[256,1152]{1,0:T(8,128)(2,1)S(1)}, u32[]{:S(2)}, u32[]{:S(2)}) collective-permute-start(bf16[256,1152]{1,0:T(8,128)(2,1)S(1)} %collective-permute-done.4.refs_2_), channel_id=1, source_target_pairs={{0,16},{16,0},{1,17},{17,1},{2,18},{18,2},{3,19},{19,3},{4,20},{20... | collective-permute-start | bytes 1769480 | tf_op jit(solution)/shard_map/ppermute | solution.py:74
  67.9 25.5 %copy-start.10 = (bf16[256,1152]{1,0:T(8,128)(2,1)}, bf16[256,1152]{1,0:T(8,128)(2,1)S(1)}, u32[]{:S(2)}) copy-start(bf16[256,1152]{1,0:T(8,128)(2,1)S(1)} %collective-permute-done.9.refs_18_) | copy-start | bytes 1769476
  67.9 25.5 %copy-start.11 = (bf16[256,1152]{1,0:T(8,128)(2,1)}, bf16[256,1152]{1,0:T(8,128)(2,1)S(1)}, u32[]{:S(2)}) copy-start(bf16[256,1152]{1,0:T(8,128)(2,1)S(1)} %collective-permute-done.12.refs_25_) | copy-start | bytes 1769476
  67.9 12.6 %collective-permute-start.13 = (bf16[256,1152]{1,0:T(8,128)(2,1)S(1)}, bf16[256,1152]{1,0:T(8,128)(2,1)S(1)}, u32[]{:S(2)}, u32[]{:S(2)}) collective-permute-start(bf16[256,1152]{1,0:T(8,128)(2,1)S(1)} %collective-permute-done.9.refs_18_), channel_id=1, source_target_pairs={{0,32},{16,60},{32,4},{48,16},{4,36},{20,48},{36,8},{52,20},{8,40}... | collective-permute-start | bytes 1769480 | tf_op jit(solution)/shard_map/ppermute | solution.py:70
  68.0 12.6 %collective-permute-start.16 = (bf16[256,1152]{1,0:T(8,128)(2,1)S(1)}, bf16[256,1152]{1,0:T(8,128)(2,1)S(1)}, u32[]{:S(2)}, u32[]{:S(2)}) collective-permute-start(bf16[256,1152]{1,0:T(8,128)(2,1)S(1)} %collective-permute-done.9.refs_18_), channel_id=1, source_target_pairs={{0,16},{16,0},{1,17},{17,1},{2,18},{18,2},{3,19},{19,3},{4,20},{20... | collective-permute-start | bytes 1769480 | tf_op jit(solution)/shard_map/ppermute | solution.py:74
  74.2 19.2 %copy-start.12 = (bf16[256,1152]{1,0:T(8,128)(2,1)}, bf16[256,1152]{1,0:T(8,128)(2,1)S(1)}, u32[]{:S(2)}) copy-start(bf16[256,1152]{1,0:T(8,128)(2,1)S(1)} %collective-permute-done.7.refs_3_) | copy-start | bytes 1769476
  74.2 19.2 %copy-start.13 = (bf16[256,1152]{1,0:T(8,128)(2,1)}, bf16[256,1152]{1,0:T(8,128)(2,1)S(1)}, u32[]{:S(2)}) copy-start(bf16[256,1152]{1,0:T(8,128)(2,1)S(1)} %collective-permute-done.10.refs_10_) | copy-start | bytes 1769476
  74.2 12.7 %collective-permute-start.11 = (bf16[256,1152]{1,0:T(8,128)(2,1)S(1)}, bf16[256,1152]{1,0:T(8,128)(2,1)}, u32[]{:S(2)}, u32[]{:S(2)}) collective-permute-start(bf16[256,1152]{1,0:T(8,128)(2,1)S(1)} %collective-permute-done.7.refs_3_), channel_id=1, source_target_pairs={{0,32},{16,60},{32,4},{48,16},{4,36},{20,48},{36,8},{52,20},{8,40}... | collective-permute-start | bytes 1769480 | tf_op jit(solution)/shard_map/ppermute | solution.py:70
  74.3 12.7 %collective-permute-start.14 = (bf16[256,1152]{1,0:T(8,128)(2,1)S(1)}, bf16[256,1152]{1,0:T(8,128)(2,1)S(1)}, u32[]{:S(2)}, u32[]{:S(2)}) collective-permute-start(bf16[256,1152]{1,0:T(8,128)(2,1)S(1)} %collective-permute-done.7.refs_3_), channel_id=1, source_target_pairs={{0,16},{16,0},{1,17},{17,1},{2,18},{18,2},{3,19},{19,3},{4,20},{20... | collective-permute-start | bytes 1769480 | tf_op jit(solution)/shard_map/ppermute | solution.py:74
  80.5 12.9 %copy-start.14 = (bf16[256,1152]{1,0:T(8,128)(2,1)}, bf16[256,1152]{1,0:T(8,128)(2,1)S(1)}, u32[]{:S(2)}) copy-start(bf16[256,1152]{1,0:T(8,128)(2,1)S(1)} %collective-permute-done.13.refs_19_) | copy-start | bytes 1769476
  80.5 12.9 %copy-start.15 = (bf16[256,1152]{1,0:T(8,128)(2,1)}, bf16[256,1152]{1,0:T(8,128)(2,1)S(1)}, u32[]{:S(2)}) copy-start(bf16[256,1152]{1,0:T(8,128)(2,1)S(1)} %collective-permute-done.16.refs_26_) | copy-start | bytes 1769476
  80.5 12.7 %collective-permute-start.17 = (bf16[256,1152]{1,0:T(8,128)(2,1)S(1)}, bf16[256,1152]{1,0:T(8,128)(2,1)}, u32[]{:S(2)}, u32[]{:S(2)}) collective-permute-start(bf16[256,1152]{1,0:T(8,128)(2,1)S(1)} %collective-permute-done.13.refs_19_), channel_id=1, source_target_pairs={{0,32},{16,60},{32,4},{48,16},{4,36},{20,48},{36,8},{52,20},{8,40}... | collective-permute-start | bytes 1769480 | tf_op jit(solution)/shard_map/ppermute | solution.py:70
  80.6 12.7 %collective-permute-start.20 = (bf16[256,1152]{1,0:T(8,128)(2,1)S(1)}, bf16[256,1152]{1,0:T(8,128)(2,1)S(1)}, u32[]{:S(2)}, u32[]{:S(2)}) collective-permute-start(bf16[256,1152]{1,0:T(8,128)(2,1)S(1)} %collective-permute-done.13.refs_19_), channel_id=1, source_target_pairs={{0,16},{16,0},{1,17},{17,1},{2,18},{18,2},{3,19},{19,3},{4,20},{20... | collective-permute-start | bytes 1769480 | tf_op jit(solution)/shard_map/ppermute | solution.py:74
  86.9 14.0 %collective-permute-start.15 = (bf16[256,1152]{1,0:T(8,128)(2,1)}, bf16[256,1152]{1,0:T(8,128)(2,1)}, u32[]{:S(2)}, u32[]{:S(2)}) collective-permute-start(bf16[256,1152]{1,0:T(8,128)(2,1)} %collective-permute-done.11.refs_4_), channel_id=1, source_target_pairs={{0,32},{16,60},{32,4},{48,16},{4,36},{20,48},{36,8},{52,20},{8,40}... | collective-permute-start | bytes 1769480 | tf_op jit(solution)/shard_map/ppermute | solution.py:70
  86.9 14.0 %collective-permute-start.18 = (bf16[256,1152]{1,0:T(8,128)(2,1)}, bf16[256,1152]{1,0:T(8,128)(2,1)}, u32[]{:S(2)}, u32[]{:S(2)}) collective-permute-start(bf16[256,1152]{1,0:T(8,128)(2,1)} %collective-permute-done.11.refs_4_), channel_id=1, source_target_pairs={{0,16},{16,0},{1,17},{17,1},{2,18},{18,2},{3,19},{19,3},{4,20},{20... | collective-permute-start | bytes 1769480 | tf_op jit(solution)/shard_map/ppermute | solution.py:74
  93.3 12.6 %collective-permute-start.21 = (bf16[256,1152]{1,0:T(8,128)(2,1)}, bf16[256,1152]{1,0:T(8,128)(2,1)}, u32[]{:S(2)}, u32[]{:S(2)}) collective-permute-start(bf16[256,1152]{1,0:T(8,128)(2,1)} %collective-permute-done.17.refs_20_), channel_id=1, source_target_pairs={{0,32},{16,60},{32,4},{48,16},{4,36},{20,48},{36,8},{52,20},{8,40}... | collective-permute-start | bytes 1769480 | tf_op jit(solution)/shard_map/ppermute | solution.py:70
  94.1 11.8 %collective-permute-start.26 = (bf16[256,1152]{1,0:T(8,128)(2,1)}, bf16[256,1152]{1,0:T(8,128)(2,1)}, u32[]{:S(2)}, u32[]{:S(2)}) collective-permute-start(bf16[256,1152]{1,0:T(8,128)(2,1)} %collective-permute-done.17.refs_20_), channel_id=1, source_target_pairs={{0,16},{16,0},{1,17},{17,1},{2,18},{18,2},{3,19},{19,3},{4,20},{20... | collective-permute-start | bytes 1769480 | tf_op jit(solution)/shard_map/ppermute | solution.py:74
  94.1 55.1 %all-to-all-start.2 = ((bf16[16,24,4096]{2,1,0:T(8,128)(2,1)}), bf16[16,24,4096]{2,1,0:T(8,128)(2,1)}, u32[]{:S(2)}, u32[]{:S(2)}) async-start(bf16[16,24,4096]{2,1,0:T(8,128)(2,1)} %bitcast.49), calls=%async_computation.2 | async-start | bytes 6291456 | tf_op jit(solution)/shard_map/all_to_all | solution.py:316
  100.9 11.5 %collective-permute-start.19 = (bf16[256,1152]{1,0:T(8,128)(2,1)}, bf16[256,1152]{1,0:T(8,128)(2,1)}, u32[]{:S(2)}, u32[]{:S(2)}) collective-permute-start(bf16[256,1152]{1,0:T(8,128)(2,1)} %collective-permute-done.15.refs_5_), channel_id=1, source_target_pairs={{0,32},{16,60},{32,4},{48,16},{4,36},{20,48},{36,8},{52,20},{8,40}... | collective-permute-start | bytes 1769480 | tf_op jit(solution)/shard_map/ppermute | solution.py:70
  101.4 11.0 %collective-permute-start.22 = (bf16[256,1152]{1,0:T(8,128)(2,1)}, bf16[256,1152]{1,0:T(8,128)(2,1)}, u32[]{:S(2)}, u32[]{:S(2)}) collective-permute-start(bf16[256,1152]{1,0:T(8,128)(2,1)} %collective-permute-done.15.refs_5_), channel_id=1, source_target_pairs={{0,16},{16,0},{1,17},{17,1},{2,18},{18,2},{3,19},{19,3},{4,20},{20... | collective-permute-start | bytes 1769480 | tf_op jit(solution)/shard_map/ppermute | solution.py:74
  105.9 12.8 %collective-permute-start.27 = (bf16[256,1152]{1,0:T(8,128)(2,1)}, bf16[256,1152]{1,0:T(8,128)(2,1)}, u32[]{:S(2)}, u32[]{:S(2)}) collective-permute-start(bf16[256,1152]{1,0:T(8,128)(2,1)} %collective-permute-done.21.refs_21_), channel_id=1, source_target_pairs={{0,32},{16,60},{32,4},{48,16},{4,36},{20,48},{36,8},{52,20},{8,40}... | collective-permute-start | bytes 1769480 | tf_op jit(solution)/shard_map/ppermute | solution.py:70
  105.9 12.8 %collective-permute-start.28 = (bf16[256,1152]{1,0:T(8,128)(2,1)}, bf16[256,1152]{1,0:T(8,128)(2,1)}, u32[]{:S(2)}, u32[]{:S(2)}) collective-permute-start(bf16[256,1152]{1,0:T(8,128)(2,1)} %collective-permute-done.21.refs_21_), channel_id=1, source_target_pairs={{0,16},{16,0},{1,17},{17,1},{2,18},{18,2},{3,19},{19,3},{4,20},{20... | collective-permute-start | bytes 1769480 | tf_op jit(solution)/shard_map/ppermute | solution.py:74
  112.4 12.6 %collective-permute-start.23 = (bf16[256,1152]{1,0:T(8,128)(2,1)}, bf16[256,1152]{1,0:T(8,128)(2,1)}, u32[]{:S(2)}, u32[]{:S(2)}) collective-permute-start(bf16[256,1152]{1,0:T(8,128)(2,1)} %collective-permute-done.19.refs_6_), channel_id=1, source_target_pairs={{0,32},{16,60},{32,4},{48,16},{4,36},{20,48},{36,8},{52,20},{8,40}... | collective-permute-start | bytes 1769480 | tf_op jit(solution)/shard_map/ppermute | solution.py:70
  118.7 12.6 %collective-permute-start.29 = (bf16[256,1152]{1,0:T(8,128)(2,1)}, bf16[256,1152]{1,0:T(8,128)(2,1)}, u32[]{:S(2)}, u32[]{:S(2)}) collective-permute-start(bf16[256,1152]{1,0:T(8,128)(2,1)} %collective-permute-done.27.refs_22_), channel_id=1, source_target_pairs={{0,32},{16,60},{32,4},{48,16},{4,36},{20,48},{36,8},{52,20},{8,40}... | collective-permute-start | bytes 1769480 | tf_op jit(solution)/shard_map/ppermute | solution.py:70
  118.7 13.3 %collective-permute-start.24 = (bf16[256,1152]{1,0:T(8,128)(2,1)}, bf16[256,1152]{1,0:T(8,128)(2,1)}, u32[]{:S(2)}, u32[]{:S(2)}) collective-permute-start(bf16[256,1152]{1,0:T(8,128)(2,1)} %collective-permute-done.19.refs_6_), channel_id=1, source_target_pairs={{0,16},{16,0},{1,17},{17,1},{2,18},{18,2},{3,19},{19,3},{4,20},{20... | collective-permute-start | bytes 1769480 | tf_op jit(solution)/shard_map/ppermute | solution.py:74
  120.2 11.9 %collective-permute-start.30 = (bf16[256,1152]{1,0:T(8,128)(2,1)}, bf16[256,1152]{1,0:T(8,128)(2,1)}, u32[]{:S(2)}, u32[]{:S(2)}) collective-permute-start(bf16[256,1152]{1,0:T(8,128)(2,1)} %collective-permute-done.27.refs_22_), channel_id=1, source_target_pairs={{0,16},{16,0},{1,17},{17,1},{2,18},{18,2},{3,19},{19,3},{4,20},{20... | collective-permute-start | bytes 1769480 | tf_op jit(solution)/shard_map/ppermute | solution.py:74
  125.1 7.0 %collective-permute-start.25 = (bf16[256,1152]{1,0:T(8,128)(2,1)}, bf16[256,1152]{1,0:T(8,128)(2,1)}, u32[]{:S(2)}, u32[]{:S(2)}) collective-permute-start(bf16[256,1152]{1,0:T(8,128)(2,1)} %collective-permute-done.23.refs_7_), channel_id=1, source_target_pairs={{0,16},{16,0},{1,17},{17,1},{2,18},{18,2},{3,19},{19,3},{4,20},{20... | collective-permute-start | bytes 1769480 | tf_op jit(solution)/shard_map/ppermute | solution.py:74
  131.4 2.3 collective-permute-start.31
  149.1 48.7 %all-to-all-start.1 = ((bf16[16,24,4096]{2,1,0:T(8,128)(2,1)}), bf16[16,24,4096]{2,1,0:T(8,128)(2,1)}, u32[]{:S(2)}, u32[]{:S(2)}) async-start(bf16[16,24,4096]{2,1,0:T(8,128)(2,1)} %bitcast.48), calls=%async_computation.1 | async-start | bytes 6291456 | tf_op jit(solution)/shard_map/all_to_all | solution.py:323
  197.8 52.2 %all-to-all-start.3 = ((bf16[16,24,4096]{2,1,0:T(8,128)(2,1)}), bf16[16,24,4096]{2,1,0:T(8,128)(2,1)S(1)}, u32[]{:S(2)}, u32[]{:S(2)}) async-start(bf16[16,24,4096]{2,1,0:T(8,128)(2,1)} %bitcast.22), calls=%async_computation.3 | async-start | bytes 6291456 | tf_op jit(solution)/shard_map/all_to_all | solution.py:323
  (7 other events, 41.8 us)

commit v4 on v3

--- a/solution.py
+++ b/solution.py
@@ -240,7 +240,7 @@
     depth = firsts[0].shape[0]
     return pl.pallas_call(
         expert_kernel,
-        out_shape=jax.ShapeDtypeStruct((rows, width), jnp.bfloat16),
+        out_shape=pltpu.HBM((rows, width), jnp.bfloat16),
         in_specs=[SMEM, HBM] + [HBM] * 32,
         out_specs=HBM,
         scratch_shapes=[
@@ -310,7 +310,7 @@
     second = spread(packed_second)
     firsts, seconds = rings(first, second, outgoing)
     gate = (packed_first, packed_second)
-    mixed = []
+    mixed = jnp.zeros((steps, row_dev, width), jnp.bfloat16)
     received = []
     for s in range(steps):
         arrived = lax.all_to_all(
@@ -321,12 +321,12 @@
     for s in range(steps):
         expert_out = experts_of(table, received[s], firsts, seconds, units)
         returned = lax.all_to_all(expert_out, ("x", "y"), split_axis=0, concat_axis=0, tiled=True)
-        mixed.append(
-            jnp.dot(combine_table[s], returned, preferred_element_type=jnp.float32).astype(
-                jnp.bfloat16
-            )
+        returned = pltpu.with_memory_space_constraint(returned, pl.ANY)
+        part = jnp.dot(combine_table[s], returned, preferred_element_type=jnp.float32)
+        mixed = lax.dynamic_update_slice(
+            after(mixed), part.astype(jnp.bfloat16)[None], (s, 0, 0)
         )
-    return jnp.stack(mixed)
+    return mixed
 
 
 def solution(mesh):

time: 254 us -> 253 us (level)
  waiting for transfers between devices: 139 us -> 131 us
  starting transfers between devices: 57.1 us -> 64.5 us
    ppermute x14, waiting for transfers between devices: 78 us -> 70.9 us  [pass_on(): return in_hbm(lax.ppermute(block, ('zl', 'core', 'zh'), PASS_ON))]
    ppermute x16, starting transfers between devices: 8.88 us -> 15.2 us  [other_core(): return in_hbm(lax.ppermute(block, 'core', [(0, 1), (1, 0)]))]
where the time goes in v4:
time: 253 us; the launch traced here: 251 us
  waiting for transfers between devices  131 us (52%)
  starting transfers between devices  64.5 us (25%)
  Pallas kernels  39.9 us (16%)
  matrix products  12 us (5%)
  local copies, waits for them, and re-layouts  3 us (1%)
    ppermute x14, waiting for transfers between devices, pass_on(): return in_hbm(lax.ppermute(block, ('zl', 'core', 'zh'), PASS_ON))  70.9 us
    all_to_all x2, waiting for transfers between devices, per_device(): lax.all_to_all(expert_out, ('x', 'y'), split_axis=0, concat_axis=0, tiled...  58 us
    pallas_call x2, Pallas kernels, experts_of(): pl.pallas_call(expert_kernel, out_shape=pltpu.HBM((rows, width), jnp.bflo...  33 us
    all_to_all x2, starting transfers between devices, per_device(): lax.all_to_all(expert_out, ('x', 'y'), split_axis=0, concat_axis=0, tiled...  18.8 us
    all_to_all x2, starting transfers between devices, per_device(): lax.all_to_all(after(outgoing[s], *gate), ('x', 'y'), split_axis=0, conca...  16 us
    ppermute x16, starting transfers between devices, other_core(): return in_hbm(lax.ppermute(block, 'core', [(0, 1), (1, 0)]))  15.2 us
    ppermute x2, starting transfers between devices, spread(): return in_hbm(lax.ppermute(block, ('x', 'zl', 'core', 'zh'), SPREAD))  12.1 us
    dot_general x2, matrix products, per_device(): jnp.einsum('rp,rd->pd', dispatch_table[s], tokens[s], preferred_element_t...  6.62 us
  transfers between devices with their start and end apart: 36, of which 16 were waited for; matrix products, arithmetic and copies ran while one was open for 5% of the time, Pallas kernels for 14%

profile of v4, /device:TPU:8, one launch (start us, length us, event | category | flops | bytes accessed | tf_op | source)
XLA Modules:
  0.0 250.7 jit_solution(10531359247697336888)
XLA Ops:
  0.0 3.7 %second_block.1 = bf16[256,1152]{1,0:T(8,128)(2,1)} custom-call(f32[256,1536]{1,0:T(8,128)} %bitcast.55, f32[256,1536]{1,0:T(8,128)} %bitcast.57, bf16[256,1536]{1,0:T(8,128)(2,1)} %bitcast.61, f32[768,256]{1,0:T(8,128)} %bitcast.63, f32[768,256]{1,0:T(8,128)} %bitcast.64, bf16[768,256]{1,0:T(8,128)(2,1)} %bitcast.65), custom_call_target="tpu_custom_call" | custom-call | tf_op jit(solution)/shard_map/second_block/pallas_call | solution.py:153
  3.7 6.1 %collective-permute-start.2 = (bf16[256,1152]{1,0:T(8,128)(2,1)}, bf16[256,1152]{1,0:T(8,128)(2,1)}, u32[]{:S(2)}, u32[]{:S(2)}) collective-permute-start(bf16[256,1152]{1,0:T(8,128)(2,1)} %second_block.1), channel_id=1, source_target_pairs={{0,0},{4,68},{8,136},{12,204},{16,56},{20,124},{24,176},{28,244},{... | collective-permute-start | bytes 1769480 | tf_op jit(solution)/shard_map/ppermute | solution.py:66
  9.8 3.1 %first_block.1 = bf16[256,1152]{1,0:T(8,128)(2,1)} custom-call(f32[256,1536]{1,0:T(8,128)} %bitcast.56, f32[256,1536]{1,0:T(8,128)} %bitcast.58, bf16[256,1536]{1,0:T(8,128)(2,1)} %bitcast.62), custom_call_target="tpu_custom_call" | custom-call | tf_op jit(solution)/shard_map/first_block/pallas_call | solution.py:145
  13.0 6.0 %collective-permute-start = (bf16[256,1152]{1,0:T(8,128)(2,1)}, bf16[256,1152]{1,0:T(8,128)(2,1)}, u32[]{:S(2)}, u32[]{:S(2)}) collective-permute-start(bf16[256,1152]{1,0:T(8,128)(2,1)} %first_block.1), channel_id=1, source_target_pairs={{0,0},{4,68},{8,136},{12,204},{16,56},{20,124},{24,176},{28,244},{... | collective-permute-start | bytes 1769480 | tf_op jit(solution)/shard_map/ppermute | solution.py:66
  19.3 2.7 %convolution_convert_fusion.1 = bf16[384,4096]{1,0:T(8,128)(2,1)} fusion(bf16[2,128,4096]{2,1,0:T(8,128)(2,1)S(1)} %copy-done, pred[2,128,384]{2,1,0:T(8,128)(4,1)S(1)} %fusion.12), kind=kOutput, calls=%fused_computation.2 | convolution fusion | flops 404226048 | bytes 4243456 | tf_op jit(solution)/shard_map/rp,rd->pd/dot_general | solution.py:304
  22.0 8.7 %all-to-all-start = ((bf16[16,24,4096]{2,1,0:T(8,128)(2,1)}), bf16[16,24,4096]{2,1,0:T(8,128)(2,1)S(1)}, u32[]{:S(2)}, u32[]{:S(2)}) async-start(bf16[16,24,4096]{2,1,0:T(8,128)(2,1)} %bitcast.53), calls=%async_computation | async-start | bytes 6291456 | tf_op jit(solution)/shard_map/all_to_all | solution.py:316
  30.7 3.9 %convolution_convert_fusion = bf16[384,4096]{1,0:T(8,128)(2,1)} fusion(bf16[2,128,4096]{2,1,0:T(8,128)(2,1)} %param.10, pred[2,128,384]{2,1,0:T(8,128)(4,1)S(1)} %fusion.12), kind=kOutput, calls=%fused_computation.1 | convolution fusion | flops 404226048 | bytes 4243456 | tf_op jit(solution)/shard_map/rp,rd->pd/dot_general | solution.py:304
  34.6 1.0 collective-permute-start.5
  35.6 2.3 collective-permute-start.8
  37.9 3.2 %collective-permute-start.3 = (bf16[256,1152]{1,0:T(8,128)(2,1)}, bf16[256,1152]{1,0:T(8,128)(2,1)S(1)}, u32[]{:S(2)}, u32[]{:S(2)}) collective-permute-start(bf16[256,1152]{1,0:T(8,128)(2,1)} %collective-permute-done.refs_0_), channel_id=1, source_target_pairs={{0,16},{16,0},{1,17},{17,1},{2,18},{18,2},{3,19},{19,3},{4,20},{20... | collective-permute-start | bytes 1769480 | tf_op jit(solution)/shard_map/ppermute | solution.py:74
  41.1 7.2 %collective-permute-done.5.refs_17_ = bf16[256,1152]{1,0:T(8,128)(2,1)S(1)} collective-permute-done((bf16[256,1152]{1,0:T(8,128)(2,1)}, bf16[256,1152]{1,0:T(8,128)(2,1)S(1)}, u32[]{:S(2)}, u32[]{:S(2)}) %collective-permute-start.5) | collective-permute-done | bytes 589856 | tf_op jit(solution)/shard_map/ppermute | solution.py:70
  48.4 1.1 collective-permute-start.12
  49.5 5.1 %collective-permute-done.1.refs_1_ = bf16[256,1152]{1,0:T(8,128)(2,1)S(1)} collective-permute-done((bf16[256,1152]{1,0:T(8,128)(2,1)}, bf16[256,1152]{1,0:T(8,128)(2,1)S(1)}, u32[]{:S(2)}, u32[]{:S(2)}) %collective-permute-start.1) | collective-permute-done | bytes 589856 | tf_op jit(solution)/shard_map/ppermute | solution.py:70
  54.7 1.1 collective-permute-start.6
  55.8 5.1 %collective-permute-done.9.refs_18_ = bf16[256,1152]{1,0:T(8,128)(2,1)S(1)} collective-permute-done((bf16[256,1152]{1,0:T(8,128)(2,1)S(1)}, bf16[256,1152]{1,0:T(8,128)(2,1)S(1)}, u32[]{:S(2)}, u32[]{:S(2)}) %collective-permute-start.9) | collective-permute-done | bytes 589856 | tf_op jit(solution)/shard_map/ppermute | solution.py:70
  61.0 1.1 collective-permute-start.16
  62.1 5.1 %collective-permute-done.4.refs_2_ = bf16[256,1152]{1,0:T(8,128)(2,1)S(1)} collective-permute-done((bf16[256,1152]{1,0:T(8,128)(2,1)S(1)}, bf16[256,1152]{1,0:T(8,128)(2,1)S(1)}, u32[]{:S(2)}, u32[]{:S(2)}) %collective-permute-start.4) | collective-permute-done | bytes 589856 | tf_op jit(solution)/shard_map/ppermute | solution.py:70
  67.4 1.1 collective-permute-start.10
  68.4 5.1 %collective-permute-done.13.refs_19_ = bf16[256,1152]{1,0:T(8,128)(2,1)S(1)} collective-permute-done((bf16[256,1152]{1,0:T(8,128)(2,1)S(1)}, bf16[256,1152]{1,0:T(8,128)(2,1)S(1)}, u32[]{:S(2)}, u32[]{:S(2)}) %collective-permute-start.13) | collective-permute-done | bytes 589856 | tf_op jit(solution)/shard_map/ppermute | solution.py:70
  73.7 1.1 collective-permute-start.20
  74.8 5.1 %collective-permute-done.7.refs_3_ = bf16[256,1152]{1,0:T(8,128)(2,1)S(1)} collective-permute-done((bf16[256,1152]{1,0:T(8,128)(2,1)S(1)}, bf16[256,1152]{1,0:T(8,128)(2,1)S(1)}, u32[]{:S(2)}, u32[]{:S(2)}) %collective-permute-start.7) | collective-permute-done | bytes 589856 | tf_op jit(solution)/shard_map/ppermute | solution.py:70
  80.0 0.8 collective-permute-start.14
  80.8 5.5 %collective-permute-done.17.refs_20_ = bf16[256,1152]{1,0:T(8,128)(2,1)} collective-permute-done((bf16[256,1152]{1,0:T(8,128)(2,1)S(1)}, bf16[256,1152]{1,0:T(8,128)(2,1)}, u32[]{:S(2)}, u32[]{:S(2)}) %collective-permute-start.17) | collective-permute-done | bytes 589856 | tf_op jit(solution)/shard_map/ppermute | solution.py:70
  86.3 0.8 collective-permute-start.26
  87.1 5.5 %collective-permute-done.11.refs_4_ = bf16[256,1152]{1,0:T(8,128)(2,1)} collective-permute-done((bf16[256,1152]{1,0:T(8,128)(2,1)S(1)}, bf16[256,1152]{1,0:T(8,128)(2,1)}, u32[]{:S(2)}, u32[]{:S(2)}) %collective-permute-start.11) | collective-permute-done | bytes 589856 | tf_op jit(solution)/shard_map/ppermute | solution.py:70
  92.8 0.7 copy-done.15
  93.7 7.3 %all-to-all-start.2 = ((bf16[16,24,4096]{2,1,0:T(8,128)(2,1)}), bf16[16,24,4096]{2,1,0:T(8,128)(2,1)}, u32[]{:S(2)}, u32[]{:S(2)}) async-start(bf16[16,24,4096]{2,1,0:T(8,128)(2,1)} %bitcast.52), calls=%async_computation.2 | async-start | bytes 6291456 | tf_op jit(solution)/shard_map/all_to_all | solution.py:316
  101.0 0.9 collective-permute-start.27
  101.9 0.9 collective-permute-start.28
  102.8 2.5 %collective-permute-done.15.refs_5_ = bf16[256,1152]{1,0:T(8,128)(2,1)} collective-permute-done((bf16[256,1152]{1,0:T(8,128)(2,1)}, bf16[256,1152]{1,0:T(8,128)(2,1)}, u32[]{:S(2)}, u32[]{:S(2)}) %collective-permute-start.15) | collective-permute-done | bytes 589856 | tf_op jit(solution)/shard_map/ppermute | solution.py:70
  105.3 0.8 collective-permute-start.22
  106.1 6.4 %collective-permute-done.27.refs_22_ = bf16[256,1152]{1,0:T(8,128)(2,1)} collective-permute-done((bf16[256,1152]{1,0:T(8,128)(2,1)}, bf16[256,1152]{1,0:T(8,128)(2,1)}, u32[]{:S(2)}, u32[]{:S(2)}) %collective-permute-start.27) | collective-permute-done | bytes 589856 | tf_op jit(solution)/shard_map/ppermute | solution.py:70
  112.5 6.3 %collective-permute-done.19.refs_6_ = bf16[256,1152]{1,0:T(8,128)(2,1)} collective-permute-done((bf16[256,1152]{1,0:T(8,128)(2,1)}, bf16[256,1152]{1,0:T(8,128)(2,1)}, u32[]{:S(2)}, u32[]{:S(2)}) %collective-permute-start.19) | collective-permute-done | bytes 589856 | tf_op jit(solution)/shard_map/ppermute | solution.py:70
  118.8 0.9 collective-permute-start.30
  119.7 5.4 %collective-permute-done.29.refs_23_ = bf16[256,1152]{1,0:T(8,128)(2,1)} collective-permute-done((bf16[256,1152]{1,0:T(8,128)(2,1)}, bf16[256,1152]{1,0:T(8,128)(2,1)}, u32[]{:S(2)}, u32[]{:S(2)}) %collective-permute-start.29) | collective-permute-done | bytes 589856 | tf_op jit(solution)/shard_map/ppermute | solution.py:70
  125.1 6.3 %collective-permute-done.23.refs_7_ = bf16[256,1152]{1,0:T(8,128)(2,1)} collective-permute-done((bf16[256,1152]{1,0:T(8,128)(2,1)}, bf16[256,1152]{1,0:T(8,128)(2,1)}, u32[]{:S(2)}, u32[]{:S(2)}) %collective-permute-start.23) | collective-permute-done | bytes 589856 | tf_op jit(solution)/shard_map/ppermute | solution.py:70
  131.4 0.7 fusion.16.table
  132.1 1.6 collective-permute-done.25.refs_15_
  133.8 14.3 %experts.2 = bf16[384,4096]{1,0:T(8,128)(2,1)} custom-call(s32[16]{0:T(128)S(1)} %fusion.16.table, bf16[384,4096]{1,0:T(8,128)(2,1)S(1)} %bitcast.51, bf16[256,1152]{1,0:T(8,128)(2,1)} %collective-permute-done.refs_0_, bf16[256,1152]{1,0:T(8,128)(2,1)} %copy-done.4, bf16[256,1152]{1,0:T(8,128)(2,1)} %copy-done.8, bf16[256,1152]{1,0:T(8,128)(2,1)} %copy-done.12, ...), custom_call_target="tpu_custom_call" | custom-call | flops 7247757312 | bytes 25165824 | tf_op jit(solution)/shard_map/experts/pallas_call | solution.py:241
  148.1 7.2 %all-to-all-start.1 = ((bf16[16,24,4096]{2,1,0:T(8,128)(2,1)}), bf16[16,24,4096]{2,1,0:T(8,128)(2,1)}, u32[]{:S(2)}, u32[]{:S(2)}) async-start(bf16[16,24,4096]{2,1,0:T(8,128)(2,1)} %bitcast.60), calls=%async_computation.1 | async-start | bytes 6291456 | tf_op jit(solution)/shard_map/all_to_all | solution.py:323
  155.3 18.7 %experts.3 = bf16[384,4096]{1,0:T(8,128)(2,1)} custom-call(s32[16]{0:T(128)S(1)} %fusion.16.table, bf16[384,4096]{1,0:T(8,128)(2,1)} %bitcast.21.x_hbm, bf16[256,1152]{1,0:T(8,128)(2,1)} %collective-permute-done.refs_0_, bf16[256,1152]{1,0:T(8,128)(2,1)} %copy-done.4, bf16[256,1152]{1,0:T(8,128)(2,1)} %copy-done.8, bf16[256,1152]{1,0:T(8,128)(2,1)} %copy-done.12, ...), custom_call_target="tpu_custom_call" | custom-call | flops 7247757312 | bytes 25165824 | tf_op jit(solution)/shard_map/experts/pallas_call | solution.py:241
  174.0 22.7 %all-to-all-done.1 = bf16[16,24,4096]{2,1,0:T(8,128)(2,1)} async-done(((bf16[16,24,4096]{2,1,0:T(8,128)(2,1)}), bf16[16,24,4096]{2,1,0:T(8,128)(2,1)}, u32[]{:S(2)}, u32[]{:S(2)}) %all-to-all-start.1) | async-done | bytes 3145760 | tf_op jit(solution)/shard_map/all_to_all | solution.py:323
  196.8 11.6 %all-to-all-start.3 = ((bf16[16,24,4096]{2,1,0:T(8,128)(2,1)}), bf16[16,24,4096]{2,1,0:T(8,128)(2,1)S(1)}, u32[]{:S(2)}, u32[]{:S(2)}) async-start(bf16[16,24,4096]{2,1,0:T(8,128)(2,1)} %bitcast.59), calls=%async_computation.3 | async-start | bytes 6291456 | tf_op jit(solution)/shard_map/all_to_all | solution.py:323
  208.3 0.2 select_reduce_fusion
  208.6 1.6 broadcast_in_dim.42
  210.1 3.6 %fusion.2 = bf16[2,128,4096]{2,1,0:T(8,128)(2,1)} fusion(bf16[2,128,4096]{2,1,0:T(8,128)(2,1)} %broadcast_in_dim.42, bf16[384,4096]{1,0:T(8,128)(2,1)} %bitcast.17, bf16[2,128,384]{2,1,0:T(8,128)(2,1)S(1)} %select_reduce_fusion), kind=kOutput, calls=%fused_computation.6 | convolution fusion | flops 403177472 | bytes 4292608 | tf_op jit(solution)/shard_map/dot_general | solution.py:325
  213.7 35.3 %all-to-all-done.3 = bf16[16,24,4096]{2,1,0:T(8,128)(2,1)S(1)} async-done(((bf16[16,24,4096]{2,1,0:T(8,128)(2,1)}), bf16[16,24,4096]{2,1,0:T(8,128)(2,1)S(1)}, u32[]{:S(2)}, u32[]{:S(2)}) %all-to-all-start.3) | async-done | bytes 3145760 | tf_op jit(solution)/shard_map/all_to_all | solution.py:323
  249.0 1.7 fusion.4
  (75 shorter events, 1.1 us)
Async XLA Ops:
  3.7 15.2 %copy-start.1 = (s32[2,128,2]{1,2,0:T(2,128)S(1)}, s32[2,128,2]{1,2,0:T(2,128)}, u32[]{:S(2)}) copy-start(s32[2,128,2]{1,2,0:T(2,128)} %param.11) | copy-start | bytes 6148
  3.7 15.6 %copy-start = (bf16[2,128,4096]{2,1,0:T(8,128)(2,1)S(1)}, bf16[2,128,4096]{2,1,0:T(8,128)(2,1)}, u32[]{:S(2)}) copy-start(bf16[2,128,4096]{2,1,0:T(8,128)(2,1)} %param.10) | copy-start | bytes 6291460
  3.7 30.9 %collective-permute-start.2 = (bf16[256,1152]{1,0:T(8,128)(2,1)}, bf16[256,1152]{1,0:T(8,128)(2,1)}, u32[]{:S(2)}, u32[]{:S(2)}) collective-permute-start(bf16[256,1152]{1,0:T(8,128)(2,1)} %second_block.1), channel_id=1, source_target_pairs={{0,0},{4,68},{8,136},{12,204},{16,56},{20,124},{24,176},{28,244},{... | collective-permute-start | bytes 1769480 | tf_op jit(solution)/shard_map/ppermute | solution.py:66
  13.0 24.9 %collective-permute-start = (bf16[256,1152]{1,0:T(8,128)(2,1)}, bf16[256,1152]{1,0:T(8,128)(2,1)}, u32[]{:S(2)}, u32[]{:S(2)}) collective-permute-start(bf16[256,1152]{1,0:T(8,128)(2,1)} %first_block.1), channel_id=1, source_target_pairs={{0,0},{4,68},{8,136},{12,204},{16,56},{20,124},{24,176},{28,244},{... | collective-permute-start | bytes 1769480 | tf_op jit(solution)/shard_map/ppermute | solution.py:66
  22.0 71.7 %all-to-all-start = ((bf16[16,24,4096]{2,1,0:T(8,128)(2,1)}), bf16[16,24,4096]{2,1,0:T(8,128)(2,1)S(1)}, u32[]{:S(2)}, u32[]{:S(2)}) async-start(bf16[16,24,4096]{2,1,0:T(8,128)(2,1)} %bitcast.53), calls=%async_computation | async-start | bytes 6291456 | tf_op jit(solution)/shard_map/all_to_all | solution.py:316
  34.6 13.7 %collective-permute-start.5 = (bf16[256,1152]{1,0:T(8,128)(2,1)}, bf16[256,1152]{1,0:T(8,128)(2,1)S(1)}, u32[]{:S(2)}, u32[]{:S(2)}) collective-permute-start(bf16[256,1152]{1,0:T(8,128)(2,1)} %collective-permute-done.2.refs_16_), channel_id=1, source_target_pairs={{0,32},{16,60},{32,4},{48,16},{4,36},{20,48},{36,8},{52,20},{8,40}... | collective-permute-start | bytes 1769480 | tf_op jit(solution)/shard_map/ppermute | solution.py:70
  35.6 12.7 %collective-permute-start.8 = (bf16[256,1152]{1,0:T(8,128)(2,1)}, bf16[256,1152]{1,0:T(8,128)(2,1)S(1)}, u32[]{:S(2)}, u32[]{:S(2)}) collective-permute-start(bf16[256,1152]{1,0:T(8,128)(2,1)} %collective-permute-done.2.refs_16_), channel_id=1, source_target_pairs={{0,16},{16,0},{1,17},{17,1},{2,18},{18,2},{3,19},{19,3},{4,20},{20... | collective-permute-start | bytes 1769480 | tf_op jit(solution)/shard_map/ppermute | solution.py:74
  37.9 16.7 %collective-permute-start.1 = (bf16[256,1152]{1,0:T(8,128)(2,1)}, bf16[256,1152]{1,0:T(8,128)(2,1)S(1)}, u32[]{:S(2)}, u32[]{:S(2)}) collective-permute-start(bf16[256,1152]{1,0:T(8,128)(2,1)} %collective-permute-done.refs_0_), channel_id=1, source_target_pairs={{0,32},{16,60},{32,4},{48,16},{4,36},{20,48},{36,8},{52,20},{8,40}... | collective-permute-start | bytes 1769480 | tf_op jit(solution)/shard_map/ppermute | solution.py:70
  37.9 16.7 %collective-permute-start.3 = (bf16[256,1152]{1,0:T(8,128)(2,1)}, bf16[256,1152]{1,0:T(8,128)(2,1)S(1)}, u32[]{:S(2)}, u32[]{:S(2)}) collective-permute-start(bf16[256,1152]{1,0:T(8,128)(2,1)} %collective-permute-done.refs_0_), channel_id=1, source_target_pairs={{0,16},{16,0},{1,17},{17,1},{2,18},{18,2},{3,19},{19,3},{4,20},{20... | collective-permute-start | bytes 1769480 | tf_op jit(solution)/shard_map/ppermute | solution.py:74
  48.3 44.4 %copy-start.2 = (bf16[256,1152]{1,0:T(8,128)(2,1)}, bf16[256,1152]{1,0:T(8,128)(2,1)S(1)}, u32[]{:S(2)}) copy-start(bf16[256,1152]{1,0:T(8,128)(2,1)S(1)} %collective-permute-done.5.refs_17_) | copy-start | bytes 1769476
  48.3 44.4 %copy-start.3 = (bf16[256,1152]{1,0:T(8,128)(2,1)}, bf16[256,1152]{1,0:T(8,128)(2,1)S(1)}, u32[]{:S(2)}) copy-start(bf16[256,1152]{1,0:T(8,128)(2,1)S(1)} %collective-permute-done.8.refs_24_) | copy-start | bytes 1769476
  48.3 12.6 %collective-permute-start.9 = (bf16[256,1152]{1,0:T(8,128)(2,1)S(1)}, bf16[256,1152]{1,0:T(8,128)(2,1)S(1)}, u32[]{:S(2)}, u32[]{:S(2)}) collective-permute-start(bf16[256,1152]{1,0:T(8,128)(2,1)S(1)} %collective-permute-done.5.refs_17_), channel_id=1, source_target_pairs={{0,32},{16,60},{32,4},{48,16},{4,36},{20,48},{36,8},{52,20},{8,40}... | collective-permute-start | bytes 1769480 | tf_op jit(solution)/shard_map/ppermute | solution.py:70
  48.4 12.6 %collective-permute-start.12 = (bf16[256,1152]{1,0:T(8,128)(2,1)S(1)}, bf16[256,1152]{1,0:T(8,128)(2,1)S(1)}, u32[]{:S(2)}, u32[]{:S(2)}) collective-permute-start(bf16[256,1152]{1,0:T(8,128)(2,1)S(1)} %collective-permute-done.5.refs_17_), channel_id=1, source_target_pairs={{0,16},{16,0},{1,17},{17,1},{2,18},{18,2},{3,19},{19,3},{4,20},{20... | collective-permute-start | bytes 1769480 | tf_op jit(solution)/shard_map/ppermute | solution.py:74
  54.6 38.1 %copy-start.4 = (bf16[256,1152]{1,0:T(8,128)(2,1)}, bf16[256,1152]{1,0:T(8,128)(2,1)S(1)}, u32[]{:S(2)}) copy-start(bf16[256,1152]{1,0:T(8,128)(2,1)S(1)} %collective-permute-done.1.refs_1_) | copy-start | bytes 1769476
  54.6 38.1 %copy-start.5 = (bf16[256,1152]{1,0:T(8,128)(2,1)}, bf16[256,1152]{1,0:T(8,128)(2,1)S(1)}, u32[]{:S(2)}) copy-start(bf16[256,1152]{1,0:T(8,128)(2,1)S(1)} %collective-permute-done.3.refs_8_) | copy-start | bytes 1769476
  54.6 12.6 %collective-permute-start.4 = (bf16[256,1152]{1,0:T(8,128)(2,1)S(1)}, bf16[256,1152]{1,0:T(8,128)(2,1)S(1)}, u32[]{:S(2)}, u32[]{:S(2)}) collective-permute-start(bf16[256,1152]{1,0:T(8,128)(2,1)S(1)} %collective-permute-done.1.refs_1_), channel_id=1, source_target_pairs={{0,32},{16,60},{32,4},{48,16},{4,36},{20,48},{36,8},{52,20},{8,40}... | collective-permute-start | bytes 1769480 | tf_op jit(solution)/shard_map/ppermute | solution.py:70
  54.7 12.6 %collective-permute-start.6 = (bf16[256,1152]{1,0:T(8,128)(2,1)S(1)}, bf16[256,1152]{1,0:T(8,128)(2,1)S(1)}, u32[]{:S(2)}, u32[]{:S(2)}) collective-permute-start(bf16[256,1152]{1,0:T(8,128)(2,1)S(1)} %collective-permute-done.1.refs_1_), channel_id=1, source_target_pairs={{0,16},{16,0},{1,17},{17,1},{2,18},{18,2},{3,19},{19,3},{4,20},{20... | collective-permute-start | bytes 1769480 | tf_op jit(solution)/shard_map/ppermute | solution.py:74
  61.0 31.8 %copy-start.6 = (bf16[256,1152]{1,0:T(8,128)(2,1)}, bf16[256,1152]{1,0:T(8,128)(2,1)S(1)}, u32[]{:S(2)}) copy-start(bf16[256,1152]{1,0:T(8,128)(2,1)S(1)} %collective-permute-done.9.refs_18_) | copy-start | bytes 1769476
  61.0 31.8 %copy-start.7 = (bf16[256,1152]{1,0:T(8,128)(2,1)}, bf16[256,1152]{1,0:T(8,128)(2,1)S(1)}, u32[]{:S(2)}) copy-start(bf16[256,1152]{1,0:T(8,128)(2,1)S(1)} %collective-permute-done.12.refs_25_) | copy-start | bytes 1769476
  61.0 12.6 %collective-permute-start.13 = (bf16[256,1152]{1,0:T(8,128)(2,1)S(1)}, bf16[256,1152]{1,0:T(8,128)(2,1)S(1)}, u32[]{:S(2)}, u32[]{:S(2)}) collective-permute-start(bf16[256,1152]{1,0:T(8,128)(2,1)S(1)} %collective-permute-done.9.refs_18_), channel_id=1, source_target_pairs={{0,32},{16,60},{32,4},{48,16},{4,36},{20,48},{36,8},{52,20},{8,40}... | collective-permute-start | bytes 1769480 | tf_op jit(solution)/shard_map/ppermute | solution.py:70
  61.0 12.6 %collective-permute-start.16 = (bf16[256,1152]{1,0:T(8,128)(2,1)S(1)}, bf16[256,1152]{1,0:T(8,128)(2,1)S(1)}, u32[]{:S(2)}, u32[]{:S(2)}) collective-permute-start(bf16[256,1152]{1,0:T(8,128)(2,1)S(1)} %collective-permute-done.9.refs_18_), channel_id=1, source_target_pairs={{0,16},{16,0},{1,17},{17,1},{2,18},{18,2},{3,19},{19,3},{4,20},{20... | collective-permute-start | bytes 1769480 | tf_op jit(solution)/shard_map/ppermute | solution.py:74
  67.3 25.5 %copy-start.8 = (bf16[256,1152]{1,0:T(8,128)(2,1)}, bf16[256,1152]{1,0:T(8,128)(2,1)S(1)}, u32[]{:S(2)}) copy-start(bf16[256,1152]{1,0:T(8,128)(2,1)S(1)} %collective-permute-done.4.refs_2_) | copy-start | bytes 1769476
  67.3 25.5 %copy-start.9 = (bf16[256,1152]{1,0:T(8,128)(2,1)}, bf16[256,1152]{1,0:T(8,128)(2,1)S(1)}, u32[]{:S(2)}) copy-start(bf16[256,1152]{1,0:T(8,128)(2,1)S(1)} %collective-permute-done.6.refs_9_) | copy-start | bytes 1769476
  67.3 12.6 %collective-permute-start.7 = (bf16[256,1152]{1,0:T(8,128)(2,1)S(1)}, bf16[256,1152]{1,0:T(8,128)(2,1)S(1)}, u32[]{:S(2)}, u32[]{:S(2)}) collective-permute-start(bf16[256,1152]{1,0:T(8,128)(2,1)S(1)} %collective-permute-done.4.refs_2_), channel_id=1, source_target_pairs={{0,32},{16,60},{32,4},{48,16},{4,36},{20,48},{36,8},{52,20},{8,40}... | collective-permute-start | bytes 1769480 | tf_op jit(solution)/shard_map/ppermute | solution.py:70
  67.4 12.6 %collective-permute-start.10 = (bf16[256,1152]{1,0:T(8,128)(2,1)S(1)}, bf16[256,1152]{1,0:T(8,128)(2,1)S(1)}, u32[]{:S(2)}, u32[]{:S(2)}) collective-permute-start(bf16[256,1152]{1,0:T(8,128)(2,1)S(1)} %collective-permute-done.4.refs_2_), channel_id=1, source_target_pairs={{0,16},{16,0},{1,17},{17,1},{2,18},{18,2},{3,19},{19,3},{4,20},{20... | collective-permute-start | bytes 1769480 | tf_op jit(solution)/shard_map/ppermute | solution.py:74
  73.6 19.2 %copy-start.10 = (bf16[256,1152]{1,0:T(8,128)(2,1)}, bf16[256,1152]{1,0:T(8,128)(2,1)S(1)}, u32[]{:S(2)}) copy-start(bf16[256,1152]{1,0:T(8,128)(2,1)S(1)} %collective-permute-done.13.refs_19_) | copy-start | bytes 1769476
  73.6 19.2 %copy-start.11 = (bf16[256,1152]{1,0:T(8,128)(2,1)}, bf16[256,1152]{1,0:T(8,128)(2,1)S(1)}, u32[]{:S(2)}) copy-start(bf16[256,1152]{1,0:T(8,128)(2,1)S(1)} %collective-permute-done.16.refs_26_) | copy-start | bytes 1769476
  73.6 12.7 %collective-permute-start.17 = (bf16[256,1152]{1,0:T(8,128)(2,1)S(1)}, bf16[256,1152]{1,0:T(8,128)(2,1)}, u32[]{:S(2)}, u32[]{:S(2)}) collective-permute-start(bf16[256,1152]{1,0:T(8,128)(2,1)S(1)} %collective-permute-done.13.refs_19_), channel_id=1, source_target_pairs={{0,32},{16,60},{32,4},{48,16},{4,36},{20,48},{36,8},{52,20},{8,40}... | collective-permute-start | bytes 1769480 | tf_op jit(solution)/shard_map/ppermute | solution.py:70
  73.7 12.7 %collective-permute-start.20 = (bf16[256,1152]{1,0:T(8,128)(2,1)S(1)}, bf16[256,1152]{1,0:T(8,128)(2,1)S(1)}, u32[]{:S(2)}, u32[]{:S(2)}) collective-permute-start(bf16[256,1152]{1,0:T(8,128)(2,1)S(1)} %collective-permute-done.13.refs_19_), channel_id=1, source_target_pairs={{0,16},{16,0},{1,17},{17,1},{2,18},{18,2},{3,19},{19,3},{4,20},{20... | collective-permute-start | bytes 1769480 | tf_op jit(solution)/shard_map/ppermute | solution.py:74
  79.9 12.7 %collective-permute-start.11 = (bf16[256,1152]{1,0:T(8,128)(2,1)S(1)}, bf16[256,1152]{1,0:T(8,128)(2,1)}, u32[]{:S(2)}, u32[]{:S(2)}) collective-permute-start(bf16[256,1152]{1,0:T(8,128)(2,1)S(1)} %collective-permute-done.7.refs_3_), channel_id=1, source_target_pairs={{0,32},{16,60},{32,4},{48,16},{4,36},{20,48},{36,8},{52,20},{8,40}... | collective-permute-start | bytes 1769480 | tf_op jit(solution)/shard_map/ppermute | solution.py:70
  80.0 12.7 %collective-permute-start.14 = (bf16[256,1152]{1,0:T(8,128)(2,1)S(1)}, bf16[256,1152]{1,0:T(8,128)(2,1)S(1)}, u32[]{:S(2)}, u32[]{:S(2)}) collective-permute-start(bf16[256,1152]{1,0:T(8,128)(2,1)S(1)} %collective-permute-done.7.refs_3_), channel_id=1, source_target_pairs={{0,16},{16,0},{1,17},{17,1},{2,18},{18,2},{3,19},{19,3},{4,20},{20... | collective-permute-start | bytes 1769480 | tf_op jit(solution)/shard_map/ppermute | solution.py:74
  86.3 14.6 %collective-permute-start.21 = (bf16[256,1152]{1,0:T(8,128)(2,1)}, bf16[256,1152]{1,0:T(8,128)(2,1)}, u32[]{:S(2)}, u32[]{:S(2)}) collective-permute-start(bf16[256,1152]{1,0:T(8,128)(2,1)} %collective-permute-done.17.refs_20_), channel_id=1, source_target_pairs={{0,32},{16,60},{32,4},{48,16},{4,36},{20,48},{36,8},{52,20},{8,40}... | collective-permute-start | bytes 1769480 | tf_op jit(solution)/shard_map/ppermute | solution.py:70
  86.3 14.6 %collective-permute-start.26 = (bf16[256,1152]{1,0:T(8,128)(2,1)}, bf16[256,1152]{1,0:T(8,128)(2,1)}, u32[]{:S(2)}, u32[]{:S(2)}) collective-permute-start(bf16[256,1152]{1,0:T(8,128)(2,1)} %collective-permute-done.17.refs_20_), channel_id=1, source_target_pairs={{0,16},{16,0},{1,17},{17,1},{2,18},{18,2},{3,19},{19,3},{4,20},{20... | collective-permute-start | bytes 1769480 | tf_op jit(solution)/shard_map/ppermute | solution.py:74
  92.7 12.6 %collective-permute-start.15 = (bf16[256,1152]{1,0:T(8,128)(2,1)}, bf16[256,1152]{1,0:T(8,128)(2,1)}, u32[]{:S(2)}, u32[]{:S(2)}) collective-permute-start(bf16[256,1152]{1,0:T(8,128)(2,1)} %collective-permute-done.11.refs_4_), channel_id=1, source_target_pairs={{0,32},{16,60},{32,4},{48,16},{4,36},{20,48},{36,8},{52,20},{8,40}... | collective-permute-start | bytes 1769480 | tf_op jit(solution)/shard_map/ppermute | solution.py:70
  93.5 11.8 %collective-permute-start.18 = (bf16[256,1152]{1,0:T(8,128)(2,1)}, bf16[256,1152]{1,0:T(8,128)(2,1)}, u32[]{:S(2)}, u32[]{:S(2)}) collective-permute-start(bf16[256,1152]{1,0:T(8,128)(2,1)} %collective-permute-done.11.refs_4_), channel_id=1, source_target_pairs={{0,16},{16,0},{1,17},{17,1},{2,18},{18,2},{3,19},{19,3},{4,20},{20... | collective-permute-start | bytes 1769480 | tf_op jit(solution)/shard_map/ppermute | solution.py:74
  93.7 54.4 %all-to-all-start.2 = ((bf16[16,24,4096]{2,1,0:T(8,128)(2,1)}), bf16[16,24,4096]{2,1,0:T(8,128)(2,1)}, u32[]{:S(2)}, u32[]{:S(2)}) async-start(bf16[16,24,4096]{2,1,0:T(8,128)(2,1)} %bitcast.52), calls=%async_computation.2 | async-start | bytes 6291456 | tf_op jit(solution)/shard_map/all_to_all | solution.py:316
  101.0 11.5 %collective-permute-start.27 = (bf16[256,1152]{1,0:T(8,128)(2,1)}, bf16[256,1152]{1,0:T(8,128)(2,1)}, u32[]{:S(2)}, u32[]{:S(2)}) collective-permute-start(bf16[256,1152]{1,0:T(8,128)(2,1)} %collective-permute-done.21.refs_21_), channel_id=1, source_target_pairs={{0,32},{16,60},{32,4},{48,16},{4,36},{20,48},{36,8},{52,20},{8,40}... | collective-permute-start | bytes 1769480 | tf_op jit(solution)/shard_map/ppermute | solution.py:70
  101.9 10.6 %collective-permute-start.28 = (bf16[256,1152]{1,0:T(8,128)(2,1)}, bf16[256,1152]{1,0:T(8,128)(2,1)}, u32[]{:S(2)}, u32[]{:S(2)}) collective-permute-start(bf16[256,1152]{1,0:T(8,128)(2,1)} %collective-permute-done.21.refs_21_), channel_id=1, source_target_pairs={{0,16},{16,0},{1,17},{17,1},{2,18},{18,2},{3,19},{19,3},{4,20},{20... | collective-permute-start | bytes 1769480 | tf_op jit(solution)/shard_map/ppermute | solution.py:74
  105.3 13.5 %collective-permute-start.19 = (bf16[256,1152]{1,0:T(8,128)(2,1)}, bf16[256,1152]{1,0:T(8,128)(2,1)}, u32[]{:S(2)}, u32[]{:S(2)}) collective-permute-start(bf16[256,1152]{1,0:T(8,128)(2,1)} %collective-permute-done.15.refs_5_), channel_id=1, source_target_pairs={{0,32},{16,60},{32,4},{48,16},{4,36},{20,48},{36,8},{52,20},{8,40}... | collective-permute-start | bytes 1769480 | tf_op jit(solution)/shard_map/ppermute | solution.py:70
  105.3 13.5 %collective-permute-start.22 = (bf16[256,1152]{1,0:T(8,128)(2,1)}, bf16[256,1152]{1,0:T(8,128)(2,1)}, u32[]{:S(2)}, u32[]{:S(2)}) collective-permute-start(bf16[256,1152]{1,0:T(8,128)(2,1)} %collective-permute-done.15.refs_5_), channel_id=1, source_target_pairs={{0,16},{16,0},{1,17},{17,1},{2,18},{18,2},{3,19},{19,3},{4,20},{20... | collective-permute-start | bytes 1769480 | tf_op jit(solution)/shard_map/ppermute | solution.py:74
  112.5 12.6 %collective-permute-start.29 = (bf16[256,1152]{1,0:T(8,128)(2,1)}, bf16[256,1152]{1,0:T(8,128)(2,1)}, u32[]{:S(2)}, u32[]{:S(2)}) collective-permute-start(bf16[256,1152]{1,0:T(8,128)(2,1)} %collective-permute-done.27.refs_22_), channel_id=1, source_target_pairs={{0,32},{16,60},{32,4},{48,16},{4,36},{20,48},{36,8},{52,20},{8,40}... | collective-permute-start | bytes 1769480 | tf_op jit(solution)/shard_map/ppermute | solution.py:70
  118.8 12.6 %collective-permute-start.23 = (bf16[256,1152]{1,0:T(8,128)(2,1)}, bf16[256,1152]{1,0:T(8,128)(2,1)}, u32[]{:S(2)}, u32[]{:S(2)}) collective-permute-start(bf16[256,1152]{1,0:T(8,128)(2,1)} %collective-permute-done.19.refs_6_), channel_id=1, source_target_pairs={{0,32},{16,60},{32,4},{48,16},{4,36},{20,48},{36,8},{52,20},{8,40}... | collective-permute-start | bytes 1769480 | tf_op jit(solution)/shard_map/ppermute | solution.py:70
  118.8 13.3 %collective-permute-start.30 = (bf16[256,1152]{1,0:T(8,128)(2,1)}, bf16[256,1152]{1,0:T(8,128)(2,1)}, u32[]{:S(2)}, u32[]{:S(2)}) collective-permute-start(bf16[256,1152]{1,0:T(8,128)(2,1)} %collective-permute-done.27.refs_22_), channel_id=1, source_target_pairs={{0,16},{16,0},{1,17},{17,1},{2,18},{18,2},{3,19},{19,3},{4,20},{20... | collective-permute-start | bytes 1769480 | tf_op jit(solution)/shard_map/ppermute | solution.py:74
  119.7 12.5 %collective-permute-start.24 = (bf16[256,1152]{1,0:T(8,128)(2,1)}, bf16[256,1152]{1,0:T(8,128)(2,1)}, u32[]{:S(2)}, u32[]{:S(2)}) collective-permute-start(bf16[256,1152]{1,0:T(8,128)(2,1)} %collective-permute-done.19.refs_6_), channel_id=1, source_target_pairs={{0,16},{16,0},{1,17},{17,1},{2,18},{18,2},{3,19},{19,3},{4,20},{20... | collective-permute-start | bytes 1769480 | tf_op jit(solution)/shard_map/ppermute | solution.py:74
  125.1 7.0 %collective-permute-start.31 = (bf16[256,1152]{1,0:T(8,128)(2,1)}, bf16[256,1152]{1,0:T(8,128)(2,1)}, u32[]{:S(2)}, u32[]{:S(2)}) collective-permute-start(bf16[256,1152]{1,0:T(8,128)(2,1)} %collective-permute-done.29.refs_23_), channel_id=1, source_target_pairs={{0,16},{16,0},{1,17},{17,1},{2,18},{18,2},{3,19},{19,3},{4,20},{20... | collective-permute-start | bytes 1769480 | tf_op jit(solution)/shard_map/ppermute | solution.py:74
  131.4 2.3 collective-permute-start.25
  148.1 48.7 %all-to-all-start.1 = ((bf16[16,24,4096]{2,1,0:T(8,128)(2,1)}), bf16[16,24,4096]{2,1,0:T(8,128)(2,1)}, u32[]{:S(2)}, u32[]{:S(2)}) async-start(bf16[16,24,4096]{2,1,0:T(8,128)(2,1)} %bitcast.60), calls=%async_computation.1 | async-start | bytes 6291456 | tf_op jit(solution)/shard_map/all_to_all | solution.py:323
  196.8 52.2 %all-to-all-start.3 = ((bf16[16,24,4096]{2,1,0:T(8,128)(2,1)}), bf16[16,24,4096]{2,1,0:T(8,128)(2,1)S(1)}, u32[]{:S(2)}, u32[]{:S(2)}) async-start(bf16[16,24,4096]{2,1,0:T(8,128)(2,1)} %bitcast.59), calls=%async_computation.3 | async-start | bytes 6291456 | tf_op jit(solution)/shard_map/all_to_all | solution.py:323
  (5 other events, 44.6 us)
